TPU v7x, 32 devices: a whole 2x2x4 slice. The times are simulated.
32 devices in a mesh: seq: 4 (over z), fsdp: 8 (over y, x, core).
Axes of the slice: x: 2, y: 2, z: 4, core: 2. Of those that a mesh axis runs over, the one named last changes fastest.
Arguments:
- tokens: bfloat16 [8, 1024, 768], P('fsdp', 'seq'), may hold values from -12 to 12
- cotangent: bfloat16 [8, 1024, 768], P('fsdp', 'seq'), may hold values from -6 to 6
- lengths: int32 [8], P('fsdp'), may hold values from 128 to 1024, as said below
- w_attn: float32 [4, 768, 768], P(None, 'fsdp', 'seq'), may hold values from -0.8660254 to 0.8660254
- attn_first: float32 [4, 768, 768], P(None, 'fsdp', 'seq'), may hold values from -0.3 to 0.3
- attn_second: float32 [4, 768, 768], P(None, 'fsdp', 'seq'), may hold values from 1e-06 to 0.0001
- w_ffn: float32 [2, 768, 3072], P(None, 'fsdp', 'seq'), may hold values from -0.21650635 to 0.21650635
- ffn_first: float32 [2, 768, 3072], P(None, 'fsdp', 'seq'), may hold values from -0.3 to 0.3
- ffn_second: float32 [2, 768, 3072], P(None, 'fsdp', 'seq'), may hold values from 1e-06 to 0.0001
- vectors: float32 [12, 768], P(None, ('seq', 'fsdp')), may hold values from -1 to 1.5
- vec_first: float32 [12, 768], P(None, ('seq', 'fsdp')), may hold values from -0.3 to 0.3
- vec_second: float32 [12, 768], P(None, ('seq', 'fsdp')), may hold values from 1e-06 to 0.0001
Outputs:
- block_out: bfloat16 [8, 1024, 768], P('fsdp', 'seq')
- input_grad: float32 [8, 1024, 768], P('fsdp', 'seq')
- grad_attn: float32 [4, 768, 768], P(None, 'fsdp', 'seq')
- grad_ffn: float32 [2, 768, 3072], P(None, 'fsdp', 'seq')
- grad_vec: float32 [12, 768], P(None, ('seq', 'fsdp'))
- attn_new: float32 [4, 768, 768], P(None, 'fsdp', 'seq')
- attn_first_new: float32 [4, 768, 768], P(None, 'fsdp', 'seq')
- attn_second_new: float32 [4, 768, 768], P(None, 'fsdp', 'seq')
- ffn_new: float32 [2, 768, 3072], P(None, 'fsdp', 'seq')
- ffn_first_new: float32 [2, 768, 3072], P(None, 'fsdp', 'seq')
- ffn_second_new: float32 [2, 768, 3072], P(None, 'fsdp', 'seq')
- vec_new: float32 [12, 768], P(None, ('seq', 'fsdp'))
- vec_first_new: float32 [12, 768], P(None, ('seq', 'fsdp'))
- vec_second_new: float32 [12, 768], P(None, ('seq', 'fsdp'))
Inputs may be any that keep to these rules, and one draw needn't show every extreme that they name: `lengths`: in every draw one sequence has all 1024 tokens valid and one has 128.
All inputs are finite; a program needn't handle non-finite values.
Results may differ from a plain program's by a relative error of at most 0.011.
The roundings to bfloat16 on the way count: a program that leaves them out, or rounds other values in their place, can miss the bound.
Values may be sent and summed in bfloat16 or wider, within the bound.
No kernel may reach another device: no remote copies, remote signals or barrier semaphores. Data moves between devices by JAX's collectives and lax.ppermute only.
A program may use at most 128 MiB of HBM per device.

v0:
```python
import math

import jax
import jax.numpy as jnp
from jax import lax
from jax.experimental import pallas as pl
from jax.experimental.pallas import tpu as pltpu
from jax.sharding import PartitionSpec as P


HEAD = 64
STEP = 3
SCORE_SCALE = 1.0 / math.sqrt(HEAD)


EPS_NORM = 1e-12
ADAM_RATE = 0.005
BETA_ONE = 0.9
BETA_TWO = 0.999
ADAM_EPS = 1e-08
WEIGHT_DECAY = 0.01


def layer_norm(values):
    center = values - jnp.mean(values, axis=-1, keepdims=True)
    inv_scale = lax.rsqrt(jnp.mean(center * center, axis=-1, keepdims=True) + EPS_NORM)
    return (center * inv_scale, inv_scale)


def norm_back(grad_normed, normed, inv_scale):
    return inv_scale * (
        grad_normed
        - jnp.mean(grad_normed, axis=-1, keepdims=True)
        - normed * jnp.mean(grad_normed * normed, axis=-1, keepdims=True)
    )


def gelu_pair(preact):
    normal_cdf = 0.5 * (1.0 + jax.scipy.special.erf(preact * (1.0 / math.sqrt(2.0))))
    density = jnp.exp(-0.5 * preact * preact) * (1.0 / math.sqrt(2.0 * math.pi))
    return (preact * normal_cdf, normal_cdf + preact * density)


def dot_right_t(left, right):
    return lax.dot_general(
        left, right, (((1,), (1,)), ((), ())), preferred_element_type=jnp.float32
    )


def from_behind(piece, distance):
    count = lax.axis_size("seq")
    if distance % count == 0:
        return piece
    return lax.ppermute(piece, "seq", [(i, (i + distance) % count) for i in range(count)])


def gather_behind(piece):
    return [from_behind(piece, r) for r in range(lax.axis_size("seq"))]


def swap_behind(pieces):
    count = len(pieces)
    return [from_behind(pieces[(-r) % count], r) for r in range(count)]


def turn_blocks(blocks):
    count = blocks.shape[0]
    place = lax.axis_index("seq")
    order = (place - jnp.arange(count, dtype=jnp.int32)) % count
    mask = order[:, None] == jnp.arange(count, dtype=jnp.int32)[None, :]
    mask = mask.reshape((count, count) + (1,) * (blocks.ndim - 1))
    return jnp.sum(jnp.where(mask, blocks[None], jnp.zeros((), blocks.dtype)), axis=1)


def adam_step(parameter, gradient, moment_one, moment_two, decay_rate):
    one_new = BETA_ONE * moment_one + (1.0 - BETA_ONE) * gradient
    two_new = BETA_TWO * moment_two + (1.0 - BETA_TWO) * gradient * gradient
    one_hat = one_new / (1.0 - BETA_ONE**STEP)
    two_hat = two_new / (1.0 - BETA_TWO**STEP)
    update = one_hat / (jnp.sqrt(two_hat) + ADAM_EPS)
    return (parameter - ADAM_RATE * (update + decay_rate * parameter), one_new, two_new)


def after(values, *earlier):
    return lax.optimization_barrier((values, earlier))[0]


def halving(blocks, bit, from_low):
    count = blocks.shape[0]
    own = (lax.axis_index("fsdp") >> bit) & 1
    split = (count // 2, 2) if from_low else (2, count // 2)
    axis = 1 if from_low else 0
    view = blocks.reshape(split + blocks.shape[1:])
    kept = lax.dynamic_index_in_dim(view, own, axis, keepdims=False)
    sent = lax.dynamic_index_in_dim(view, 1 - own, axis, keepdims=False)
    return kept, sent.astype(jnp.bfloat16)


def swapped(sent, bit):
    pairs = [(i, i ^ (1 << bit)) for i in range(lax.axis_size("fsdp"))]
    return lax.ppermute(sent, "fsdp", pairs)


def joined(kept, received):
    return kept.astype(jnp.float32) + received.astype(jnp.float32)


def attend_kernel(
    place_ref, length_ref, bias_ref, *refs
):
    count = (len(refs) - 3 - 4) // 2
    token_refs, weight_refs = refs[:count], refs[count : count + 3]
    q_ref, k_ref, v_ref, lse_ref = refs[count + 3 : count + 7]
    mixed_refs = refs[count + 7 :]
    shard_len = token_refs[0].shape[0]
    _, width = q_ref.shape
    for r, token_ref in enumerate(token_refs):
        piece = token_ref[...]
        for k, (weight_ref, out_ref) in enumerate(
            zip(weight_refs, (q_ref, k_ref, v_ref), strict=True)
        ):
            out = jnp.dot(piece, weight_ref[...], preferred_element_type=jnp.float32)
            if k != 1:
                out = out + bias_ref[k // 2 : k // 2 + 1, :]
            out_ref[r * shard_len : (r + 1) * shard_len, :] = out.astype(jnp.bfloat16)
    masked = key_mask(place_ref[0], length_ref[0], count, shard_len)

    for i, mixed_ref in enumerate(mixed_refs):
        at = slice(i * shard_len, (i + 1) * shard_len)
        queries = q_ref[at, :]
        mixed = []
        for h in range(width // HEAD):
            cols = slice(h * HEAD, (h + 1) * HEAD)
            scores = dot_right_t(queries[:, cols] * SCORE_SCALE, k_ref[:, cols]) + masked
            top = jnp.max(scores, axis=1, keepdims=True)
            raised = jnp.exp(scores - top)
            total = jnp.sum(raised, axis=1, keepdims=True)
            probs = (raised * (1.0 / total)).astype(jnp.bfloat16)
            mixed.append(jnp.dot(probs, v_ref[:, cols], preferred_element_type=jnp.float32))
            lse_ref[at, h : h + 1] = top + jnp.log(total)
        mixed_ref[...] = jnp.concatenate(mixed, axis=1).astype(jnp.bfloat16)


def key_mask(place, length, count, shard_len):
    column = lax.broadcasted_iota(jnp.int32, (1, shard_len), 1)
    pieces = []
    for r in range(count):
        start = lax.rem(place + count - r, count) * shard_len
        pieces.append(jnp.where(column + start < length, 0.0, -jnp.inf))
    return jnp.concatenate(pieces, axis=1)


def attend(place, length, bias, token_pieces, weights):
    shard_len = token_pieces[0].shape[0]
    rows, width = shard_len * len(token_pieces), weights[0].shape[1]
    half = jax.ShapeDtypeStruct((rows, width), jnp.bfloat16)
    smem, vmem = pl.BlockSpec(memory_space=pltpu.SMEM), pl.BlockSpec(memory_space=pltpu.VMEM)
    arrays = (bias, *token_pieces, *weights)
    return pl.pallas_call(
        attend_kernel,
        out_shape=(half, half, half, jax.ShapeDtypeStruct((rows, 8), jnp.float32))
        + (jax.ShapeDtypeStruct((shard_len, width), jnp.bfloat16),) * len(token_pieces),
        in_specs=[smem, smem] + [vmem] * len(arrays),
        out_specs=(vmem,) * (4 + len(token_pieces)),
        compiler_params=pltpu.CompilerParams(vmem_limit_bytes=40 << 20),
        cost_estimate=pl.CostEstimate(
            flops=2 * rows * width * (3 * weights[0].shape[0] + 8 * rows),
            bytes_accessed=8 << 20,
            transcendentals=rows * rows * (width // HEAD),
        ),
        name="attend",
    )(place.reshape(1), length.reshape(1), *arrays)


def attend_back_kernel(
    place_ref,
    length_ref,
    q_ref,
    k_ref,
    v_ref,
    lse_ref,
    *refs,
):
    count = (len(refs) - 3 - 2 - 2) // 3
    mixed_refs, grad_refs = refs[:count], refs[count : 2 * count]
    weight_refs, refs = refs[2 * count : 2 * count + 3], refs[2 * count + 3 :]
    all_ref, sums_ref = refs[:2]
    part_refs = refs[2 : 2 + count]
    dk_sum, dv_sum = refs[2 + count :]
    shard_len = grad_refs[0].shape[0]
    _, width = q_ref.shape
    masked = key_mask(place_ref[0], length_ref[0], count, shard_len)
    for i, (grad_ref, mixed_ref) in enumerate(zip(grad_refs, mixed_refs, strict=True)):
        at = slice(i * shard_len, (i + 1) * shard_len)
        queries, grad = q_ref[at, :], grad_ref[...]
        product = grad.astype(jnp.float32) * mixed_ref[...].astype(jnp.float32)
        parts = []
        for h in range(width // HEAD):
            cols = slice(h * HEAD, (h + 1) * HEAD)
            head_q, head_grad = queries[:, cols], grad[:, cols]
            scores = dot_right_t(head_q * SCORE_SCALE, k_ref[:, cols]) + masked
            probs = jnp.exp(scores - lse_ref[at, h : h + 1])
            delta = jnp.sum(product[:, cols], axis=1, keepdims=True)
            grad_probs = dot_right_t(head_grad, v_ref[:, cols])
            grad_scores = (probs * (grad_probs - delta)).astype(jnp.bfloat16)
            parts.append(
                jnp.dot(grad_scores, k_ref[:, cols], preferred_element_type=jnp.float32)
                * SCORE_SCALE
            )
            dk = jnp.dot(head_q.T, grad_scores, preferred_element_type=jnp.float32)
            dv = jnp.dot(head_grad.T, probs.astype(jnp.bfloat16), preferred_element_type=jnp.float32)
            if i == 0:
                dk_sum[cols, :] = dk
                dv_sum[cols, :] = dv
            else:
                dk_sum[cols, :] += dk
                dv_sum[cols, :] += dv
        all_ref[at, :width] = jnp.concatenate(parts, axis=1).astype(jnp.bfloat16)
    all_ref[:, width : 2 * width] = (dk_sum[...].T * SCORE_SCALE).astype(jnp.bfloat16)
    all_ref[:, 2 * width :] = dv_sum[...].T.astype(jnp.bfloat16)
    sums_ref[...] = jnp.zeros_like(sums_ref)
    sums_ref[:1, :] = jnp.sum(all_ref[...].astype(jnp.float32), axis=0, keepdims=True)
    for i, part_ref in enumerate(part_refs):
        at = slice(i * shard_len, (i + 1) * shard_len)
        part = dot_right_t(all_ref[at, :width], weight_refs[0][...])
        part = part + dot_right_t(all_ref[at, width : 2 * width], weight_refs[1][...])
        part = part + dot_right_t(all_ref[at, 2 * width :], weight_refs[2][...])
        part_ref[...] = part.astype(part_ref.dtype)


def attend_back(
    place, length, queries, keys_all, values_all, lse, mixed_pieces, grad_pieces, weights
):
    rows, width = queries.shape
    shard_len, model_width = mixed_pieces[0].shape[0], weights[0].shape[0]
    smem, vmem = pl.BlockSpec(memory_space=pltpu.SMEM), pl.BlockSpec(memory_space=pltpu.VMEM)
    arrays = (queries, keys_all, values_all, lse, *mixed_pieces, *grad_pieces, *weights)
    parts = [jax.ShapeDtypeStruct((shard_len, model_width), jnp.float32)] + [
        jax.ShapeDtypeStruct((shard_len, model_width), jnp.bfloat16)
    ] * (len(mixed_pieces) - 1)
    return pl.pallas_call(
        attend_back_kernel,
        out_shape=(
            jax.ShapeDtypeStruct((rows, 3 * width), jnp.bfloat16),
            jax.ShapeDtypeStruct((16, 3 * width), jnp.float32),
            *parts,
        ),
        in_specs=[smem, smem] + [vmem] * len(arrays),
        out_specs=(vmem,) * (2 + len(parts)),
        scratch_shapes=[pltpu.VMEM((width, rows), jnp.float32)] * 2,
        compiler_params=pltpu.CompilerParams(vmem_limit_bytes=48 << 20),
        cost_estimate=pl.CostEstimate(
            flops=20 * rows * width * rows,
            bytes_accessed=8 << 20,
            transcendentals=rows * rows * (width // HEAD),
        ),
        name="attend_back",
    )(place.reshape(1), length.reshape(1), *arrays)


def vector_kernel(
    place_ref, one_ref, two_ref, resid_ref, normed_one_ref, normed_two_ref, cot_ref, pre_ref, out_ref
):
    seq_count, _, head_width = out_ref.shape
    model_width = one_ref.shape[1]
    resid = resid_ref[...]
    cot = cot_ref[...].astype(jnp.float32)
    rows = [
        one_ref[...],
        two_ref[...],
        resid * normed_one_ref[...],
        resid,
        cot * normed_two_ref[...],
        cot,
    ]
    out_ref[...] = jnp.zeros_like(out_ref)
    for k, values in enumerate(rows):
        total = jnp.sum(values, axis=0, keepdims=True)
        for j in range(seq_count):
            out_ref[j, 2 + k : 3 + k, :] = total[:, j * head_width : (j + 1) * head_width]
    pre = pre_ref[...].astype(jnp.float32)
    per_place = pre.shape[1] // seq_count // model_width
    totals = [
        jnp.sum(pre[:, k * model_width : (k + 1) * model_width], axis=0, keepdims=True)
        for k in range(seq_count * per_place)
    ]
    for k in range(seq_count):
        owner = (place_ref[0] + seq_count - k) % seq_count
        for i in range(per_place):
            row = 8 + owner * per_place + i
            total = totals[k * per_place + i]
            for j in range(seq_count):
                out_ref[j, pl.ds(row, 1), :] = total[:, j * head_width : (j + 1) * head_width]


def vector_sums(place, seq_count, head_width, *arrays):
    return pl.pallas_call(
        vector_kernel,
        out_shape=jax.ShapeDtypeStruct((seq_count, 16, head_width), jnp.float32),
        in_specs=[pl.BlockSpec(memory_space=pltpu.SMEM)]
        + [pl.BlockSpec(memory_space=pltpu.VMEM)] * len(arrays),
        out_specs=pl.BlockSpec(memory_space=pltpu.VMEM),
        compiler_params=pltpu.CompilerParams(vmem_limit_bytes=32 << 20),
        name="vector_sums",
    )(place.reshape(1), *arrays)


def layer(
    tokens,
    cotangent,
    lengths,
    w_attn,
    attn_first,
    attn_second,
    w_ffn,
    ffn_first,
    ffn_second,
    vectors,
    vec_first,
    vec_second,
):
    bf16, f32 = jnp.bfloat16, jnp.float32
    _, shard_len, model_width = tokens.shape
    seq_count, fsdp_count = lax.axis_size("seq"), lax.axis_size("fsdp")
    place, member = lax.axis_index("seq"), lax.axis_index("fsdp")
    _, row_shard, head_width = w_attn.shape
    hidden_shard = w_ffn.shape[2]
    vec_rows, vec_shard = vectors.shape
    token_rows = tokens.reshape(shard_len, model_width)
    cot_half = cotangent.reshape(shard_len, model_width)
    cot_rows = cot_half.astype(f32)
    bits = list(range(fsdp_count.bit_length() - 1))

    own_shard = jnp.concatenate([w_ffn[0], w_ffn[1], w_attn[3]], axis=1).astype(bf16)
    early_shard = jnp.concatenate([w_ffn[0], w_attn[3]], axis=1).astype(bf16)
    late_shard = w_ffn[1].astype(bf16)
    vec_placed = lax.dynamic_update_slice(
        jnp.zeros((16, head_width), bf16), vectors.astype(bf16), (0, member * vec_shard)
    )
    qkv_shard = jnp.concatenate(
        [w_attn[:3].astype(bf16).reshape(3 * row_shard, head_width), vec_placed], axis=0
    )
    own_all = lax.all_gather(own_shard, "fsdp", axis=0, tiled=True)
    token_pieces = gather_behind(token_rows)
    early_pieces = gather_behind(early_shard)
    qkv_all = lax.all_gather(qkv_shard, "fsdp", axis=0, tiled=False)
    early_pieces = after(early_pieces, qkv_all)
    early_cat = jnp.concatenate(
        [piece[:, :hidden_shard] for piece in early_pieces[1:]]
        + [piece[:, hidden_shard:] for piece in early_pieces[1:]],
        axis=1,
    )
    early_all = lax.all_gather(early_cat, "fsdp", axis=0, tiled=True)
    late_pieces = gather_behind(after(late_shard, early_pieces[1]))[1:]

    def times(left, parts):
        return jnp.concatenate(
            [jnp.dot(left, part, preferred_element_type=f32) for part in parts], axis=1
        )

    def times_t(left, parts):
        width = parts[0].shape[1]
        return dot_right_t(left[:, :width], parts[0]) + dot_right_t(left[:, width:], parts[1])

    w_qkv = [
        qkv_all[:, i * row_shard : (i + 1) * row_shard].reshape(model_width, head_width)
        for i in range(3)
    ]
    vec_own = jnp.sum(qkv_all[:, 3 * row_shard :].astype(f32), axis=0)[:vec_rows]
    vec_near = [piece.astype(f32) for piece in gather_behind(vec_own.astype(bf16))]

    def near(order):
        return sum(jnp.where(order == r, piece, 0.0) for r, piece in enumerate(vec_near))

    vec_wide = jnp.concatenate(
        [near((place - j) % seq_count) for j in range(seq_count)], axis=1
    )
    up_bias = turn_blocks(vec_wide[8:12].reshape(seq_count, hidden_shard)).reshape(-1)

    valid_len = lengths[0]
    queries, keys_all, values_all, lse, *mixed_pieces = attend(
        place, valid_len, vec_own[:2], token_pieces, w_qkv
    )
    late_pieces = after(late_pieces, mixed_pieces)
    late_all = lax.all_gather(jnp.concatenate(late_pieces, axis=1), "fsdp", axis=0, tiled=True)
    up_parts = [own_all[:, :hidden_shard], early_all[:, : hidden_shard * (seq_count - 1)]]
    down_parts = [own_all[:, hidden_shard : 2 * hidden_shard], late_all]
    out_parts = [own_all[:, 2 * hidden_shard :], early_all[:, hidden_shard * (seq_count - 1) :]]
    mixed_rows = jnp.concatenate(swap_behind(mixed_pieces), axis=1)

    hidden_one = token_rows.astype(f32) + times_t(mixed_rows, out_parts) + vec_wide[2]
    normed_one, inv_one = layer_norm(hidden_one)
    resid_one = normed_one * vec_wide[4] + vec_wide[5]
    resid_half = resid_one.astype(bf16)
    preact = times(resid_half, up_parts) + up_bias
    activation, gelu_slope = gelu_pair(preact)
    act_half = activation.astype(bf16)
    hidden_two = resid_one + times_t(act_half, down_parts) + vec_wide[3]
    normed_two, inv_two = layer_norm(hidden_two)
    block_out = (normed_two * vec_wide[6] + vec_wide[7]).astype(bf16)
    grad_two = norm_back(cot_rows * vec_wide[6], normed_two, inv_two)
    grad_two_half = grad_two.astype(bf16)

    def outer(left, right):
        return lax.dot_general(
            left, right, (((0,), (0,)), ((), ())), preferred_element_type=f32
        ).astype(bf16)

    def total_of(pieces):
        total = pieces[0].astype(f32)
        for piece in pieces[1:]:
            total = total + piece.astype(f32)
        return total

    def halves_of(pieces):
        return [piece.astype(bf16) for piece in pieces]

    down_local, grad_two_half = lax.optimization_barrier(
        (outer(grad_two_half, act_half), grad_two_half)
    )
    down_part = lax.psum_scatter(down_local, "fsdp", scatter_dimension=0, tiled=True)
    grad_pre_half = (times(grad_two_half, down_parts) * gelu_slope).astype(bf16)
    up_kept, up_sent = halving(
        outer(resid_half, grad_pre_half).reshape(fsdp_count, row_shard, -1), bits[0], True
    )
    up_sent, up_kept, grad_pre_half = lax.optimization_barrier((up_sent, up_kept, grad_pre_half))
    up_received = swapped(up_sent, bits[0])
    grad_resid = grad_two + times_t(grad_pre_half, up_parts)
    grad_one = norm_back(grad_resid * vec_wide[4], normed_one, inv_one)
    grad_one_half = grad_one.astype(bf16)
    grad_mixed = times(grad_one_half, out_parts).astype(bf16)
    grad_pieces = swap_behind(jnp.split(grad_mixed, seq_count, axis=1))

    out_kept, out_sent = halving(
        outer(after(grad_one_half, grad_mixed), mixed_rows).reshape(fsdp_count, row_shard, -1),
        bits[0],
        True,
    )
    out_received = swapped(out_sent, bits[0])
    vec_blocks = vector_sums(
        place,
        seq_count,
        head_width,
        grad_one,
        grad_two,
        grad_resid,
        normed_one,
        normed_two,
        cot_half,
        grad_pre_half,
    )
    vec_order = turn_blocks(vec_blocks)
    vec_moved = swap_behind([vec_order[r] for r in range(seq_count)])
    up_wide = joined(up_kept, up_received)
    out_wide = joined(out_kept, out_received)
    near_places = seq_count // 2
    up_cut, out_cut = near_places * hidden_shard, near_places * head_width
    wide = [
        jnp.concatenate([up_wide[..., :up_cut], out_wide[..., :out_cut]], axis=-1),
        jnp.concatenate([up_wide[..., up_cut:], out_wide[..., out_cut:]], axis=-1),
    ]
    routes = [list(bits[1:]), list(reversed(bits[1:]))]
    wide_moving = []
    for half, route, low in zip(wide, routes, (True, False), strict=True):
        kept, sent = halving(half, route[0], low)
        wide_moving.append((kept, swapped(sent, route[0])))
        grad_pieces = after(grad_pieces, sent)

    grad_qkv, head_sums, input_own, *input_parts = attend_back(
        place,
        valid_len,
        queries,
        keys_all,
        values_all,
        lse,
        mixed_pieces,
        grad_pieces,
        w_qkv,
    )
    input_moved = swap_behind([input_own, *input_parts])
    vec_part = sum(vec_moved)
    vec_lines = jnp.concatenate(
        [head_sums[:1, :head_width], head_sums[:1, 2 * head_width :], vec_part[2:]], axis=0
    )
    vec_lines = jnp.pad(vec_lines, ((0, 0), (0, 2 * head_width)))
    token_all = jnp.concatenate(token_pieces, axis=0)
    qkv_local = lax.dot_general(
        token_all, grad_qkv, (((0,), (0,)), ((), ())), preferred_element_type=f32
    ).astype(bf16)
    qkv_blocks = jnp.concatenate(
        [
            qkv_local.reshape(fsdp_count, row_shard, 3 * head_width),
            jnp.broadcast_to(
                vec_lines.astype(bf16)[None], (fsdp_count, 16, 3 * head_width)
            ),
        ],
        axis=1,
    )

    def place_pieces(half, count):
        ups, outs = half[:, : count * hidden_shard], half[:, count * hidden_shard :]
        return [
            jnp.concatenate(
                [
                    ups[:, r * hidden_shard : (r + 1) * hidden_shard],
                    outs[:, r * head_width : (r + 1) * head_width],
                ],
                axis=1,
            )
            for r in range(count)
        ]

    qkv_kept, qkv_sent = halving(qkv_blocks, bits[0], True)
    qkv_received = swapped(qkv_sent, bits[0])
    step = qkv_sent
    down_moved = None
    for at in range(1, len(bits)):
        moving = []
        for (kept, received), route, low in zip(wide_moving, routes, (True, False), strict=True):
            half = joined(kept, after(received, step))
            if at < len(bits) - 1:
                kept, sent = halving(half, route[at], low)
                moving.append((kept, swapped(sent, route[at])))
                step = sent
            else:
                moving.append(half[0])
        wide_moving = moving
        if down_moved is None:
            down_pieces = jnp.split(after(down_part, step), seq_count, axis=1)
            down_moved = swap_behind(down_pieces)
            step = down_pieces
        if at < len(bits) - 1:
            qkv_half = joined(qkv_kept, after(qkv_received, step))
            qkv_kept, qkv_sent = halving(qkv_half, bits[at], True)
            qkv_received = swapped(qkv_sent, bits[at])
            step = qkv_sent
    wide_pieces = place_pieces(wide_moving[0], near_places) + place_pieces(
        wide_moving[1], seq_count - near_places
    )
    wide_sent = halves_of(wide_pieces[1:])
    wide_moved = swap_behind([wide_pieces[0]] + wide_sent)
    qkv_half = joined(qkv_kept, after(qkv_received, wide_sent))
    qkv_kept, qkv_sent = halving(qkv_half, bits[-1], True)
    qkv_sum = joined(qkv_kept, swapped(qkv_sent, bits[-1]))[0]
    down_sum = total_of([down_moved[0]] + after(down_moved[1:], qkv_sum))
    input_grad = grad_one + total_of([input_moved[0]] + after(input_moved[1:], down_sum))
    up_out_sum = total_of([wide_moved[0]] + after(wide_moved[1:], input_grad))

    token_total = shard_len * seq_count * fsdp_count
    grad_scale = float(token_total) ** (-0.5)
    attn_grad = grad_scale * jnp.concatenate(
        [
            qkv_sum[:row_shard].reshape(row_shard, 3, head_width).transpose(1, 0, 2),
            up_out_sum[None, :, hidden_shard:],
        ],
        axis=0,
    )
    ffn_grad = grad_scale * jnp.stack([up_out_sum[:, :hidden_shard], down_sum])
    vec_grad = grad_scale * lax.dynamic_slice(
        qkv_sum[row_shard:], (0, member * vec_shard), (vec_rows, vec_shard)
    )
    attn_new, attn_one, attn_two = adam_step(
        w_attn, attn_grad, attn_first, attn_second, WEIGHT_DECAY
    )
    ffn_new, ffn_one, ffn_two = adam_step(w_ffn, ffn_grad, ffn_first, ffn_second, WEIGHT_DECAY)
    vec_new, vec_one, vec_two = adam_step(vectors, vec_grad, vec_first, vec_second, 0.0)
    return (
        block_out.reshape(tokens.shape),
        input_grad.reshape(tokens.shape),
        attn_grad,
        ffn_grad,
        vec_grad,
        attn_new,
        attn_one,
        attn_two,
        ffn_new,
        ffn_one,
        ffn_two,
        vec_new,
        vec_one,
        vec_two,
    )


def solution(mesh):
    placed = (
        P("fsdp", "seq", None),
        P("fsdp", "seq", None),
        P("fsdp"),
        P(None, "fsdp", "seq"),
        P(None, "fsdp", "seq"),
        P(None, "fsdp", "seq"),
        P(None, "fsdp", "seq"),
        P(None, "fsdp", "seq"),
        P(None, "fsdp", "seq"),
        P(None, ("seq", "fsdp")),
        P(None, ("seq", "fsdp")),
        P(None, ("seq", "fsdp")),
    )
    return jax.shard_map(
        layer,
        mesh=mesh,
        in_specs=placed,
        out_specs=(
            P("fsdp", "seq", None),
            P("fsdp", "seq", None),
            P(None, "fsdp", "seq"),
            P(None, "fsdp", "seq"),
            P(None, ("seq", "fsdp")),
            P(None, "fsdp", "seq"),
            P(None, "fsdp", "seq"),
            P(None, "fsdp", "seq"),
            P(None, "fsdp", "seq"),
            P(None, "fsdp", "seq"),
            P(None, "fsdp", "seq"),
            P(None, ("seq", "fsdp")),
            P(None, ("seq", "fsdp")),
            P(None, ("seq", "fsdp")),
        ),
        check_vma=False,
    )
```

profile of v0, /device:TPU:8, one launch (start us, length us, event | category | flops | bytes accessed | tf_op | source)
XLA Modules:
  0.0 302.8 jit_solution(568091130654204250)
XLA Ops:
  16.1 11.9 %all-gather.1 = bf16[8,304,192]{1,2,0:T(8,128)(2,1)S(1)} all-gather(bf16[1,304,192]{1,2,0:T(8,128)(2,1)S(1)} %copy.152), channel_id=2, replica_groups=mesh['seq'=4,'fsdp'=8] {'fsdp'}, dimensions={0}, use_global_device_ids=true | all-gather | bytes 1050624 | tf_op jit(solution)/shard_map/all_gather | solution.py:346
  40.4 2.6 collective-permute-start.13
  45.9 26.8 %collective-permute-done.1.refs_2_ = bf16[256,768]{1,0:T(8,128)(2,1)S(1)} collective-permute-done((bf16[256,768]{1,0:T(8,128)(2,1)S(1)}, bf16[256,768]{1,0:T(8,128)(2,1)S(1)}, u32[]{:S(2)}, u32[]{:S(2)}) %collective-permute-start.1) | collective-permute-done | bytes 393248 | tf_op jit(solution)/shard_map/ppermute | solution.py:54
  74.9 9.0 %attend.1 = (bf16[1024,192]{1,0:T(8,128)(2,1)S(1)}, bf16[1024,192]{1,0:T(8,128)(2,1)S(1)}, bf16[1024,192]{1,0:T(8,128)(2,1)S(1)}, f32[1024,8]{1,0:T(8,128)S(1)},...) custom-call(s32[1]{0:T(128)} %bitcast.1.place_ref, ...), custom_call_target="tpu_custom_call" | custom-call | flops 4127195136 | bytes 8388608 | tf_op jit(solution)/shard_map/attend/pallas_call | solution.py:159
  98.0 2.8 collective-permute-start.3
  101.8 5.9 %collective-permute-done.5 = bf16[256,192]{1,0:T(8,128)(2,1)S(1)} collective-permute-done((bf16[256,192]{1,0:T(8,128)(2,1)S(1)}, bf16[256,192]{1,0:T(8,128)(2,1)S(1)}, u32[]{:S(2)}, u32[]{:S(2)}) %collective-permute-start.5) | collective-permute-done | bytes 98336 | tf_op jit(solution)/shard_map/ppermute | solution.py:54
  118.0 19.6 %all-gather.10.cloned.1.call-done = bf16[768,2304]{1,0:T(8,128)(2,1)} async-done(((bf16[96,2304]{1,0:T(8,128)(2,1)}), bf16[768,2304]{1,0:T(8,128)(2,1)}) %all-gather.10.cloned.1.call-update) | async-done | bytes 3538960 | tf_op jit(solution)/shard_map/all_gather | solution.py:385
  137.7 3.1 %fusion.26 = f32[256,768]{1,0:T(8,128)S(1)} fusion(bf16[768,2304]{1,0:T(8,128)(2,1)} %all-gather.10.cloned.1.call-done, bf16[256,3072]{1,0:T(8,128)(2,1)S(1)} %multiply_convert_fusion), kind=kOutput, calls=%fused_computation.46 | convolution fusion | flops 905969664 | bytes 5505024 | tf_op jit(solution)/shard_map/dot_general | solution.py:45
  144.9 3.6 %convolution_convert_fusion.1 = bf16[768,3072]{1,0:T(8,128)(2,1)} fusion(bf16[256,768]{1,0:T(8,128)(2,1)S(1)} %get-tuple-element.75, bf16[256,3072]{1,0:T(8,128)(2,1)S(1)} %copy-done.46), kind=kOutput, calls=%fused_computation.1 | convolution fusion | flops 1210318848 | bytes 6684672 | tf_op jit(solution)/shard_map/dot_general | solution.py:405
  148.5 3.2 %fusion.110 = f32[256,2304]{1,0:T(8,128)S(1)} fusion(bf16[256,768]{1,0:T(8,128)(2,1)S(1)} %get-tuple-element.75, bf16[768,2304]{1,0:T(8,128)(2,1)} %all-gather.10.cloned.1.call-done), kind=kOutput, calls=%fused_computation.229 | convolution fusion | flops 905969664 | bytes 6291456 | tf_op jit(solution)/shard_map/dot_general | solution.py:358
  156.4 2.6 dynamic-slice_bitcast_fusion
  169.9 2.4 collective-permute-start.26
  172.3 2.4 collective-permute-start.25
  183.0 2.5 convert_add_fusion
  194.7 10.2 %attend_back.1 = (bf16[1024,576]{1,0:T(8,128)(2,1)}, f32[16,576]{1,0:T(8,128)S(1)}, f32[256,768]{1,0:T(8,128)}, bf16[256,768]{1,0:T(8,128)(2,1)S(1)}, bf16[256,7...) custom-call(s32[1]{0:T(128)} %bitcast.1.place_ref, s32[1]{0:T(128)S(6)} %copy.182.length_ref, ...), custom_call_target="tpu_custom_call" | custom-call | flops 4026531840 | bytes 8388608 | tf_op jit(solution)/shard_map/attend_back/pallas_call | solution.py:241
  208.3 3.4 %fusion.18 = bf16[768,576]{0,1:T(8,128)(2,1)} fusion(bf16[1024,576]{1,0:T(8,128)(2,1)} %get-tuple-element.96, bf16[256,768]{1,0:T(8,128)(2,1)S(1)} %copy-done.23, bf16[256,768]{1,0:T(8,128)(2,1)S(1)} %copy-done.21, bf16[256,768]{1,0:T(8,128)(2,1)S(1)} %copy-done.19, bf16[256,768]{1,0:T(8,128)(2,1)S(1)} %bitcast.116), kind=kOutput, calls=%fused_computation.36 | convolution fusion | flops 912703488 | bytes 3637248 | tf_op jit(solution)/shard_map/dot_general | solution.py:487
  214.2 3.3 %collective-permute-done.24 = bf16[2,96,1920]{2,1,0:T(8,128)(2,1)} collective-permute-done((bf16[2,96,1920]{2,1,0:T(8,128)(2,1)}, bf16[2,96,1920]{2,1,0:T(8,128)(2,1)}, u32[]{:S(2)}, u32[]{:S(2)}) %collective-permute-start.24) | collective-permute-done | bytes 737312 | tf_op jit(solution)/shard_map/ppermute | solution.py:101
  224.9 13.2 %reduce-scatter.2.cloned.1.call-done = bf16[96,3072]{1,0:T(8,128)(2,1)} async-done(((bf16[768,3072]{1,0:T(8,128)(2,1)}), bf16[96,3072]{1,0:T(8,128)(2,1)}) %reduce-scatter.2.cloned.1.call-update) | async-done | bytes 589840 | tf_op jit(solution)/shard_map/reduce_scatter | solution.py:421
  244.7 5.2 %collective-permute-done.34 = bf16[1,96,1920]{2,1,0:T(8,128)(2,1)S(1)} collective-permute-done((bf16[1,96,1920]{2,1,0:T(8,128)(2,1)}, bf16[1,96,1920]{2,1,0:T(8,128)(2,1)S(1)}, u32[]{:S(2)}, u32[]{:S(2)}) %collective-permute-start.34) | collective-permute-done | bytes 368672 | tf_op jit(solution)/shard_map/ppermute | solution.py:101
  253.3 7.6 %collective-permute-done.29 = bf16[96,768]{1,0:T(8,128)(2,1)S(1)} collective-permute-done((bf16[96,768]{1,0:T(8,128)(2,1)S(1)}, bf16[96,768]{1,0:T(8,128)(2,1)S(1)}, u32[]{:S(2)}, u32[]{:S(2)}) %collective-permute-start.29) | collective-permute-done | bytes 147488 | tf_op jit(solution)/shard_map/ppermute | solution.py:54
  263.3 3.4 %collective-permute-start.37 = (bf16[96,960]{1,0:T(8,128)(2,1)S(1)}, bf16[96,960]{1,0:T(8,128)(2,1)S(1)}, u32[]{:S(2)}, u32[]{:S(2)}) collective-permute-start(bf16[96,960]{1,0:T(8,128)(2,1)S(1)} %pad_maximum_fusion.8), channel_id=1, source_target_pairs={{0,16},{8,24},{16,0},{24,8},{1,17},{9,25},{17,1},{25,9},{2,18},{10... | collective-permute-start | bytes 552968 | tf_op jit(solution)/shard_map/ppermute | solution.py:54
  271.2 8.2 %collective-permute-done.37 = bf16[96,960]{1,0:T(8,128)(2,1)S(1)} collective-permute-done((bf16[96,960]{1,0:T(8,128)(2,1)S(1)}, bf16[96,960]{1,0:T(8,128)(2,1)S(1)}, u32[]{:S(2)}, u32[]{:S(2)}) %collective-permute-start.37) | collective-permute-done | bytes 184352 | tf_op jit(solution)/shard_map/ppermute | solution.py:54
  279.4 3.8 %collective-permute-done.38 = bf16[96,960]{1,0:T(8,128)(2,1)S(1)} collective-permute-done((bf16[96,960]{1,0:T(8,128)(2,1)S(1)}, bf16[96,960]{1,0:T(8,128)(2,1)S(1)}, u32[]{:S(2)}, u32[]{:S(2)}) %collective-permute-start.38) | collective-permute-done | bytes 184352 | tf_op jit(solution)/shard_map/ppermute | solution.py:54
  285.9 5.0 %collective-permute-done.35 = bf16[1,112,576]{2,1,0:T(8,128)(2,1)S(1)} collective-permute-done((bf16[1,112,576]{2,1,0:T(8,128)(2,1)S(1)}, bf16[1,112,576]{2,1,0:T(8,128)(2,1)S(1)}, u32[]{:S(2)}, u32[]{:S(2)}) %collective-permute-start.35) | collective-permute-done | bytes 129056 | tf_op jit(solution)/shard_map/ppermute | solution.py:101
  (390 shorter events, 124.8 us)
Async XLA Ops:
  7.2 101.2 %all-gather.8.cloned.1.call-start = ((), (), s32[]{:S(2)}) async-start(), calls=%async_computation.2 | async-start | bytes 5087232 | tf_op jit(solution)/shard_map/all_gather | solution.py:353
  9.3 18.7 %collective-permute-start.6 = (bf16[96,960]{1,0:T(8,128)(2,1)S(1)}, bf16[96,960]{1,0:T(8,128)(2,1)S(1)}, u32[]{:S(2)}, u32[]{:S(2)}) collective-permute-start(bf16[96,960]{1,0:T(8,128)(2,1)S(1)} %pad_maximum_fusion.6), channel_id=1, source_target_pairs={{0,8},{8,16},{16,24},{24,0},{1,9},{9,17},{17,25},{25,1},{2,10},{10... | collective-permute-start | bytes 552968 | tf_op jit(solution)/shard_map/ppermute | solution.py:54
  10.9 17.1 %collective-permute-start.7 = (bf16[96,960]{1,0:T(8,128)(2,1)S(1)}, bf16[96,960]{1,0:T(8,128)(2,1)S(1)}, u32[]{:S(2)}, u32[]{:S(2)}) collective-permute-start(bf16[96,960]{1,0:T(8,128)(2,1)S(1)} %pad_maximum_fusion.6), channel_id=1, source_target_pairs={{0,16},{8,24},{16,0},{24,8},{1,17},{9,25},{17,1},{25,9},{2,18},{10... | collective-permute-start | bytes 552968 | tf_op jit(solution)/shard_map/ppermute | solution.py:54
  12.0 17.5 %collective-permute-start.8 = (bf16[96,960]{1,0:T(8,128)(2,1)S(1)}, bf16[96,960]{1,0:T(8,128)(2,1)S(1)}, u32[]{:S(2)}, u32[]{:S(2)}) collective-permute-start(bf16[96,960]{1,0:T(8,128)(2,1)S(1)} %pad_maximum_fusion.6), channel_id=1, source_target_pairs={{0,24},{8,0},{16,8},{24,16},{1,25},{9,1},{17,9},{25,17},{2,26},{10... | collective-permute-start | bytes 552968 | tf_op jit(solution)/shard_map/ppermute | solution.py:54
  30.6 79.6 %all-gather.6.cloned.1.call-start = ((), (), s32[]{:S(2)}) async-start(), calls=%async_computation.1 | async-start | bytes 3096576 | tf_op jit(solution)/shard_map/all_gather | solution.py:343
  31.5 106.2 %all-gather.10.cloned.1.call-start = ((), (), s32[]{:S(2)}) async-start(), calls=%async_computation.3 | async-start | bytes 3981312 | tf_op jit(solution)/shard_map/all_gather | solution.py:385
  31.6 41.1 %collective-permute-start.1 = (bf16[256,768]{1,0:T(8,128)(2,1)S(1)}, bf16[256,768]{1,0:T(8,128)(2,1)S(1)}, u32[]{:S(2)}, u32[]{:S(2)}) collective-permute-start(bf16[256,768]{1,0:T(8,128)(2,1)S(1)} %bitcast.113), channel_id=1, source_target_pairs={{0,16},{8,24},{16,0},{24,8},{1,17},{9,25},{17,1},{25,9},{2,18},{10... | collective-permute-start | bytes 1179656 | tf_op jit(solution)/shard_map/ppermute | solution.py:54
  33.8 41.1 %collective-permute-start.2 = (bf16[256,768]{1,0:T(8,128)(2,1)S(1)}, bf16[256,768]{1,0:T(8,128)(2,1)S(1)}, u32[]{:S(2)}, u32[]{:S(2)}) collective-permute-start(bf16[256,768]{1,0:T(8,128)(2,1)S(1)} %bitcast.114), channel_id=1, source_target_pairs={{0,24},{8,0},{16,8},{24,16},{1,25},{9,1},{17,9},{25,17},{2,26},{10... | collective-permute-start | bytes 1179656 | tf_op jit(solution)/shard_map/ppermute | solution.py:54
  39.7 47.6 %collective-permute-start.12 = (bf16[96,768]{1,0:T(8,128)(2,1)S(1)}, bf16[96,768]{1,0:T(8,128)(2,1)S(1)}, u32[]{:S(2)}, u32[]{:S(2)}) collective-permute-start(bf16[96,768]{1,0:T(8,128)(2,1)S(1)} %copy-done.68), channel_id=1, source_target_pairs={{0,8},{8,16},{16,24},{24,0},{1,9},{9,17},{17,25},{25,1},{2,10},{10... | collective-permute-start | bytes 442376 | tf_op jit(solution)/shard_map/ppermute | solution.py:54
  40.4 46.9 %collective-permute-start.13 = (bf16[96,768]{1,0:T(8,128)(2,1)S(1)}, bf16[96,768]{1,0:T(8,128)(2,1)S(1)}, u32[]{:S(2)}, u32[]{:S(2)}) collective-permute-start(bf16[96,768]{1,0:T(8,128)(2,1)S(1)} %copy-done.68), channel_id=1, source_target_pairs={{0,16},{8,24},{16,0},{24,8},{1,17},{9,25},{17,1},{25,9},{2,18},{10... | collective-permute-start | bytes 442376 | tf_op jit(solution)/shard_map/ppermute | solution.py:54
  43.6 43.7 %collective-permute-start.14 = (bf16[96,768]{1,0:T(8,128)(2,1)S(1)}, bf16[96,768]{1,0:T(8,128)(2,1)S(1)}, u32[]{:S(2)}, u32[]{:S(2)}) collective-permute-start(bf16[96,768]{1,0:T(8,128)(2,1)S(1)} %copy-done.68), channel_id=1, source_target_pairs={{0,24},{8,0},{16,8},{24,16},{1,25},{9,1},{17,9},{25,17},{2,26},{10... | collective-permute-start | bytes 442376 | tf_op jit(solution)/shard_map/ppermute | solution.py:54
  88.1 150.0 %reduce-scatter.2.cloned.1.call-start = ((), (), s32[]{:S(2)}) async-start(), calls=%async_computation.4 | async-start | bytes 5308416 | tf_op jit(solution)/shard_map/reduce_scatter | solution.py:421
  160.9 21.7 %collective-permute-start.18 = (bf16[4,96,3072]{2,1,0:T(8,128)(2,1)}, bf16[4,96,3072]{2,1,0:T(8,128)(2,1)}, u32[]{:S(2)}, u32[]{:S(2)}) collective-permute-start(bf16[4,96,3072]{2,1,0:T(8,128)(2,1)} %get-tuple-element.82), channel_id=1, source_target_pairs={{0,1},{1,0},{2,3},{3,2},{4,5},{5,4},{6,7},{7,6},{8,9},{9,8},{10,11... | collective-permute-start | bytes 7077896 | tf_op jit(solution)/shard_map/ppermute | solution.py:101
  164.8 16.4 %collective-permute-start.19 = (bf16[4,96,768]{2,1,0:T(8,128)(2,1)}, bf16[4,96,768]{2,1,0:T(8,128)(2,1)}, u32[]{:S(2)}, u32[]{:S(2)}) collective-permute-start(bf16[4,96,768]{2,1,0:T(8,128)(2,1)} %dynamic-slice_bitcast_fusion.2), channel_id=1, source_target_pairs={{0,1},{1,0},{2,3},{3,2},{4,5},{5,4},{6,7},{7,6},{8,9},{9,8},{10,11... | collective-permute-start | bytes 1769480 | tf_op jit(solution)/shard_map/ppermute | solution.py:101
  187.3 30.2 %collective-permute-start.24 = (bf16[2,96,1920]{2,1,0:T(8,128)(2,1)}, bf16[2,96,1920]{2,1,0:T(8,128)(2,1)}, u32[]{:S(2)}, u32[]{:S(2)}) collective-permute-start(bf16[2,96,1920]{2,1,0:T(8,128)(2,1)} %fusion.40), channel_id=1, source_target_pairs={{0,2},{1,3},{2,0},{3,1},{4,6},{5,7},{6,4},{7,5},{8,10},{9,11},{10,... | collective-permute-start | bytes 2211848 | tf_op jit(solution)/shard_map/ppermute | solution.py:101
  192.6 27.5 %collective-permute-start.23 = (bf16[2,96,1920]{2,1,0:T(8,128)(2,1)}, bf16[2,96,1920]{2,1,0:T(8,128)(2,1)}, u32[]{:S(2)}, u32[]{:S(2)}) collective-permute-start(bf16[2,96,1920]{2,1,0:T(8,128)(2,1)} %fusion.39), channel_id=1, source_target_pairs={{0,4},{1,5},{2,6},{3,7},{4,0},{5,1},{6,2},{7,3},{8,12},{9,13},{10,... | collective-permute-start | bytes 2211848 | tf_op jit(solution)/shard_map/ppermute | solution.py:101
  204.9 58.4 %collective-permute-start.20 = (bf16[256,768]{1,0:T(8,128)(2,1)S(1)}, bf16[256,768]{1,0:T(8,128)(2,1)S(1)}, u32[]{:S(2)}, u32[]{:S(2)}) collective-permute-start(bf16[256,768]{1,0:T(8,128)(2,1)S(1)} %get-tuple-element.92), channel_id=1, source_target_pairs={{0,8},{8,16},{16,24},{24,0},{1,9},{9,17},{17,25},{25,1},{2,10},{10... | collective-permute-start | bytes 1179656 | tf_op jit(solution)/shard_map/ppermute | solution.py:54
  204.9 61.9 %collective-permute-start.21 = (bf16[256,768]{1,0:T(8,128)(2,1)S(1)}, bf16[256,768]{1,0:T(8,128)(2,1)}, u32[]{:S(2)}, u32[]{:S(2)}) collective-permute-start(bf16[256,768]{1,0:T(8,128)(2,1)S(1)} %get-tuple-element.93), channel_id=1, source_target_pairs={{0,16},{8,24},{16,0},{24,8},{1,17},{9,25},{17,1},{25,9},{2,18},{10... | collective-permute-start | bytes 1179656 | tf_op jit(solution)/shard_map/ppermute | solution.py:54
  206.3 62.5 %collective-permute-start.22 = (bf16[256,768]{1,0:T(8,128)(2,1)S(1)}, bf16[256,768]{1,0:T(8,128)(2,1)}, u32[]{:S(2)}, u32[]{:S(2)}) collective-permute-start(bf16[256,768]{1,0:T(8,128)(2,1)S(1)} %get-tuple-element.94), channel_id=1, source_target_pairs={{0,24},{8,0},{16,8},{24,16},{1,25},{9,1},{17,9},{25,17},{2,26},{10... | collective-permute-start | bytes 1179656 | tf_op jit(solution)/shard_map/ppermute | solution.py:54
  217.5 21.7 %collective-permute-start.31 = (bf16[4,112,576]{2,1,0:T(8,128)(2,1)}, bf16[4,112,576]{2,1,0:T(8,128)(2,1)}, u32[]{:S(2)}, u32[]{:S(2)}) collective-permute-start(bf16[4,112,576]{2,1,0:T(8,128)(2,1)} %fusion.45), channel_id=1, source_target_pairs={{0,1},{1,0},{2,3},{3,2},{4,5},{5,4},{6,7},{7,6},{8,9},{9,8},{10,11... | collective-permute-start | bytes 1548296 | tf_op jit(solution)/shard_map/ppermute | solution.py:101
  220.1 22.0 %collective-permute-start.33 = (bf16[1,96,1920]{2,1,0:T(8,128)(2,1)}, bf16[1,96,1920]{2,1,0:T(8,128)(2,1)}, u32[]{:S(2)}, u32[]{:S(2)}) collective-permute-start(bf16[1,96,1920]{2,1,0:T(8,128)(2,1)} %dynamic-slice_convert_fusion.2), channel_id=1, source_target_pairs={{0,4},{1,5},{2,6},{3,7},{4,0},{5,1},{6,2},{7,3},{8,12},{9,13},{10,... | collective-permute-start | bytes 1105928 | tf_op jit(solution)/shard_map/ppermute | solution.py:101
  260.9 24.2 %collective-permute-start.32 = (bf16[2,112,576]{2,1,0:T(8,128)(2,1)S(1)}, bf16[2,112,576]{2,1,0:T(8,128)(2,1)S(1)}, u32[]{:S(2)}, u32[]{:S(2)}) collective-permute-start(bf16[2,112,576]{2,1,0:T(8,128)(2,1)S(1)} %fusion.67), channel_id=1, source_target_pairs={{0,2},{1,3},{2,0},{3,1},{4,6},{5,7},{6,4},{7,5},{8,10},{9,11},{10,... | collective-permute-start | bytes 774152 | tf_op jit(solution)/shard_map/ppermute | solution.py:101
  263.3 16.0 %collective-permute-start.37 = (bf16[96,960]{1,0:T(8,128)(2,1)S(1)}, bf16[96,960]{1,0:T(8,128)(2,1)S(1)}, u32[]{:S(2)}, u32[]{:S(2)}) collective-permute-start(bf16[96,960]{1,0:T(8,128)(2,1)S(1)} %pad_maximum_fusion.8), channel_id=1, source_target_pairs={{0,16},{8,24},{16,0},{24,8},{1,17},{9,25},{17,1},{25,9},{2,18},{10... | collective-permute-start | bytes 552968 | tf_op jit(solution)/shard_map/ppermute | solution.py:54
  266.8 16.4 %collective-permute-start.38 = (bf16[96,960]{1,0:T(8,128)(2,1)S(1)}, bf16[96,960]{1,0:T(8,128)(2,1)S(1)}, u32[]{:S(2)}, u32[]{:S(2)}) collective-permute-start(bf16[96,960]{1,0:T(8,128)(2,1)S(1)} %pad_maximum_fusion.7), channel_id=1, source_target_pairs={{0,24},{8,0},{16,8},{24,16},{1,25},{9,1},{17,9},{25,17},{2,26},{10... | collective-permute-start | bytes 552968 | tf_op jit(solution)/shard_map/ppermute | solution.py:54
  (114 other events, 916.3 us)
Sparse Core Ops, SparseCore 0:
  30.7 38.1 all-gather.7
  71.4 30.5 all-gather.5
  103.8 33.8 all-gather.9
  165.2 72.8 reduce-scatter.1
where the time goes:
time: 307 us; the launch traced here: 303 us
  waiting for transfers between devices  106 us (35%)
  starting transfers between devices  52.5 us (17%)
  local copies, waits for them, and re-layouts  41.2 us (13%)
  matrix products  29.3 us (10%)
  other arithmetic  25.5 us (8%)
  Pallas kernels  19.9 us (6%)
  between operations  16.3 us (5%)
  blocking collectives  11.9 us (4%)
    ppermute x30, waiting for transfers between devices, from_behind(): lax.ppermute(piece, 'seq', [(i, (i + distance) % count) for i in range(co...  59.9 us
    ppermute x30, starting transfers between devices, from_behind(): lax.ppermute(piece, 'seq', [(i, (i + distance) % count) for i in range(co...  43.9 us
    unnamed x197, local copies, waits for them, and re-layouts  22.6 us
    all_gather x1, waiting for transfers between devices, layer(): lax.all_gather(jnp.concatenate(late_pieces, axis=1), 'fsdp', axis=0, tile...  19.6 us
    ppermute x9, waiting for transfers between devices, swapped(): return lax.ppermute(sent, 'fsdp', pairs)  13.5 us
    reduce_scatter x1, waiting for transfers between devices, layer(): lax.psum_scatter(down_local, 'fsdp', scatter_dimension=0, tiled=True)  13.2 us
    all_gather x1, blocking collectives, layer(): qkv_all = lax.all_gather(qkv_shard, 'fsdp', axis=0, tiled=False)  11.9 us
    pallas_call x1, Pallas kernels, attend_back(): pl.pallas_call(attend_back_kernel, out_shape=(jax.ShapeDtypeStruct((rows,...  10.2 us
  transfers between devices with their start and end apart: 43, of which 16 were waited for; matrix products, arithmetic and copies ran while one was open for 17% of the time, Pallas kernels for 7%

commit v1 on v0

--- a/solution.py
+++ b/solution.py
@@ -4,6 +4,7 @@
 import jax.numpy as jnp
 from jax import lax
 from jax.experimental import pallas as pl
+from jax.experimental.layout import Layout, with_layout_constraint
 from jax.experimental.pallas import tpu as pltpu
 from jax.sharding import PartitionSpec as P
 
@@ -108,25 +109,33 @@
 def attend_kernel(
     place_ref, length_ref, bias_ref, *refs
 ):
-    count = (len(refs) - 3 - 4) // 2
+    count = (len(refs) - 3 - 4 - 2) // 2
     token_refs, weight_refs = refs[:count], refs[count : count + 3]
     q_ref, k_ref, v_ref, lse_ref = refs[count + 3 : count + 7]
-    mixed_refs = refs[count + 7 :]
+    mixed_refs, (mixed_all, token_all) = refs[count + 7 : -2], refs[-2:]
     shard_len = token_refs[0].shape[0]
     _, width = q_ref.shape
     for r, token_ref in enumerate(token_refs):
-        piece = token_ref[...]
+        token_all[r * shard_len : (r + 1) * shard_len, :] = token_ref[...]
+
+    def project(i, carry):
+        at = pl.ds(pl.multiple_of(i * shard_len, shard_len), shard_len)
+        piece = token_all[at, :]
         for k, (weight_ref, out_ref) in enumerate(
             zip(weight_refs, (q_ref, k_ref, v_ref), strict=True)
         ):
             out = jnp.dot(piece, weight_ref[...], preferred_element_type=jnp.float32)
             if k != 1:
                 out = out + bias_ref[k // 2 : k // 2 + 1, :]
-            out_ref[r * shard_len : (r + 1) * shard_len, :] = out.astype(jnp.bfloat16)
+            out_ref[at, :] = out.astype(jnp.bfloat16)
+        return carry
+
+    lax.fori_loop(0, count, project, 0)
     masked = key_mask(place_ref[0], length_ref[0], count, shard_len)
 
-    for i, mixed_ref in enumerate(mixed_refs):
-        at = slice(i * shard_len, (i + 1) * shard_len)
+
+    def block(i, carry):
+        at = pl.ds(pl.multiple_of(i * shard_len, shard_len), shard_len)
         queries = q_ref[at, :]
         mixed = []
         for h in range(width // HEAD):
@@ -138,7 +147,12 @@
             probs = (raised * (1.0 / total)).astype(jnp.bfloat16)
             mixed.append(jnp.dot(probs, v_ref[:, cols], preferred_element_type=jnp.float32))
             lse_ref[at, h : h + 1] = top + jnp.log(total)
-        mixed_ref[...] = jnp.concatenate(mixed, axis=1).astype(jnp.bfloat16)
+        mixed_all[at, :] = jnp.concatenate(mixed, axis=1).astype(jnp.bfloat16)
+        return carry
+
+    lax.fori_loop(0, count, block, 0)
+    for i, mixed_ref in enumerate(mixed_refs):
+        mixed_ref[...] = mixed_all[i * shard_len : (i + 1) * shard_len, :]
 
 
 def key_mask(place, length, count, shard_len):
@@ -162,6 +176,10 @@
         + (jax.ShapeDtypeStruct((shard_len, width), jnp.bfloat16),) * len(token_pieces),
         in_specs=[smem, smem] + [vmem] * len(arrays),
         out_specs=(vmem,) * (4 + len(token_pieces)),
+        scratch_shapes=[
+            pltpu.VMEM((rows, width), jnp.bfloat16),
+            pltpu.VMEM((rows, weights[0].shape[0]), jnp.bfloat16),
+        ],
         compiler_params=pltpu.CompilerParams(vmem_limit_bytes=40 << 20),
         cost_estimate=pl.CostEstimate(
             flops=2 * rows * width * (3 * weights[0].shape[0] + 8 * rows),
@@ -181,19 +199,26 @@
     lse_ref,
     *refs,
 ):
-    count = (len(refs) - 3 - 2 - 2) // 3
+    count = (len(refs) - 3 - 2 - 5) // 3
     mixed_refs, grad_refs = refs[:count], refs[count : 2 * count]
     weight_refs, refs = refs[2 * count : 2 * count + 3], refs[2 * count + 3 :]
     all_ref, sums_ref = refs[:2]
     part_refs = refs[2 : 2 + count]
-    dk_sum, dv_sum = refs[2 + count :]
+    dk_sum, dv_sum, mixed_all, grad_all, part_all = refs[2 + count :]
     shard_len = grad_refs[0].shape[0]
     _, width = q_ref.shape
     masked = key_mask(place_ref[0], length_ref[0], count, shard_len)
-    for i, (grad_ref, mixed_ref) in enumerate(zip(grad_refs, mixed_refs, strict=True)):
+    for i in range(count):
         at = slice(i * shard_len, (i + 1) * shard_len)
-        queries, grad = q_ref[at, :], grad_ref[...]
-        product = grad.astype(jnp.float32) * mixed_ref[...].astype(jnp.float32)
+        mixed_all[at, :] = mixed_refs[i][...]
+        grad_all[at, :] = grad_refs[i][...]
+    dk_sum[...] = jnp.zeros_like(dk_sum)
+    dv_sum[...] = jnp.zeros_like(dv_sum)
+
+    def block(i, carry):
+        at = pl.ds(pl.multiple_of(i * shard_len, shard_len), shard_len)
+        queries, grad = q_ref[at, :], grad_all[at, :]
+        product = grad.astype(jnp.float32) * mixed_all[at, :].astype(jnp.float32)
         parts = []
         for h in range(width // HEAD):
             cols = slice(h * HEAD, (h + 1) * HEAD)
@@ -207,25 +232,33 @@
                 jnp.dot(grad_scores, k_ref[:, cols], preferred_element_type=jnp.float32)
                 * SCORE_SCALE
             )
-            dk = jnp.dot(head_q.T, grad_scores, preferred_element_type=jnp.float32)
-            dv = jnp.dot(head_grad.T, probs.astype(jnp.bfloat16), preferred_element_type=jnp.float32)
-            if i == 0:
-                dk_sum[cols, :] = dk
-                dv_sum[cols, :] = dv
-            else:
-                dk_sum[cols, :] += dk
-                dv_sum[cols, :] += dv
+            dk_sum[cols, :] += jnp.dot(head_q.T, grad_scores, preferred_element_type=jnp.float32)
+            dv_sum[cols, :] += jnp.dot(
+                head_grad.T, probs.astype(jnp.bfloat16), preferred_element_type=jnp.float32
+            )
         all_ref[at, :width] = jnp.concatenate(parts, axis=1).astype(jnp.bfloat16)
+        return carry
+
+    lax.fori_loop(0, count, block, 0)
     all_ref[:, width : 2 * width] = (dk_sum[...].T * SCORE_SCALE).astype(jnp.bfloat16)
     all_ref[:, 2 * width :] = dv_sum[...].T.astype(jnp.bfloat16)
     sums_ref[...] = jnp.zeros_like(sums_ref)
     sums_ref[:1, :] = jnp.sum(all_ref[...].astype(jnp.float32), axis=0, keepdims=True)
-    for i, part_ref in enumerate(part_refs):
-        at = slice(i * shard_len, (i + 1) * shard_len)
+
+    def part_of(at):
         part = dot_right_t(all_ref[at, :width], weight_refs[0][...])
         part = part + dot_right_t(all_ref[at, width : 2 * width], weight_refs[1][...])
-        part = part + dot_right_t(all_ref[at, 2 * width :], weight_refs[2][...])
-        part_ref[...] = part.astype(part_ref.dtype)
+        return part + dot_right_t(all_ref[at, 2 * width :], weight_refs[2][...])
+
+    def other(i, carry):
+        at = pl.ds(pl.multiple_of(i * shard_len, shard_len), shard_len)
+        part_all[at, :] = part_of(at).astype(jnp.bfloat16)
+        return carry
+
+    part_refs[0][...] = part_of(slice(0, shard_len))
+    lax.fori_loop(1, count, other, 0)
+    for i in range(1, count):
+        part_refs[i][...] = part_all[i * shard_len : (i + 1) * shard_len, :]
 
 
 def attend_back(
@@ -247,7 +280,9 @@
         ),
         in_specs=[smem, smem] + [vmem] * len(arrays),
         out_specs=(vmem,) * (2 + len(parts)),
-        scratch_shapes=[pltpu.VMEM((width, rows), jnp.float32)] * 2,
+        scratch_shapes=[pltpu.VMEM((width, rows), jnp.float32)] * 2
+        + [pltpu.VMEM((rows, width), jnp.bfloat16)] * 2
+        + [pltpu.VMEM((rows, model_width), jnp.bfloat16)],
         compiler_params=pltpu.CompilerParams(vmem_limit_bytes=48 << 20),
         cost_estimate=pl.CostEstimate(
             flops=20 * rows * width * rows,
@@ -344,30 +379,31 @@
     token_pieces = gather_behind(token_rows)
     early_pieces = gather_behind(early_shard)
     qkv_all = lax.all_gather(qkv_shard, "fsdp", axis=0, tiled=False)
-    early_pieces = after(early_pieces, qkv_all)
-    early_cat = jnp.concatenate(
-        [piece[:, :hidden_shard] for piece in early_pieces[1:]]
-        + [piece[:, hidden_shard:] for piece in early_pieces[1:]],
-        axis=1,
-    )
-    early_all = lax.all_gather(early_cat, "fsdp", axis=0, tiled=True)
-    late_pieces = gather_behind(after(late_shard, early_pieces[1]))[1:]
-
-    def times(left, parts):
-        return jnp.concatenate(
-            [jnp.dot(left, part, preferred_element_type=f32) for part in parts], axis=1
-        )
-
-    def times_t(left, parts):
-        width = parts[0].shape[1]
-        return dot_right_t(left[:, :width], parts[0]) + dot_right_t(left[:, width:], parts[1])
-
     w_qkv = [
         qkv_all[:, i * row_shard : (i + 1) * row_shard].reshape(model_width, head_width)
         for i in range(3)
     ]
     vec_own = jnp.sum(qkv_all[:, 3 * row_shard :].astype(f32), axis=0)[:vec_rows]
-    vec_near = [piece.astype(f32) for piece in gather_behind(vec_own.astype(bf16))]
+    vec_half = vec_own.astype(bf16)
+    early_pieces = after(early_pieces, w_qkv, vec_half)
+    early_cat = jnp.concatenate(
+        [piece[:, :hidden_shard] for piece in early_pieces[1:]]
+        + [piece[:, hidden_shard:] for piece in early_pieces[1:]],
+        axis=1,
+    )
+    early_all = lax.all_gather(early_cat, "fsdp", axis=0, tiled=True)
+    late_pieces = gather_behind(after(late_shard, early_pieces[1]))[1:]
+
+    def times(left, parts):
+        return jnp.concatenate(
+            [jnp.dot(left, part, preferred_element_type=f32) for part in parts], axis=1
+        )
+
+    def times_t(left, parts):
+        width = parts[0].shape[1]
+        return dot_right_t(left[:, :width], parts[0]) + dot_right_t(left[:, width:], parts[1])
+
+    vec_near = [piece.astype(f32) for piece in gather_behind(vec_half)]
 
     def near(order):
         return sum(jnp.where(order == r, piece, 0.0) for r, piece in enumerate(vec_near))
@@ -379,10 +415,11 @@
 
     valid_len = lengths[0]
     queries, keys_all, values_all, lse, *mixed_pieces = attend(
-        place, valid_len, vec_own[:2], token_pieces, w_qkv
+        place, valid_len, vec_own[:2], after(token_pieces, vec_wide, up_bias), w_qkv
     )
     late_pieces = after(late_pieces, mixed_pieces)
-    late_all = lax.all_gather(jnp.concatenate(late_pieces, axis=1), "fsdp", axis=0, tiled=True)
+    late_cat = jnp.concatenate(late_pieces, axis=1)
+    late_all = lax.all_gather(late_cat, "fsdp", axis=0, tiled=True)
     up_parts = [own_all[:, :hidden_shard], early_all[:, : hidden_shard * (seq_count - 1)]]
     down_parts = [own_all[:, hidden_shard : 2 * hidden_shard], late_all]
     out_parts = [own_all[:, 2 * hidden_shard :], early_all[:, hidden_shard * (seq_count - 1) :]]
@@ -478,7 +515,7 @@
         w_qkv,
     )
     input_moved = swap_behind([input_own, *input_parts])
-    vec_part = sum(vec_moved)
+    vec_part = sum(after(vec_moved, input_own))
     vec_lines = jnp.concatenate(
         [head_sums[:1, :head_width], head_sums[:1, 2 * head_width :], vec_part[2:]], axis=0
     )
@@ -548,12 +585,15 @@
 
     token_total = shard_len * seq_count * fsdp_count
     grad_scale = float(token_total) ** (-0.5)
-    attn_grad = grad_scale * jnp.concatenate(
-        [
-            qkv_sum[:row_shard].reshape(row_shard, 3, head_width).transpose(1, 0, 2),
-            up_out_sum[None, :, hidden_shard:],
-        ],
-        axis=0,
+    attn_grad = grad_scale * with_layout_constraint(
+        jnp.stack(
+            [
+                qkv_sum[:row_shard, i * head_width : (i + 1) * head_width]
+                for i in range(3)
+            ]
+            + [up_out_sum[:, hidden_shard:]]
+        ),
+        Layout(major_to_minor=(0, 1, 2)),
     )
     ffn_grad = grad_scale * jnp.stack([up_out_sum[:, :hidden_shard], down_sum])
     vec_grad = grad_scale * lax.dynamic_slice(

time: 307 us -> 301 us (0.980)
  the two profiles are of different devices: /device:TPU:8 before, /device:TPU:0 now
where the time goes in v1:
time: 301 us
  waiting for transfers between devices  117 us (39%)
  starting transfers between devices  50.3 us (17%)
  local copies, waits for them, and re-layouts  30.2 us (10%)
  matrix products  26.7 us (9%)
  other arithmetic  23.7 us (8%)
  Pallas kernels  23 us (8%)
  between operations  15.8 us (5%)
  blocking collectives  13.8 us (5%)
    ppermute x30, waiting for transfers between devices, from_behind(): lax.ppermute(piece, 'seq', [(i, (i + distance) % count) for i in range(co...  97 us
    ppermute x30, starting transfers between devices, from_behind(): lax.ppermute(piece, 'seq', [(i, (i + distance) % count) for i in range(co...  44.5 us
    all_gather x1, blocking collectives, layer(): qkv_all = lax.all_gather(qkv_shard, 'fsdp', axis=0, tiled=False)  13.8 us
    pallas_call x1, Pallas kernels, attend_back(): pl.pallas_call(attend_back_kernel, out_shape=(jax.ShapeDtypeStruct((rows,...  12.2 us
    all_gather x1, waiting for transfers between devices, layer(): late_all = lax.all_gather(late_cat, 'fsdp', axis=0, tiled=True)  10.5 us
    pallas_call x1, Pallas kernels, attend(): pl.pallas_call(attend_kernel, out_shape=(half, half, half, jax.ShapeDtype...  10.1 us
    dot_general x6, matrix products, dot_right_t(): lax.dot_general(left, right, (((1,), (1,)), ((), ())), preferred_element_...  10 us
    unnamed x150, local copies, waits for them, and re-layouts  9.35 us
  transfers between devices with their start and end apart: 43, of which 12 were waited for; matrix products, arithmetic and copies ran while one was open for 18% of the time, Pallas kernels for 8%

profile of v1, /device:TPU:0, one launch (start us, length us, event | category | flops | bytes accessed | tf_op | source)
XLA Modules:
  0.0 300.5 jit_solution(9187676653368151122)
XLA Ops:
  10.8 5.1 %collective-permute-start.11 = (bf16[96,960]{1,0:T(8,128)(2,1)}, bf16[96,960]{1,0:T(8,128)(2,1)}, u32[]{:S(2)}, u32[]{:S(2)}) collective-permute-start(bf16[96,960]{1,0:T(8,128)(2,1)} %pad_maximum_fusion.6), channel_id=1, source_target_pairs={{0,24},{8,0},{16,8},{24,16},{1,25},{9,1},{17,9},{25,17},{2,26},{10... | collective-permute-start | bytes 552968 | tf_op jit(solution)/shard_map/ppermute | solution.py:55
  18.4 13.8 %all-gather.1 = bf16[8,304,192]{1,2,0:T(8,128)(2,1)S(1)} all-gather(bf16[1,304,192]{1,2,0:T(8,128)(2,1)S(1)} %copy.97), channel_id=2, replica_groups=mesh['seq'=4,'fsdp'=8] {'fsdp'}, dimensions={0}, use_global_device_ids=true | all-gather | bytes 1050624 | tf_op jit(solution)/shard_map/all_gather | solution.py:381
  49.3 3.7 %collective-permute-start.14 = (bf16[96,768]{1,0:T(8,128)(2,1)S(1)}, bf16[96,768]{1,0:T(8,128)(2,1)S(1)}, u32[]{:S(2)}, u32[]{:S(2)}) collective-permute-start(bf16[96,768]{1,0:T(8,128)(2,1)S(1)} %get-tuple-element.83), channel_id=1, source_target_pairs={{0,24},{8,0},{16,8},{24,16},{1,25},{9,1},{17,9},{25,17},{2,26},{10... | collective-permute-start | bytes 442376 | tf_op jit(solution)/shard_map/ppermute | solution.py:55
  53.1 4.9 %collective-permute-done.2.refs_3_ = bf16[256,768]{1,0:T(8,128)(2,1)S(1)} collective-permute-done((bf16[256,768]{1,0:T(8,128)(2,1)S(1)}, bf16[256,768]{1,0:T(8,128)(2,1)S(1)}, u32[]{:S(2)}, u32[]{:S(2)}) %collective-permute-start.2) | collective-permute-done | bytes 393248 | tf_op jit(solution)/shard_map/ppermute | solution.py:55
  58.6 30.4 %collective-permute-done.1.refs_2_ = bf16[256,768]{1,0:T(8,128)(2,1)S(1)} collective-permute-done((bf16[256,768]{1,0:T(8,128)(2,1)S(1)}, bf16[256,768]{1,0:T(8,128)(2,1)S(1)}, u32[]{:S(2)}, u32[]{:S(2)}) %collective-permute-start.1) | collective-permute-done | bytes 393248 | tf_op jit(solution)/shard_map/ppermute | solution.py:55
  89.0 10.1 %attend.1 = (bf16[1024,192]{1,0:T(8,128)(2,1)S(1)}, bf16[1024,192]{1,0:T(8,128)(2,1)S(1)}, bf16[1024,192]{1,0:T(8,128)(2,1)S(1)}, f32[1024,8]{1,0:T(8,128)S(1)},...) custom-call(s32[1]{0:T(128)} %bitcast.1.place_ref, ...), custom_call_target="tpu_custom_call" | custom-call | flops 4127195136 | bytes 8388608 | tf_op jit(solution)/shard_map/attend/pallas_call | solution.py:173
  105.7 2.9 collective-permute-start.8
  112.5 4.6 %collective-permute-done.7 = bf16[256,192]{1,0:T(8,128)(2,1)S(1)} collective-permute-done((bf16[256,192]{1,0:T(8,128)(2,1)S(1)}, bf16[256,192]{1,0:T(8,128)(2,1)S(1)}, u32[]{:S(2)}, u32[]{:S(2)}) %collective-permute-start.7) | collective-permute-done | bytes 98336 | tf_op jit(solution)/shard_map/ppermute | solution.py:55
  125.0 10.5 %all-gather.10.cloned.1.call-done = bf16[768,2304]{1,0:T(8,128)(2,1)} async-done(((bf16[96,2304]{1,0:T(8,128)(2,1)}), bf16[768,2304]{1,0:T(8,128)(2,1)}) %all-gather.10.cloned.1.call-update) | async-done | bytes 3538960 | tf_op jit(solution)/shard_map/all_gather | solution.py:422
  135.5 3.1 %fusion.26 = f32[256,768]{1,0:T(8,128)S(1)} fusion(bf16[768,2304]{1,0:T(8,128)(2,1)} %all-gather.10.cloned.1.call-done, bf16[256,3072]{1,0:T(8,128)(2,1)S(1)} %multiply_convert_fusion), kind=kOutput, calls=%fused_computation.46 | convolution fusion | flops 905969664 | bytes 5505024 | tf_op jit(solution)/shard_map/dot_general | solution.py:46
  142.3 3.6 %convolution_convert_fusion.1 = bf16[768,3072]{1,0:T(8,128)(2,1)} fusion(bf16[256,768]{1,0:T(8,128)(2,1)S(1)} %get-tuple-element.87, bf16[256,3072]{1,0:T(8,128)(2,1)S(1)} %copy-done.38), kind=kOutput, calls=%fused_computation.1 | convolution fusion | flops 1210318848 | bytes 6684672 | tf_op jit(solution)/shard_map/dot_general | solution.py:442
  146.0 3.2 %fusion.109 = f32[256,2304]{1,0:T(8,128)S(1)} fusion(bf16[256,768]{1,0:T(8,128)(2,1)S(1)} %get-tuple-element.87, bf16[768,2304]{1,0:T(8,128)(2,1)} %all-gather.10.cloned.1.call-done), kind=kOutput, calls=%fused_computation.232 | convolution fusion | flops 905969664 | bytes 6291456 | tf_op jit(solution)/shard_map/dot_general | solution.py:399
  158.7 3.4 %collective-permute-start.27 = (f32[16,192]{1,0:T(8,128)S(1)}, f32[16,192]{1,0:T(8,128)S(1)}, u32[]{:S(2)}, u32[]{:S(2)}) collective-permute-start(f32[16,192]{1,0:T(8,128)S(1)} %get-tuple-element.189), channel_id=1, source_target_pairs={{0,24},{8,0},{16,8},{24,16},{1,25},{9,1},{17,9},{25,17},{2,26},{10... | collective-permute-start | bytes 36872 | tf_op jit(solution)/shard_map/ppermute | solution.py:55
  164.9 2.9 collective-permute-start.16
  173.7 5.6 %collective-permute-done.16.refs_6_ = bf16[256,192]{1,0:T(8,128)(2,1)S(1)} collective-permute-done((bf16[256,192]{1,0:T(8,128)(2,1)S(1)}, bf16[256,192]{1,0:T(8,128)(2,1)S(1)}, u32[]{:S(2)}, u32[]{:S(2)}) %collective-permute-start.16) | collective-permute-done | bytes 98336 | tf_op jit(solution)/shard_map/ppermute | solution.py:55
  181.2 12.2 %attend_back.1 = (bf16[1024,576]{1,0:T(8,128)(2,1)}, f32[16,576]{1,0:T(8,128)S(1)}, f32[256,768]{1,0:T(8,128)}, bf16[256,768]{1,0:T(8,128)(2,1)S(1)}, bf16[256,7...) custom-call(s32[1]{0:T(128)} %bitcast.1.place_ref, s32[1]{0:T(128)S(6)} %copy.119.length_ref, ...), custom_call_target="tpu_custom_call" | custom-call | flops 4026531840 | bytes 8388608 | tf_op jit(solution)/shard_map/attend_back/pallas_call | solution.py:274
  193.3 3.4 %fusion.18 = bf16[768,576]{0,1:T(8,128)(2,1)} fusion(bf16[1024,576]{1,0:T(8,128)(2,1)} %get-tuple-element.108, bf16[256,768]{1,0:T(8,128)(2,1)S(1)} %copy-done.12, bf16[256,768]{1,0:T(8,128)(2,1)S(1)} %copy-done.14, bf16[256,768]{1,0:T(8,128)(2,1)S(1)} %copy-done.16, bf16[256,768]{1,0:T(8,128)(2,1)S(1)} %bitcast.130), kind=kOutput, calls=%fused_computation.36 | convolution fusion | flops 912703488 | bytes 3637248 | tf_op jit(solution)/shard_map/dot_general | solution.py:524
  210.4 3.0 collective-permute-start.30
  214.9 3.0 collective-permute-done.34
  221.3 5.1 %collective-permute-done.32 = bf16[2,112,576]{2,1,0:T(8,128)(2,1)S(1)} collective-permute-done((bf16[2,112,576]{2,1,0:T(8,128)(2,1)S(1)}, bf16[2,112,576]{2,1,0:T(8,128)(2,1)S(1)}, u32[]{:S(2)}, u32[]{:S(2)}) %collective-permute-start.32) | collective-permute-done | bytes 258080 | tf_op jit(solution)/shard_map/ppermute | solution.py:102
  234.7 39.6 %collective-permute-done.29 = bf16[96,768]{1,0:T(8,128)(2,1)S(1)} collective-permute-done((bf16[96,768]{1,0:T(8,128)(2,1)}, bf16[96,768]{1,0:T(8,128)(2,1)S(1)}, u32[]{:S(2)}, u32[]{:S(2)}) %collective-permute-start.29) | collective-permute-done | bytes 147488 | tf_op jit(solution)/shard_map/ppermute | solution.py:55
  275.5 3.9 %collective-permute-start.38 = (bf16[96,960]{1,0:T(8,128)(2,1)S(1)}, bf16[96,960]{1,0:T(8,128)(2,1)S(1)}, u32[]{:S(2)}, u32[]{:S(2)}) collective-permute-start(bf16[96,960]{1,0:T(8,128)(2,1)S(1)} %pad_maximum_fusion.7), channel_id=1, source_target_pairs={{0,24},{8,0},{16,8},{24,16},{1,25},{9,1},{17,9},{25,17},{2,26},{10... | collective-permute-start | bytes 552968 | tf_op jit(solution)/shard_map/ppermute | solution.py:55
  280.5 6.1 %collective-permute-done.37 = bf16[96,960]{1,0:T(8,128)(2,1)S(1)} collective-permute-done((bf16[96,960]{1,0:T(8,128)(2,1)}, bf16[96,960]{1,0:T(8,128)(2,1)S(1)}, u32[]{:S(2)}, u32[]{:S(2)}) %collective-permute-start.37) | collective-permute-done | bytes 184352 | tf_op jit(solution)/shard_map/ppermute | solution.py:55
  286.7 3.2 %collective-permute-done.38 = bf16[96,960]{1,0:T(8,128)(2,1)S(1)} collective-permute-done((bf16[96,960]{1,0:T(8,128)(2,1)S(1)}, bf16[96,960]{1,0:T(8,128)(2,1)S(1)}, u32[]{:S(2)}, u32[]{:S(2)}) %collective-permute-start.38) | collective-permute-done | bytes 184352 | tf_op jit(solution)/shard_map/ppermute | solution.py:55
  (339 shorter events, 97.4 us)
Async XLA Ops:
  7.2 101.5 %all-gather.6.cloned.1.call-start = ((), (), s32[]{:S(2)}) async-start(), calls=%async_computation.1 | async-start | bytes 3096576 | tf_op jit(solution)/shard_map/all_gather | solution.py:378
  10.0 107.1 %all-gather.8.cloned.1.call-start = ((), (), s32[]{:S(2)}) async-start(), calls=%async_computation.2 | async-start | bytes 5087232 | tf_op jit(solution)/shard_map/all_gather | solution.py:394
  10.8 22.7 %collective-permute-start.11 = (bf16[96,960]{1,0:T(8,128)(2,1)}, bf16[96,960]{1,0:T(8,128)(2,1)}, u32[]{:S(2)}, u32[]{:S(2)}) collective-permute-start(bf16[96,960]{1,0:T(8,128)(2,1)} %pad_maximum_fusion.6), channel_id=1, source_target_pairs={{0,24},{8,0},{16,8},{24,16},{1,25},{9,1},{17,9},{25,17},{2,26},{10... | collective-permute-start | bytes 552968 | tf_op jit(solution)/shard_map/ppermute | solution.py:55
  15.8 17.6 %collective-permute-start.10 = (bf16[96,960]{1,0:T(8,128)(2,1)}, bf16[96,960]{1,0:T(8,128)(2,1)}, u32[]{:S(2)}, u32[]{:S(2)}) collective-permute-start(bf16[96,960]{1,0:T(8,128)(2,1)} %pad_maximum_fusion.6), channel_id=1, source_target_pairs={{0,16},{8,24},{16,0},{24,8},{1,17},{9,25},{17,1},{25,9},{2,18},{10... | collective-permute-start | bytes 552968 | tf_op jit(solution)/shard_map/ppermute | solution.py:55
  15.8 17.7 %collective-permute-start.9 = (bf16[96,960]{1,0:T(8,128)(2,1)}, bf16[96,960]{1,0:T(8,128)(2,1)}, u32[]{:S(2)}, u32[]{:S(2)}) collective-permute-start(bf16[96,960]{1,0:T(8,128)(2,1)} %pad_maximum_fusion.6), channel_id=1, source_target_pairs={{0,8},{8,16},{16,24},{24,0},{1,9},{9,17},{17,25},{25,1},{2,10},{10... | collective-permute-start | bytes 552968 | tf_op jit(solution)/shard_map/ppermute | solution.py:55
  39.8 95.7 %all-gather.10.cloned.1.call-start = ((), (), s32[]{:S(2)}) async-start(), calls=%async_computation.3 | async-start | bytes 3981312 | tf_op jit(solution)/shard_map/all_gather | solution.py:422
  46.8 42.2 %collective-permute-start.1 = (bf16[256,768]{1,0:T(8,128)(2,1)S(1)}, bf16[256,768]{1,0:T(8,128)(2,1)S(1)}, u32[]{:S(2)}, u32[]{:S(2)}) collective-permute-start(bf16[256,768]{1,0:T(8,128)(2,1)S(1)} %bitcast.127), channel_id=1, source_target_pairs={{0,16},{8,24},{16,0},{24,8},{1,17},{9,25},{17,1},{25,9},{2,18},{10... | collective-permute-start | bytes 1179656 | tf_op jit(solution)/shard_map/ppermute | solution.py:55
  47.8 41.2 %collective-permute-start = (bf16[256,768]{1,0:T(8,128)(2,1)S(1)}, bf16[256,768]{1,0:T(8,128)(2,1)S(1)}, u32[]{:S(2)}, u32[]{:S(2)}) collective-permute-start(bf16[256,768]{1,0:T(8,128)(2,1)S(1)} %bitcast.128), channel_id=1, source_target_pairs={{0,8},{8,16},{16,24},{24,0},{1,9},{9,17},{17,25},{25,1},{2,10},{10... | collective-permute-start | bytes 1179656 | tf_op jit(solution)/shard_map/ppermute | solution.py:55
  49.3 53.1 %collective-permute-start.14 = (bf16[96,768]{1,0:T(8,128)(2,1)S(1)}, bf16[96,768]{1,0:T(8,128)(2,1)S(1)}, u32[]{:S(2)}, u32[]{:S(2)}) collective-permute-start(bf16[96,768]{1,0:T(8,128)(2,1)S(1)} %get-tuple-element.83), channel_id=1, source_target_pairs={{0,24},{8,0},{16,8},{24,16},{1,25},{9,1},{17,9},{25,17},{2,26},{10... | collective-permute-start | bytes 442376 | tf_op jit(solution)/shard_map/ppermute | solution.py:55
  52.9 49.5 %collective-permute-start.13 = (bf16[96,768]{1,0:T(8,128)(2,1)S(1)}, bf16[96,768]{1,0:T(8,128)(2,1)S(1)}, u32[]{:S(2)}, u32[]{:S(2)}) collective-permute-start(bf16[96,768]{1,0:T(8,128)(2,1)S(1)} %get-tuple-element.83), channel_id=1, source_target_pairs={{0,16},{8,24},{16,0},{24,8},{1,17},{9,25},{17,1},{25,9},{2,18},{10... | collective-permute-start | bytes 442376 | tf_op jit(solution)/shard_map/ppermute | solution.py:55
  58.0 44.4 %collective-permute-start.12 = (bf16[96,768]{1,0:T(8,128)(2,1)S(1)}, bf16[96,768]{1,0:T(8,128)(2,1)S(1)}, u32[]{:S(2)}, u32[]{:S(2)}) collective-permute-start(bf16[96,768]{1,0:T(8,128)(2,1)S(1)} %get-tuple-element.83), channel_id=1, source_target_pairs={{0,8},{8,16},{16,24},{24,0},{1,9},{9,17},{17,25},{25,1},{2,10},{10... | collective-permute-start | bytes 442376 | tf_op jit(solution)/shard_map/ppermute | solution.py:55
  103.3 105.1 %reduce-scatter.2.cloned.1.call-start = ((), (), s32[]{:S(2)}) async-start(), calls=%async_computation.4 | async-start | bytes 5308416 | tf_op jit(solution)/shard_map/reduce_scatter | solution.py:458
  158.7 38.1 %collective-permute-start.27 = (f32[16,192]{1,0:T(8,128)S(1)}, f32[16,192]{1,0:T(8,128)S(1)}, u32[]{:S(2)}, u32[]{:S(2)}) collective-permute-start(f32[16,192]{1,0:T(8,128)S(1)} %get-tuple-element.189), channel_id=1, source_target_pairs={{0,24},{8,0},{16,8},{24,16},{1,25},{9,1},{17,9},{25,17},{2,26},{10... | collective-permute-start | bytes 36872 | tf_op jit(solution)/shard_map/ppermute | solution.py:55
  162.0 34.7 %collective-permute-start.26 = (f32[16,192]{1,0:T(8,128)S(1)}, f32[16,192]{1,0:T(8,128)S(1)}, u32[]{:S(2)}, u32[]{:S(2)}) collective-permute-start(f32[16,192]{1,0:T(8,128)S(1)} %get-tuple-element.190), channel_id=1, source_target_pairs={{0,16},{8,24},{16,0},{24,8},{1,17},{9,25},{17,1},{25,9},{2,18},{10... | collective-permute-start | bytes 36872 | tf_op jit(solution)/shard_map/ppermute | solution.py:55
  164.9 14.5 %collective-permute-start.16 = (bf16[256,192]{1,0:T(8,128)(2,1)S(1)}, bf16[256,192]{1,0:T(8,128)(2,1)S(1)}, u32[]{:S(2)}, u32[]{:S(2)}) collective-permute-start(bf16[256,192]{1,0:T(8,128)(2,1)S(1)} %get-tuple-element.181), channel_id=1, source_target_pairs={{0,16},{8,24},{16,0},{24,8},{1,17},{9,25},{17,1},{25,9},{2,18},{10... | collective-permute-start | bytes 294920 | tf_op jit(solution)/shard_map/ppermute | solution.py:55
  173.7 23.1 %collective-permute-start.25 = (f32[16,192]{1,0:T(8,128)S(1)}, f32[16,192]{1,0:T(8,128)S(1)}, u32[]{:S(2)}, u32[]{:S(2)}) collective-permute-start(f32[16,192]{1,0:T(8,128)S(1)} %get-tuple-element.191), channel_id=1, source_target_pairs={{0,8},{8,16},{16,24},{24,0},{1,9},{9,17},{17,25},{25,1},{2,10},{10... | collective-permute-start | bytes 36872 | tf_op jit(solution)/shard_map/ppermute | solution.py:55
  179.4 25.2 %collective-permute-start.23 = (bf16[2,96,1920]{2,1,0:T(8,128)(2,1)}, bf16[2,96,1920]{2,1,0:T(8,128)(2,1)}, u32[]{:S(2)}, u32[]{:S(2)}) collective-permute-start(bf16[2,96,1920]{2,1,0:T(8,128)(2,1)} %fusion.38), channel_id=1, source_target_pairs={{0,4},{1,5},{2,6},{3,7},{4,0},{5,1},{6,2},{7,3},{8,12},{9,13},{10,... | collective-permute-start | bytes 2211848 | tf_op jit(solution)/shard_map/ppermute | solution.py:102
  180.6 20.0 %collective-permute-start.24 = (bf16[2,96,1920]{2,1,0:T(8,128)(2,1)}, bf16[2,96,1920]{2,1,0:T(8,128)(2,1)}, u32[]{:S(2)}, u32[]{:S(2)}) collective-permute-start(bf16[2,96,1920]{2,1,0:T(8,128)(2,1)} %fusion.39), channel_id=1, source_target_pairs={{0,2},{1,3},{2,0},{3,1},{4,6},{5,7},{6,4},{7,5},{8,10},{9,11},{10,... | collective-permute-start | bytes 2211848 | tf_op jit(solution)/shard_map/ppermute | solution.py:102
  210.4 21.5 %collective-permute-start.30 = (bf16[96,768]{1,0:T(8,128)(2,1)}, bf16[96,768]{1,0:T(8,128)(2,1)}, u32[]{:S(2)}, u32[]{:S(2)}) collective-permute-start(bf16[96,768]{1,0:T(8,128)(2,1)} %get-tuple-element.171), channel_id=1, source_target_pairs={{0,24},{8,0},{16,8},{24,16},{1,25},{9,1},{17,9},{25,17},{2,26},{10... | collective-permute-start | bytes 442376 | tf_op jit(solution)/shard_map/ppermute | solution.py:55
  227.8 47.7 %collective-permute-start.20 = (bf16[256,768]{1,0:T(8,128)(2,1)S(1)}, bf16[256,768]{1,0:T(8,128)(2,1)S(1)}, u32[]{:S(2)}, u32[]{:S(2)}) collective-permute-start(bf16[256,768]{1,0:T(8,128)(2,1)S(1)} %get-tuple-element.104), channel_id=1, source_target_pairs={{0,8},{8,16},{16,24},{24,0},{1,9},{9,17},{17,25},{25,1},{2,10},{10... | collective-permute-start | bytes 1179656 | tf_op jit(solution)/shard_map/ppermute | solution.py:55
  228.1 51.3 %collective-permute-start.21 = (bf16[256,768]{1,0:T(8,128)(2,1)S(1)}, bf16[256,768]{1,0:T(8,128)(2,1)S(1)}, u32[]{:S(2)}, u32[]{:S(2)}) collective-permute-start(bf16[256,768]{1,0:T(8,128)(2,1)S(1)} %get-tuple-element.105), channel_id=1, source_target_pairs={{0,16},{8,24},{16,0},{24,8},{1,17},{9,25},{17,1},{25,9},{2,18},{10... | collective-permute-start | bytes 1179656 | tf_op jit(solution)/shard_map/ppermute | solution.py:55
  230.1 49.3 %collective-permute-start.22 = (bf16[256,768]{1,0:T(8,128)(2,1)S(1)}, bf16[256,768]{1,0:T(8,128)(2,1)S(1)}, u32[]{:S(2)}, u32[]{:S(2)}) collective-permute-start(bf16[256,768]{1,0:T(8,128)(2,1)S(1)} %get-tuple-element.106), channel_id=1, source_target_pairs={{0,24},{8,0},{16,8},{24,16},{1,25},{9,1},{17,9},{25,17},{2,26},{10... | collective-permute-start | bytes 1179656 | tf_op jit(solution)/shard_map/ppermute | solution.py:55
  231.9 42.5 %collective-permute-start.29 = (bf16[96,768]{1,0:T(8,128)(2,1)}, bf16[96,768]{1,0:T(8,128)(2,1)S(1)}, u32[]{:S(2)}, u32[]{:S(2)}) collective-permute-start(bf16[96,768]{1,0:T(8,128)(2,1)} %get-tuple-element.172), channel_id=1, source_target_pairs={{0,16},{8,24},{16,0},{24,8},{1,17},{9,25},{17,1},{25,9},{2,18},{10... | collective-permute-start | bytes 442376 | tf_op jit(solution)/shard_map/ppermute | solution.py:55
  233.8 40.6 %collective-permute-start.28 = (bf16[96,768]{1,0:T(8,128)(2,1)}, bf16[96,768]{1,0:T(8,128)(2,1)S(1)}, u32[]{:S(2)}, u32[]{:S(2)}) collective-permute-start(bf16[96,768]{1,0:T(8,128)(2,1)} %get-tuple-element.173), channel_id=1, source_target_pairs={{0,8},{8,16},{16,24},{24,0},{1,9},{9,17},{17,25},{25,1},{2,10},{10... | collective-permute-start | bytes 442376 | tf_op jit(solution)/shard_map/ppermute | solution.py:55
  (93 other events, 968.8 us)
Sparse Core Ops, SparseCore 0:
  10.5 35.5 all-gather.5
  48.5 37.9 all-gather.7
  103.5 31.9 all-gather.9
  146.1 60.7 reduce-scatter.1

commit v2 on v1

--- a/solution.py
+++ b/solution.py
@@ -367,8 +367,6 @@
     bits = list(range(fsdp_count.bit_length() - 1))
 
     own_shard = jnp.concatenate([w_ffn[0], w_ffn[1], w_attn[3]], axis=1).astype(bf16)
-    early_shard = jnp.concatenate([w_ffn[0], w_attn[3]], axis=1).astype(bf16)
-    late_shard = w_ffn[1].astype(bf16)
     vec_placed = lax.dynamic_update_slice(
         jnp.zeros((16, head_width), bf16), vectors.astype(bf16), (0, member * vec_shard)
     )
@@ -376,8 +374,8 @@
         [w_attn[:3].astype(bf16).reshape(3 * row_shard, head_width), vec_placed], axis=0
     )
     own_all = lax.all_gather(own_shard, "fsdp", axis=0, tiled=True)
+    weight_pieces = gather_behind(own_shard)[1:]
     token_pieces = gather_behind(token_rows)
-    early_pieces = gather_behind(early_shard)
     qkv_all = lax.all_gather(qkv_shard, "fsdp", axis=0, tiled=False)
     w_qkv = [
         qkv_all[:, i * row_shard : (i + 1) * row_shard].reshape(model_width, head_width)
@@ -385,14 +383,21 @@
     ]
     vec_own = jnp.sum(qkv_all[:, 3 * row_shard :].astype(f32), axis=0)[:vec_rows]
     vec_half = vec_own.astype(bf16)
-    early_pieces = after(early_pieces, w_qkv, vec_half)
-    early_cat = jnp.concatenate(
-        [piece[:, :hidden_shard] for piece in early_pieces[1:]]
-        + [piece[:, hidden_shard:] for piece in early_pieces[1:]],
+    weight_pieces = after(weight_pieces, w_qkv, vec_half)
+    cuts = (0, hidden_shard, 2 * hidden_shard, 2 * hidden_shard + head_width)
+    rest_cat = jnp.concatenate(
+        [
+            piece[:, low:high]
+            for low, high in zip(cuts[:-1], cuts[1:], strict=True)
+            for piece in weight_pieces
+        ],
         axis=1,
     )
-    early_all = lax.all_gather(early_cat, "fsdp", axis=0, tiled=True)
-    late_pieces = gather_behind(after(late_shard, early_pieces[1]))[1:]
+    rest_all = lax.all_gather(rest_cat, "fsdp", axis=0, tiled=True)
+    up_parts, down_parts, out_parts = (
+        [own_all[:, low:high], rest_all[:, low * (seq_count - 1) : high * (seq_count - 1)]]
+        for low, high in zip(cuts[:-1], cuts[1:], strict=True)
+    )
 
     def times(left, parts):
         return jnp.concatenate(
@@ -417,12 +422,6 @@
     queries, keys_all, values_all, lse, *mixed_pieces = attend(
         place, valid_len, vec_own[:2], after(token_pieces, vec_wide, up_bias), w_qkv
     )
-    late_pieces = after(late_pieces, mixed_pieces)
-    late_cat = jnp.concatenate(late_pieces, axis=1)
-    late_all = lax.all_gather(late_cat, "fsdp", axis=0, tiled=True)
-    up_parts = [own_all[:, :hidden_shard], early_all[:, : hidden_shard * (seq_count - 1)]]
-    down_parts = [own_all[:, hidden_shard : 2 * hidden_shard], late_all]
-    out_parts = [own_all[:, 2 * hidden_shard :], early_all[:, hidden_shard * (seq_count - 1) :]]
     mixed_rows = jnp.concatenate(swap_behind(mixed_pieces), axis=1)
 
     hidden_one = token_rows.astype(f32) + times_t(mixed_rows, out_parts) + vec_wide[2]
@@ -566,22 +565,21 @@
             down_pieces = jnp.split(after(down_part, step), seq_count, axis=1)
             down_moved = swap_behind(down_pieces)
             step = down_pieces
-        if at < len(bits) - 1:
-            qkv_half = joined(qkv_kept, after(qkv_received, step))
-            qkv_kept, qkv_sent = halving(qkv_half, bits[at], True)
-            qkv_received = swapped(qkv_sent, bits[at])
-            step = qkv_sent
     wide_pieces = place_pieces(wide_moving[0], near_places) + place_pieces(
         wide_moving[1], seq_count - near_places
     )
     wide_sent = halves_of(wide_pieces[1:])
     wide_moved = swap_behind([wide_pieces[0]] + wide_sent)
-    qkv_half = joined(qkv_kept, after(qkv_received, wide_sent))
-    qkv_kept, qkv_sent = halving(qkv_half, bits[-1], True)
-    qkv_sum = joined(qkv_kept, swapped(qkv_sent, bits[-1]))[0]
-    down_sum = total_of([down_moved[0]] + after(down_moved[1:], qkv_sum))
-    input_grad = grad_one + total_of([input_moved[0]] + after(input_moved[1:], down_sum))
-    up_out_sum = total_of([wide_moved[0]] + after(wide_moved[1:], input_grad))
+    step = wide_sent
+    for bit in bits[1:]:
+        qkv_half = joined(qkv_kept, after(qkv_received, step))
+        qkv_kept, qkv_sent = halving(qkv_half, bit, True)
+        qkv_received = swapped(qkv_sent, bit)
+        step = qkv_sent
+    qkv_sum = joined(qkv_kept, qkv_received)[0]
+    input_grad = grad_one + total_of([input_moved[0]] + after(input_moved[1:], qkv_sum))
+    down_sum = total_of([down_moved[0]] + after(down_moved[1:], input_grad))
+    up_out_sum = total_of([wide_moved[0]] + after(wide_moved[1:], down_sum))
 
     token_total = shard_len * seq_count * fsdp_count
     grad_scale = float(token_total) ** (-0.5)

time: 301 us -> 286 us (0.950)
  waiting for transfers between devices: 117 us -> 81.7 us
  starting transfers between devices: 50.3 us -> 67.6 us
  other arithmetic: 23.7 us -> 28.1 us
  local copies, waits for them, and re-layouts: 30.2 us -> 27.1 us
    ppermute x30 -> x27, waiting for transfers between devices: 97 us -> 74.6 us  [from_behind(): lax.ppermute(piece, 'seq', [(i, (i + distance) % count) for i in range(co...]
    ppermute x30 -> x27, starting transfers between devices: 44.5 us -> 58.6 us  [from_behind(): lax.ppermute(piece, 'seq', [(i, (i + distance) % count) for i in range(co...]
    all_gather x2 -> x1, waiting for transfers between devices: 10.5 us -> 0.02 us  [layer(): rest_all = lax.all_gather(rest_cat, 'fsdp', axis=0, tiled=True)]
    another operation x4 -> x6, other arithmetic: 1.16 us -> 5.24 us
    slice x6 -> x5, local copies, waits for them, and re-layouts: 5.29 us -> 1.86 us  [layer(): piece[:, low:high]]
    ppermute x9, starting transfers between devices: 5.63 us -> 8.93 us  [swapped(): return lax.ppermute(sent, 'fsdp', pairs)]
    unnamed x150 -> x138, local copies, waits for them, and re-layouts: 9.35 us -> 10.5 us
  transfers between devices with their start and end apart: 43 -> 39, of which waited for: 12 -> 13; matrix products, arithmetic and copies ran while one was open for 18% -> 17% of each run, Pallas kernels for 8% -> 8%
where the time goes in v2:
time: 286 us
  waiting for transfers between devices  81.7 us (29%)
  starting transfers between devices  67.6 us (24%)
  other arithmetic  28.1 us (10%)
  matrix products  27.5 us (10%)
  local copies, waits for them, and re-layouts  27.1 us (9%)
  Pallas kernels  23 us (8%)
  between operations  15.8 us (6%)
  blocking collectives  14.7 us (5%)
    ppermute x27, waiting for transfers between devices, from_behind(): lax.ppermute(piece, 'seq', [(i, (i + distance) % count) for i in range(co...  74.6 us
    ppermute x27, starting transfers between devices, from_behind(): lax.ppermute(piece, 'seq', [(i, (i + distance) % count) for i in range(co...  58.6 us
    all_gather x1, blocking collectives, layer(): qkv_all = lax.all_gather(qkv_shard, 'fsdp', axis=0, tiled=False)  14.7 us
    pallas_call x1, Pallas kernels, attend_back(): pl.pallas_call(attend_back_kernel, out_shape=(jax.ShapeDtypeStruct((rows,...  12.2 us
    unnamed x138, local copies, waits for them, and re-layouts  10.5 us
    pallas_call x1, Pallas kernels, attend(): pl.pallas_call(attend_kernel, out_shape=(half, half, half, jax.ShapeDtype...  10.1 us
    dot_general x6, matrix products, times(): jnp.dot(left, part, preferred_element_type=f32)  9.55 us
    ppermute x9, starting transfers between devices, swapped(): return lax.ppermute(sent, 'fsdp', pairs)  8.93 us
  transfers between devices with their start and end apart: 39, of which 13 were waited for; matrix products, arithmetic and copies ran while one was open for 17% of the time, Pallas kernels for 8%

profile of v2, /device:TPU:0, one launch (start us, length us, event | category | flops | bytes accessed | tf_op | source)
XLA Modules:
  0.0 285.5 jit_solution(2696186113898914768)
XLA Ops:
  10.2 5.1 %collective-permute-start.11 = (bf16[96,1728]{1,0:T(8,128)(2,1)}, bf16[96,1728]{1,0:T(8,128)(2,1)S(1)}, u32[]{:S(2)}, u32[]{:S(2)}) collective-permute-start(bf16[96,1728]{1,0:T(8,128)(2,1)} %pad_maximum_fusion.4), channel_id=1, source_target_pairs={{0,24},{8,0},{16,8},{24,16},{1,25},{9,1},{17,9},{25,17},{2,26},{10... | collective-permute-start | bytes 995336 | tf_op jit(solution)/shard_map/ppermute | solution.py:55
  17.0 14.7 %all-gather.1 = bf16[8,304,192]{1,2,0:T(8,128)(2,1)S(1)} all-gather(bf16[1,304,192]{1,2,0:T(8,128)(2,1)S(1)} %copy.97), channel_id=2, replica_groups=mesh['seq'=4,'fsdp'=8] {'fsdp'}, dimensions={0}, use_global_device_ids=true | all-gather | bytes 1050624 | tf_op jit(solution)/shard_map/all_gather | solution.py:379
  32.9 12.1 %collective-permute-done.10 = bf16[96,1728]{1,0:T(8,128)(2,1)} collective-permute-done((bf16[96,1728]{1,0:T(8,128)(2,1)}, bf16[96,1728]{1,0:T(8,128)(2,1)}, u32[]{:S(2)}, u32[]{:S(2)}) %collective-permute-start.10) | collective-permute-done | bytes 331808 | tf_op jit(solution)/shard_map/ppermute | solution.py:55
  48.2 2.8 collective-permute-start.1
  56.1 24.0 %collective-permute-done.4 = bf16[12,192]{0,1:T(8,128)(2,1)S(1)} collective-permute-done((bf16[12,192]{0,1:T(8,128)(2,1)S(1)}, bf16[12,192]{0,1:T(8,128)(2,1)S(1)}, u32[]{:S(2)}, u32[]{:S(2)}) %collective-permute-start.4) | collective-permute-done | bytes 4640 | tf_op jit(solution)/shard_map/ppermute | solution.py:55
  81.4 9.7 %collective-permute-done.refs_1_ = bf16[256,768]{1,0:T(8,128)(2,1)S(1)} collective-permute-done((bf16[256,768]{1,0:T(8,128)(2,1)S(1)}, bf16[256,768]{1,0:T(8,128)(2,1)S(1)}, u32[]{:S(2)}, u32[]{:S(2)}) %collective-permute-start) | collective-permute-done | bytes 393248 | tf_op jit(solution)/shard_map/ppermute | solution.py:55
  91.2 10.1 %attend.1 = (bf16[1024,192]{1,0:T(8,128)(2,1)S(1)}, bf16[1024,192]{1,0:T(8,128)(2,1)S(1)}, bf16[1024,192]{1,0:T(8,128)(2,1)S(1)}, f32[1024,8]{1,0:T(8,128)S(1)},...) custom-call(s32[1]{0:T(128)} %bitcast.1.place_ref, ...), custom_call_target="tpu_custom_call" | custom-call | flops 4127195136 | bytes 8388608 | tf_op jit(solution)/shard_map/attend/pallas_call | solution.py:173
  105.3 3.1 %collective-permute-start.8 = (bf16[256,192]{1,0:T(8,128)(2,1)S(1)}, bf16[256,192]{1,0:T(8,128)(2,1)S(1)}, u32[]{:S(2)}, u32[]{:S(2)}) collective-permute-start(bf16[256,192]{1,0:T(8,128)(2,1)S(1)} %get-tuple-element.75.refs_1_), channel_id=1, source_target_pairs={{0,24},{8,0},{16,8},{24,16},{1,25},{9,1},{17,9},{25,17},{2,26},{10... | collective-permute-start | bytes 294920 | tf_op jit(solution)/shard_map/ppermute | solution.py:55
  109.7 2.4 collective-permute-done.6
  112.2 2.8 collective-permute-done.7
  118.0 3.1 %fusion.12 = f32[256,2304]{1,0:T(8,128)S(1)} fusion(bf16[256,768]{1,0:T(8,128)(2,1)S(1)} %get-tuple-element.151, bf16[768,5184]{1,0:T(8,128)(2,1)} %all-gather.7.cloned.1.call-done), kind=kOutput, calls=%fused_computation.19 | convolution fusion | flops 905969664 | bytes 6291456 | tf_op jit(solution)/shard_map/dot_general | solution.py:404
  123.2 3.1 %fusion.8 = f32[256,768]{1,0:T(8,128)S(1)} fusion(bf16[768,5184]{1,0:T(8,128)(2,1)} %all-gather.7.cloned.1.call-done, bf16[256,3072]{1,0:T(8,128)(2,1)S(1)} %multiply_convert_fusion), kind=kOutput, calls=%fused_computation.15 | convolution fusion | flops 905969664 | bytes 5505024 | tf_op jit(solution)/shard_map/dot_general | solution.py:46
  130.1 3.7 %convolution_convert_fusion.1 = bf16[768,3072]{1,0:T(8,128)(2,1)} fusion(bf16[256,768]{1,0:T(8,128)(2,1)S(1)} %get-tuple-element.79, bf16[256,3072]{1,0:T(8,128)(2,1)S(1)} %multiply_convert_fusion), kind=kOutput, calls=%fused_computation.1 | convolution fusion | flops 1210318848 | bytes 6684672 | tf_op jit(solution)/shard_map/dot_general | solution.py:441
  135.7 3.4 %fusion.6 = f32[256,2304]{1,0:T(8,128)S(1)} fusion(bf16[256,768]{1,0:T(8,128)(2,1)} %copy-done.43, bf16[768,5184]{1,0:T(8,128)(2,1)} %all-gather.7.cloned.1.call-done), kind=kOutput, calls=%fused_computation.13 | convolution fusion | flops 905969664 | bytes 6291456 | tf_op jit(solution)/shard_map/dot_general | solution.py:404
  164.3 3.9 %collective-permute-done.13.refs_6_ = bf16[256,192]{1,0:T(8,128)(2,1)S(1)} collective-permute-done((bf16[256,192]{1,0:T(8,128)(2,1)S(1)}, bf16[256,192]{1,0:T(8,128)(2,1)S(1)}, u32[]{:S(2)}, u32[]{:S(2)}) %collective-permute-start.13) | collective-permute-done | bytes 98336 | tf_op jit(solution)/shard_map/ppermute | solution.py:55
  171.4 12.2 %attend_back.1 = (bf16[1024,576]{1,0:T(8,128)(2,1)}, f32[16,576]{1,0:T(8,128)S(1)}, f32[256,768]{1,0:T(8,128)}, bf16[256,768]{1,0:T(8,128)(2,1)S(1)}, bf16[256,7...) custom-call(s32[1]{0:T(128)} %bitcast.1.place_ref, s32[1]{0:T(128)S(6)} %copy.119.length_ref, ...), custom_call_target="tpu_custom_call" | custom-call | flops 4026531840 | bytes 8388608 | tf_op jit(solution)/shard_map/attend_back/pallas_call | solution.py:274
  183.6 3.4 %fusion.22 = bf16[768,576]{0,1:T(8,128)(2,1)} fusion(bf16[1024,576]{1,0:T(8,128)(2,1)} %get-tuple-element.99, bf16[256,768]{1,0:T(8,128)(2,1)S(1)} %copy-done.12, bf16[256,768]{1,0:T(8,128)(2,1)S(1)} %copy-done.14, bf16[256,768]{1,0:T(8,128)(2,1)S(1)} %copy-done.16, bf16[256,768]{1,0:T(8,128)(2,1)S(1)} %bitcast.128), kind=kOutput, calls=%fused_computation.40 | convolution fusion | flops 912703488 | bytes 3637248 | tf_op jit(solution)/shard_map/dot_general | solution.py:523
  189.6 4.4 %collective-permute-done.24 = bf16[2,96,1920]{2,1,0:T(8,128)(2,1)} collective-permute-done((bf16[2,96,1920]{2,1,0:T(8,128)(2,1)}, bf16[2,96,1920]{2,1,0:T(8,128)(2,1)}, u32[]{:S(2)}, u32[]{:S(2)}) %collective-permute-start.24) | collective-permute-done | bytes 737312 | tf_op jit(solution)/shard_map/ppermute | solution.py:102
  213.3 2.5 collective-permute-start.18
  229.4 12.8 %collective-permute-done.18 = bf16[256,768]{1,0:T(8,128)(2,1)S(1)} collective-permute-done((bf16[256,768]{1,0:T(8,128)(2,1)S(1)}, bf16[256,768]{1,0:T(8,128)(2,1)S(1)}, u32[]{:S(2)}, u32[]{:S(2)}) %collective-permute-start.18) | collective-permute-done | bytes 393248 | tf_op jit(solution)/shard_map/ppermute | solution.py:55
  242.2 10.1 %collective-permute-start.31 = (bf16[96,960]{1,0:T(8,128)(2,1)}, bf16[96,960]{1,0:T(8,128)(2,1)S(1)}, u32[]{:S(2)}, u32[]{:S(2)}) collective-permute-start(bf16[96,960]{1,0:T(8,128)(2,1)} %pad_maximum_fusion.6), channel_id=1, source_target_pairs={{0,16},{8,24},{16,0},{24,8},{1,17},{9,25},{17,1},{25,9},{2,18},{10... | collective-permute-start | bytes 552968 | tf_op jit(solution)/shard_map/ppermute | solution.py:55
  252.3 12.1 %collective-permute-start.30 = (bf16[96,960]{1,0:T(8,128)(2,1)}, bf16[96,960]{1,0:T(8,128)(2,1)S(1)}, u32[]{:S(2)}, u32[]{:S(2)}) collective-permute-start(bf16[96,960]{1,0:T(8,128)(2,1)} %pad_maximum_fusion.7), channel_id=1, source_target_pairs={{0,8},{8,16},{16,24},{24,0},{1,9},{9,17},{17,25},{25,1},{2,10},{10... | collective-permute-start | bytes 552968 | tf_op jit(solution)/shard_map/ppermute | solution.py:55
  264.4 2.4 add_add_fusion
  268.0 4.9 %collective-permute-done.31 = bf16[96,960]{1,0:T(8,128)(2,1)S(1)} collective-permute-done((bf16[96,960]{1,0:T(8,128)(2,1)}, bf16[96,960]{1,0:T(8,128)(2,1)S(1)}, u32[]{:S(2)}, u32[]{:S(2)}) %collective-permute-start.31) | collective-permute-done | bytes 184352 | tf_op jit(solution)/shard_map/ppermute | solution.py:55
  (318 shorter events, 101.2 us)
Async XLA Ops:
  7.2 101.2 %all-gather.5.cloned.1.call-start = ((), (), s32[]{:S(2)}) async-start(), calls=%async_computation.1 | async-start | bytes 3096576 | tf_op jit(solution)/shard_map/all_gather | solution.py:376
  10.2 104.8 %all-gather.7.cloned.1.call-start = ((), (), s32[]{:S(2)}) async-start(), calls=%async_computation.2 | async-start | bytes 9068544 | tf_op jit(solution)/shard_map/all_gather | solution.py:396
  10.2 22.7 %collective-permute-start.11 = (bf16[96,1728]{1,0:T(8,128)(2,1)}, bf16[96,1728]{1,0:T(8,128)(2,1)S(1)}, u32[]{:S(2)}, u32[]{:S(2)}) collective-permute-start(bf16[96,1728]{1,0:T(8,128)(2,1)} %pad_maximum_fusion.4), channel_id=1, source_target_pairs={{0,24},{8,0},{16,8},{24,16},{1,25},{9,1},{17,9},{25,17},{2,26},{10... | collective-permute-start | bytes 995336 | tf_op jit(solution)/shard_map/ppermute | solution.py:55
  15.4 29.6 %collective-permute-start.10 = (bf16[96,1728]{1,0:T(8,128)(2,1)}, bf16[96,1728]{1,0:T(8,128)(2,1)}, u32[]{:S(2)}, u32[]{:S(2)}) collective-permute-start(bf16[96,1728]{1,0:T(8,128)(2,1)} %pad_maximum_fusion.4), channel_id=1, source_target_pairs={{0,16},{8,24},{16,0},{24,8},{1,17},{9,25},{17,1},{25,9},{2,18},{10... | collective-permute-start | bytes 995336 | tf_op jit(solution)/shard_map/ppermute | solution.py:55
  15.4 29.6 %collective-permute-start.9 = (bf16[96,1728]{1,0:T(8,128)(2,1)}, bf16[96,1728]{1,0:T(8,128)(2,1)S(1)}, u32[]{:S(2)}, u32[]{:S(2)}) collective-permute-start(bf16[96,1728]{1,0:T(8,128)(2,1)} %pad_maximum_fusion.4), channel_id=1, source_target_pairs={{0,8},{8,16},{16,24},{24,0},{1,9},{9,17},{17,25},{25,1},{2,10},{10... | collective-permute-start | bytes 995336 | tf_op jit(solution)/shard_map/ppermute | solution.py:55
  48.0 153.1 %reduce-scatter.2.cloned.1.call-start = ((), (), s32[]{:S(2)}) async-start(), calls=%async_computation.3 | async-start | bytes 5308416 | tf_op jit(solution)/shard_map/reduce_scatter | solution.py:457
  48.1 33.3 %collective-permute-start.2 = (bf16[256,768]{1,0:T(8,128)(2,1)S(1)}, bf16[256,768]{1,0:T(8,128)(2,1)S(1)}, u32[]{:S(2)}, u32[]{:S(2)}) collective-permute-start(bf16[256,768]{1,0:T(8,128)(2,1)S(1)} %bitcast.124), channel_id=1, source_target_pairs={{0,24},{8,0},{16,8},{24,16},{1,25},{9,1},{17,9},{25,17},{2,26},{10... | collective-permute-start | bytes 1179656 | tf_op jit(solution)/shard_map/ppermute | solution.py:55
  48.2 33.3 %collective-permute-start.1 = (bf16[256,768]{1,0:T(8,128)(2,1)S(1)}, bf16[256,768]{1,0:T(8,128)(2,1)S(1)}, u32[]{:S(2)}, u32[]{:S(2)}) collective-permute-start(bf16[256,768]{1,0:T(8,128)(2,1)S(1)} %bitcast.125), channel_id=1, source_target_pairs={{0,16},{8,24},{16,0},{24,8},{1,17},{9,25},{17,1},{25,9},{2,18},{10... | collective-permute-start | bytes 1179656 | tf_op jit(solution)/shard_map/ppermute | solution.py:55
  50.9 29.1 %collective-permute-start.4 = (bf16[12,192]{0,1:T(8,128)(2,1)S(1)}, bf16[12,192]{0,1:T(8,128)(2,1)S(1)}, u32[]{:S(2)}, u32[]{:S(2)}) collective-permute-start(bf16[12,192]{0,1:T(8,128)(2,1)S(1)} %slice.394), channel_id=1, source_target_pairs={{0,16},{8,24},{16,0},{24,8},{1,17},{9,25},{17,1},{25,9},{2,18},{10... | collective-permute-start | bytes 13832 | tf_op jit(solution)/shard_map/ppermute | solution.py:55
  51.1 28.9 %collective-permute-start.3 = (bf16[12,192]{0,1:T(8,128)(2,1)S(1)}, bf16[12,192]{0,1:T(8,128)(2,1)S(1)}, u32[]{:S(2)}, u32[]{:S(2)}) collective-permute-start(bf16[12,192]{0,1:T(8,128)(2,1)S(1)} %slice.394), channel_id=1, source_target_pairs={{0,8},{8,16},{16,24},{24,0},{1,9},{9,17},{17,25},{25,1},{2,10},{10... | collective-permute-start | bytes 13832 | tf_op jit(solution)/shard_map/ppermute | solution.py:55
  53.1 27.0 %collective-permute-start.5 = (bf16[12,192]{0,1:T(8,128)(2,1)S(1)}, bf16[12,192]{0,1:T(8,128)(2,1)S(1)}, u32[]{:S(2)}, u32[]{:S(2)}) collective-permute-start(bf16[12,192]{0,1:T(8,128)(2,1)S(1)} %slice.394), channel_id=1, source_target_pairs={{0,24},{8,0},{16,8},{24,16},{1,25},{9,1},{17,9},{25,17},{2,26},{10... | collective-permute-start | bytes 13832 | tf_op jit(solution)/shard_map/ppermute | solution.py:55
  149.2 37.9 %collective-permute-start.22 = (f32[16,192]{1,0:T(8,128)S(1)}, f32[16,192]{1,0:T(8,128)S(1)}, u32[]{:S(2)}, u32[]{:S(2)}) collective-permute-start(f32[16,192]{1,0:T(8,128)S(1)} %get-tuple-element.188), channel_id=1, source_target_pairs={{0,24},{8,0},{16,8},{24,16},{1,25},{9,1},{17,9},{25,17},{2,26},{10... | collective-permute-start | bytes 36872 | tf_op jit(solution)/shard_map/ppermute | solution.py:55
  151.1 36.0 %collective-permute-start.21 = (f32[16,192]{1,0:T(8,128)S(1)}, f32[16,192]{1,0:T(8,128)S(1)}, u32[]{:S(2)}, u32[]{:S(2)}) collective-permute-start(f32[16,192]{1,0:T(8,128)S(1)} %get-tuple-element.189), channel_id=1, source_target_pairs={{0,16},{8,24},{16,0},{24,8},{1,17},{9,25},{17,1},{25,9},{2,18},{10... | collective-permute-start | bytes 36872 | tf_op jit(solution)/shard_map/ppermute | solution.py:55
  162.7 24.3 %collective-permute-start.20 = (f32[16,192]{1,0:T(8,128)S(1)}, f32[16,192]{1,0:T(8,128)S(1)}, u32[]{:S(2)}, u32[]{:S(2)}) collective-permute-start(f32[16,192]{1,0:T(8,128)S(1)} %get-tuple-element.190), channel_id=1, source_target_pairs={{0,8},{8,16},{16,24},{24,0},{1,9},{9,17},{17,25},{25,1},{2,10},{10... | collective-permute-start | bytes 36872 | tf_op jit(solution)/shard_map/ppermute | solution.py:55
  168.2 28.4 %collective-permute-start.26 = (bf16[2,96,1920]{2,1,0:T(8,128)(2,1)}, bf16[2,96,1920]{2,1,0:T(8,128)(2,1)}, u32[]{:S(2)}, u32[]{:S(2)}) collective-permute-start(bf16[2,96,1920]{2,1,0:T(8,128)(2,1)} %fusion.41), channel_id=1, source_target_pairs={{0,4},{1,5},{2,6},{3,7},{4,0},{5,1},{6,2},{7,3},{8,12},{9,13},{10,... | collective-permute-start | bytes 2211848 | tf_op jit(solution)/shard_map/ppermute | solution.py:102
  169.8 24.2 %collective-permute-start.24 = (bf16[2,96,1920]{2,1,0:T(8,128)(2,1)}, bf16[2,96,1920]{2,1,0:T(8,128)(2,1)}, u32[]{:S(2)}, u32[]{:S(2)}) collective-permute-start(bf16[2,96,1920]{2,1,0:T(8,128)(2,1)} %fusion.42), channel_id=1, source_target_pairs={{0,2},{1,3},{2,0},{3,1},{4,6},{5,7},{6,4},{7,5},{8,10},{9,11},{10,... | collective-permute-start | bytes 2211848 | tf_op jit(solution)/shard_map/ppermute | solution.py:102
  189.6 20.0 %collective-permute-start.23 = (bf16[4,112,576]{2,1,0:T(8,128)(2,1)}, bf16[4,112,576]{2,1,0:T(8,128)(2,1)}, u32[]{:S(2)}, u32[]{:S(2)}) collective-permute-start(bf16[4,112,576]{2,1,0:T(8,128)(2,1)} %fusion.45), channel_id=1, source_target_pairs={{0,1},{1,0},{2,3},{3,2},{4,5},{5,4},{6,7},{7,6},{8,9},{9,8},{10,11... | collective-permute-start | bytes 1548296 | tf_op jit(solution)/shard_map/ppermute | solution.py:102
  213.3 28.9 %collective-permute-start.18 = (bf16[256,768]{1,0:T(8,128)(2,1)S(1)}, bf16[256,768]{1,0:T(8,128)(2,1)S(1)}, u32[]{:S(2)}, u32[]{:S(2)}) collective-permute-start(bf16[256,768]{1,0:T(8,128)(2,1)S(1)} %get-tuple-element.97), channel_id=1, source_target_pairs={{0,16},{8,24},{16,0},{24,8},{1,17},{9,25},{17,1},{25,9},{2,18},{10... | collective-permute-start | bytes 1179656 | tf_op jit(solution)/shard_map/ppermute | solution.py:55
  215.8 36.5 %collective-permute-start.19 = (bf16[256,768]{1,0:T(8,128)(2,1)S(1)}, bf16[256,768]{1,0:T(8,128)(2,1)}, u32[]{:S(2)}, u32[]{:S(2)}) collective-permute-start(bf16[256,768]{1,0:T(8,128)(2,1)S(1)} %get-tuple-element.98), channel_id=1, source_target_pairs={{0,24},{8,0},{16,8},{24,16},{1,25},{9,1},{17,9},{25,17},{2,26},{10... | collective-permute-start | bytes 1179656 | tf_op jit(solution)/shard_map/ppermute | solution.py:55
  222.1 44.7 %collective-permute-start.33 = (bf16[96,768]{1,0:T(8,128)(2,1)}, bf16[96,768]{1,0:T(8,128)(2,1)S(1)}, u32[]{:S(2)}, u32[]{:S(2)}) collective-permute-start(bf16[96,768]{1,0:T(8,128)(2,1)} %get-tuple-element.163), channel_id=1, source_target_pairs={{0,8},{8,16},{16,24},{24,0},{1,9},{9,17},{17,25},{25,1},{2,10},{10... | collective-permute-start | bytes 442376 | tf_op jit(solution)/shard_map/ppermute | solution.py:55
  224.1 42.7 %collective-permute-start.34 = (bf16[96,768]{1,0:T(8,128)(2,1)}, bf16[96,768]{1,0:T(8,128)(2,1)S(1)}, u32[]{:S(2)}, u32[]{:S(2)}) collective-permute-start(bf16[96,768]{1,0:T(8,128)(2,1)} %get-tuple-element.164), channel_id=1, source_target_pairs={{0,16},{8,24},{16,0},{24,8},{1,17},{9,25},{17,1},{25,9},{2,18},{10... | collective-permute-start | bytes 442376 | tf_op jit(solution)/shard_map/ppermute | solution.py:55
  227.1 39.8 %collective-permute-start.35 = (bf16[96,768]{1,0:T(8,128)(2,1)}, bf16[96,768]{1,0:T(8,128)(2,1)S(1)}, u32[]{:S(2)}, u32[]{:S(2)}) collective-permute-start(bf16[96,768]{1,0:T(8,128)(2,1)} %get-tuple-element.165), channel_id=1, source_target_pairs={{0,24},{8,0},{16,8},{24,16},{1,25},{9,1},{17,9},{25,17},{2,26},{10... | collective-permute-start | bytes 442376 | tf_op jit(solution)/shard_map/ppermute | solution.py:55
  242.2 30.6 %collective-permute-start.31 = (bf16[96,960]{1,0:T(8,128)(2,1)}, bf16[96,960]{1,0:T(8,128)(2,1)S(1)}, u32[]{:S(2)}, u32[]{:S(2)}) collective-permute-start(bf16[96,960]{1,0:T(8,128)(2,1)} %pad_maximum_fusion.6), channel_id=1, source_target_pairs={{0,16},{8,24},{16,0},{24,8},{1,17},{9,25},{17,1},{25,9},{2,18},{10... | collective-permute-start | bytes 552968 | tf_op jit(solution)/shard_map/ppermute | solution.py:55
  252.3 20.5 %collective-permute-start.30 = (bf16[96,960]{1,0:T(8,128)(2,1)}, bf16[96,960]{1,0:T(8,128)(2,1)S(1)}, u32[]{:S(2)}, u32[]{:S(2)}) collective-permute-start(bf16[96,960]{1,0:T(8,128)(2,1)} %pad_maximum_fusion.7), channel_id=1, source_target_pairs={{0,8},{8,16},{16,24},{24,0},{1,9},{9,17},{17,25},{25,1},{2,10},{10... | collective-permute-start | bytes 552968 | tf_op jit(solution)/shard_map/ppermute | solution.py:55
  (83 other events, 852.2 us)
Sparse Core Ops, SparseCore 0:
  10.5 36.0 all-gather.4
  48.4 52.9 all-gather.6
  133.9 61.0 reduce-scatter.1

commit v3 on v2

--- a/solution.py
+++ b/solution.py
@@ -111,8 +111,8 @@
 ):
     count = (len(refs) - 3 - 4 - 2) // 2
     token_refs, weight_refs = refs[:count], refs[count : count + 3]
-    q_ref, k_ref, v_ref, lse_ref = refs[count + 3 : count + 7]
-    mixed_refs, (mixed_all, token_all) = refs[count + 7 : -2], refs[-2:]
+    q_ref, k_ref, v_ref, lse_ref, mixed_all = refs[count + 3 : count + 8]
+    mixed_refs, token_all = refs[count + 8 : -1], refs[-1]
     shard_len = token_refs[0].shape[0]
     _, width = q_ref.shape
     for r, token_ref in enumerate(token_refs):
@@ -172,14 +172,11 @@
     arrays = (bias, *token_pieces, *weights)
     return pl.pallas_call(
         attend_kernel,
-        out_shape=(half, half, half, jax.ShapeDtypeStruct((rows, 8), jnp.float32))
+        out_shape=(half, half, half, jax.ShapeDtypeStruct((rows, 8), jnp.float32), half)
         + (jax.ShapeDtypeStruct((shard_len, width), jnp.bfloat16),) * len(token_pieces),
         in_specs=[smem, smem] + [vmem] * len(arrays),
-        out_specs=(vmem,) * (4 + len(token_pieces)),
-        scratch_shapes=[
-            pltpu.VMEM((rows, width), jnp.bfloat16),
-            pltpu.VMEM((rows, weights[0].shape[0]), jnp.bfloat16),
-        ],
+        out_specs=(vmem,) * (5 + len(token_pieces)),
+        scratch_shapes=[pltpu.VMEM((rows, weights[0].shape[0]), jnp.bfloat16)],
         compiler_params=pltpu.CompilerParams(vmem_limit_bytes=40 << 20),
         cost_estimate=pl.CostEstimate(
             flops=2 * rows * width * (3 * weights[0].shape[0] + 8 * rows),
@@ -197,20 +194,20 @@
     k_ref,
     v_ref,
     lse_ref,
+    mixed_all,
     *refs,
 ):
-    count = (len(refs) - 3 - 2 - 5) // 3
-    mixed_refs, grad_refs = refs[:count], refs[count : 2 * count]
-    weight_refs, refs = refs[2 * count : 2 * count + 3], refs[2 * count + 3 :]
+    count = (len(refs) - 3 - 2 - 4) // 2
+    grad_refs = refs[:count]
+    weight_refs, refs = refs[count : count + 3], refs[count + 3 :]
     all_ref, sums_ref = refs[:2]
     part_refs = refs[2 : 2 + count]
-    dk_sum, dv_sum, mixed_all, grad_all, part_all = refs[2 + count :]
+    dk_sum, dv_sum, grad_all, part_all = refs[2 + count :]
     shard_len = grad_refs[0].shape[0]
     _, width = q_ref.shape
     masked = key_mask(place_ref[0], length_ref[0], count, shard_len)
     for i in range(count):
         at = slice(i * shard_len, (i + 1) * shard_len)
-        mixed_all[at, :] = mixed_refs[i][...]
         grad_all[at, :] = grad_refs[i][...]
     dk_sum[...] = jnp.zeros_like(dk_sum)
     dv_sum[...] = jnp.zeros_like(dv_sum)
@@ -262,15 +259,15 @@
 
 
 def attend_back(
-    place, length, queries, keys_all, values_all, lse, mixed_pieces, grad_pieces, weights
+    place, length, queries, keys_all, values_all, lse, mixed, grad_pieces, weights
 ):
     rows, width = queries.shape
-    shard_len, model_width = mixed_pieces[0].shape[0], weights[0].shape[0]
+    shard_len, model_width = grad_pieces[0].shape[0], weights[0].shape[0]
     smem, vmem = pl.BlockSpec(memory_space=pltpu.SMEM), pl.BlockSpec(memory_space=pltpu.VMEM)
-    arrays = (queries, keys_all, values_all, lse, *mixed_pieces, *grad_pieces, *weights)
+    arrays = (queries, keys_all, values_all, lse, mixed, *grad_pieces, *weights)
     parts = [jax.ShapeDtypeStruct((shard_len, model_width), jnp.float32)] + [
         jax.ShapeDtypeStruct((shard_len, model_width), jnp.bfloat16)
-    ] * (len(mixed_pieces) - 1)
+    ] * (len(grad_pieces) - 1)
     return pl.pallas_call(
         attend_back_kernel,
         out_shape=(
@@ -281,7 +278,7 @@
         in_specs=[smem, smem] + [vmem] * len(arrays),
         out_specs=(vmem,) * (2 + len(parts)),
         scratch_shapes=[pltpu.VMEM((width, rows), jnp.float32)] * 2
-        + [pltpu.VMEM((rows, width), jnp.bfloat16)] * 2
+        + [pltpu.VMEM((rows, width), jnp.bfloat16)]
         + [pltpu.VMEM((rows, model_width), jnp.bfloat16)],
         compiler_params=pltpu.CompilerParams(vmem_limit_bytes=48 << 20),
         cost_estimate=pl.CostEstimate(
@@ -293,37 +290,60 @@
     )(place.reshape(1), length.reshape(1), *arrays)
 
 
+VECTOR_CHUNK = 32
+
+
 def vector_kernel(
-    place_ref, one_ref, two_ref, resid_ref, normed_one_ref, normed_two_ref, cot_ref, pre_ref, out_ref
+    place_ref,
+    one_ref,
+    two_ref,
+    resid_ref,
+    normed_one_ref,
+    normed_two_ref,
+    cot_ref,
+    pre_ref,
+    out_ref,
+    row_sum,
+    pre_sum,
 ):
     seq_count, _, head_width = out_ref.shape
-    model_width = one_ref.shape[1]
-    resid = resid_ref[...]
-    cot = cot_ref[...].astype(jnp.float32)
-    rows = [
-        one_ref[...],
-        two_ref[...],
-        resid * normed_one_ref[...],
-        resid,
-        cot * normed_two_ref[...],
-        cot,
-    ]
+    row_total, model_width = one_ref.shape
+    row_sum[...] = jnp.zeros_like(row_sum)
+    pre_sum[...] = jnp.zeros_like(pre_sum)
+
+    def fold(values):
+        return jnp.sum(values.reshape(VECTOR_CHUNK // 8, 8, values.shape[1]), axis=0)
+
+    def add_rows(i, carry):
+        at = pl.ds(pl.multiple_of(i * VECTOR_CHUNK, VECTOR_CHUNK), VECTOR_CHUNK)
+        resid = resid_ref[at, :]
+        cot = cot_ref[at, :].astype(jnp.float32)
+        lines = [
+            one_ref[at, :],
+            two_ref[at, :],
+            resid * normed_one_ref[at, :],
+            resid,
+            cot * normed_two_ref[at, :],
+            cot,
+        ]
+        for k, values in enumerate(lines):
+            row_sum[8 * k : 8 * k + 8, :] += fold(values)
+        pre_sum[...] += fold(pre_ref[at, :].astype(jnp.float32))
+        return carry
+
+    lax.fori_loop(0, row_total // VECTOR_CHUNK, add_rows, 0)
     out_ref[...] = jnp.zeros_like(out_ref)
-    for k, values in enumerate(rows):
-        total = jnp.sum(values, axis=0, keepdims=True)
+    for k in range(6):
+        total = jnp.sum(row_sum[8 * k : 8 * k + 8, :], axis=0, keepdims=True)
         for j in range(seq_count):
             out_ref[j, 2 + k : 3 + k, :] = total[:, j * head_width : (j + 1) * head_width]
-    pre = pre_ref[...].astype(jnp.float32)
-    per_place = pre.shape[1] // seq_count // model_width
-    totals = [
-        jnp.sum(pre[:, k * model_width : (k + 1) * model_width], axis=0, keepdims=True)
-        for k in range(seq_count * per_place)
-    ]
+    per_place = pre_ref.shape[1] // seq_count // model_width
     for k in range(seq_count):
-        owner = (place_ref[0] + seq_count - k) % seq_count
+        owner = lax.rem(place_ref[0] + seq_count - k, seq_count)
         for i in range(per_place):
             row = 8 + owner * per_place + i
-            total = totals[k * per_place + i]
+            low = (k * per_place + i) * model_width
+            total = jnp.sum(pre_sum[:, low : low + model_width], axis=0, keepdims=True)
             for j in range(seq_count):
                 out_ref[j, pl.ds(row, 1), :] = total[:, j * head_width : (j + 1) * head_width]
 
@@ -335,6 +355,10 @@
         in_specs=[pl.BlockSpec(memory_space=pltpu.SMEM)]
         + [pl.BlockSpec(memory_space=pltpu.VMEM)] * len(arrays),
         out_specs=pl.BlockSpec(memory_space=pltpu.VMEM),
+        scratch_shapes=[
+            pltpu.VMEM((48, arrays[0].shape[1]), jnp.float32),
+            pltpu.VMEM((8, arrays[-1].shape[1]), jnp.float32),
+        ],
         compiler_params=pltpu.CompilerParams(vmem_limit_bytes=32 << 20),
         name="vector_sums",
     )(place.reshape(1), *arrays)
@@ -419,7 +443,7 @@
     up_bias = turn_blocks(vec_wide[8:12].reshape(seq_count, hidden_shard)).reshape(-1)
 
     valid_len = lengths[0]
-    queries, keys_all, values_all, lse, *mixed_pieces = attend(
+    queries, keys_all, values_all, lse, mixed_all, *mixed_pieces = attend(
         place, valid_len, vec_own[:2], after(token_pieces, vec_wide, up_bias), w_qkv
     )
     mixed_rows = jnp.concatenate(swap_behind(mixed_pieces), axis=1)
@@ -473,20 +497,6 @@
         True,
     )
     out_received = swapped(out_sent, bits[0])
-    vec_blocks = vector_sums(
-        place,
-        seq_count,
-        head_width,
-        grad_one,
-        grad_two,
-        grad_resid,
-        normed_one,
-        normed_two,
-        cot_half,
-        grad_pre_half,
-    )
-    vec_order = turn_blocks(vec_blocks)
-    vec_moved = swap_behind([vec_order[r] for r in range(seq_count)])
     up_wide = joined(up_kept, up_received)
     out_wide = joined(out_kept, out_received)
     near_places = seq_count // 2
@@ -509,12 +519,26 @@
         keys_all,
         values_all,
         lse,
-        mixed_pieces,
+        mixed_all,
         grad_pieces,
         w_qkv,
     )
     input_moved = swap_behind([input_own, *input_parts])
-    vec_part = sum(after(vec_moved, input_own))
+    vec_blocks = vector_sums(
+        place,
+        seq_count,
+        head_width,
+        after(grad_one, input_own),
+        grad_two,
+        grad_resid,
+        normed_one,
+        normed_two,
+        cot_half,
+        grad_pre_half,
+    )
+    vec_order = turn_blocks(vec_blocks)
+    vec_moved = swap_behind([vec_order[r] for r in range(seq_count)])
+    vec_part = sum(vec_moved)
     vec_lines = jnp.concatenate(
         [head_sums[:1, :head_width], head_sums[:1, 2 * head_width :], vec_part[2:]], axis=0
     )

time: 286 us -> 293 us (1.024)
  waiting for transfers between devices: 81.7 us -> 90.4 us
    reduce_scatter x1, waiting for transfers between devices: 0.01 us -> 8.33 us  [layer(): lax.psum_scatter(down_local, 'fsdp', scatter_dimension=0, tiled=True)]
    ppermute x27, waiting for transfers between devices: 74.6 us -> 80.6 us  [from_behind(): lax.ppermute(piece, 'seq', [(i, (i + distance) % count) for i in range(co...]
    ppermute x9, waiting for transfers between devices: 7.08 us -> 1.33 us  [swapped(): return lax.ppermute(sent, 'fsdp', pairs)]
    unnamed x138 -> x146, local copies, waits for them, and re-layouts: 10.5 us -> 13.6 us
  transfers between devices with their start and end apart: 39 -> 39, of which waited for: 13 -> 14; matrix products, arithmetic and copies ran while one was open for 17% -> 15% of each run, Pallas kernels for 8% -> 8%
where the time goes in v3:
time: 293 us; the launch traced here: 292 us
  waiting for transfers between devices  90.4 us (31%)
  starting transfers between devices  65.6 us (22%)
  other arithmetic  29 us (10%)
  local copies, waits for them, and re-layouts  28.5 us (10%)
  matrix products  25.2 us (9%)
  Pallas kernels  23.3 us (8%)
  between operations  15.8 us (5%)
  blocking collectives  14.7 us (5%)
    ppermute x27, waiting for transfers between devices, from_behind(): lax.ppermute(piece, 'seq', [(i, (i + distance) % count) for i in range(co...  80.6 us
    ppermute x27, starting transfers between devices, from_behind(): lax.ppermute(piece, 'seq', [(i, (i + distance) % count) for i in range(co...  57.9 us
    all_gather x1, blocking collectives, layer(): qkv_all = lax.all_gather(qkv_shard, 'fsdp', axis=0, tiled=False)  14.7 us
    unnamed x146, local copies, waits for them, and re-layouts  13.6 us
    pallas_call x1, Pallas kernels, attend_back(): pl.pallas_call(attend_back_kernel, out_shape=(jax.ShapeDtypeStruct((rows,...  12.4 us
    pallas_call x1, Pallas kernels, attend(): pl.pallas_call(attend_kernel, out_shape=(half, half, half, jax.ShapeDtype...  10.1 us
    dot_general x6, matrix products, times(): jnp.dot(left, part, preferred_element_type=f32)  9.55 us
    dot_general x6, matrix products, dot_right_t(): lax.dot_general(left, right, (((1,), (1,)), ((), ())), preferred_element_...  8.77 us
  transfers between devices with their start and end apart: 39, of which 14 were waited for; matrix products, arithmetic and copies ran while one was open for 15% of the time, Pallas kernels for 8%

profile of v3, /device:TPU:0, one launch (start us, length us, event | category | flops | bytes accessed | tf_op | source)
XLA Modules:
  0.0 292.4 jit_solution(5116595704291813124)
XLA Ops:
  10.2 5.1 %collective-permute-start.11 = (bf16[96,1728]{1,0:T(8,128)(2,1)}, bf16[96,1728]{1,0:T(8,128)(2,1)S(1)}, u32[]{:S(2)}, u32[]{:S(2)}) collective-permute-start(bf16[96,1728]{1,0:T(8,128)(2,1)} %pad_maximum_fusion.4), channel_id=1, source_target_pairs={{0,24},{8,0},{16,8},{24,16},{1,25},{9,1},{17,9},{25,17},{2,26},{10... | collective-permute-start | bytes 995336 | tf_op jit(solution)/shard_map/ppermute | solution.py:55
  17.0 14.7 %all-gather.1 = bf16[8,304,192]{1,2,0:T(8,128)(2,1)S(1)} all-gather(bf16[1,304,192]{1,2,0:T(8,128)(2,1)S(1)} %copy.97), channel_id=2, replica_groups=mesh['seq'=4,'fsdp'=8] {'fsdp'}, dimensions={0}, use_global_device_ids=true | all-gather | bytes 1050624 | tf_op jit(solution)/shard_map/all_gather | solution.py:403
  32.9 12.1 %collective-permute-done.10 = bf16[96,1728]{1,0:T(8,128)(2,1)} collective-permute-done((bf16[96,1728]{1,0:T(8,128)(2,1)}, bf16[96,1728]{1,0:T(8,128)(2,1)}, u32[]{:S(2)}, u32[]{:S(2)}) %collective-permute-start.10) | collective-permute-done | bytes 331808 | tf_op jit(solution)/shard_map/ppermute | solution.py:55
  48.2 2.8 collective-permute-start.1
  56.1 24.0 %collective-permute-done.4 = bf16[12,192]{0,1:T(8,128)(2,1)S(1)} collective-permute-done((bf16[12,192]{0,1:T(8,128)(2,1)S(1)}, bf16[12,192]{0,1:T(8,128)(2,1)S(1)}, u32[]{:S(2)}, u32[]{:S(2)}) %collective-permute-start.4) | collective-permute-done | bytes 4640 | tf_op jit(solution)/shard_map/ppermute | solution.py:55
  81.4 9.7 %collective-permute-done.refs_1_ = bf16[256,768]{1,0:T(8,128)(2,1)S(1)} collective-permute-done((bf16[256,768]{1,0:T(8,128)(2,1)S(1)}, bf16[256,768]{1,0:T(8,128)(2,1)S(1)}, u32[]{:S(2)}, u32[]{:S(2)}) %collective-permute-start) | collective-permute-done | bytes 393248 | tf_op jit(solution)/shard_map/ppermute | solution.py:55
  91.2 10.1 %attend.1 = (bf16[1024,192]{1,0:T(8,128)(2,1)S(1)}, bf16[1024,192]{1,0:T(8,128)(2,1)S(1)}, bf16[1024,192]{1,0:T(8,128)(2,1)S(1)}, f32[1024,8]{1,0:T(8,128)S(1)},...) custom-call(s32[1]{0:T(128)} %bitcast.1.place_ref, ...), custom_call_target="tpu_custom_call" | custom-call | flops 4127195136 | bytes 8388608 | tf_op jit(solution)/shard_map/attend/pallas_call | solution.py:173
  106.1 3.1 %collective-permute-start.8 = (bf16[256,192]{1,0:T(8,128)(2,1)S(1)}, bf16[256,192]{1,0:T(8,128)(2,1)S(1)}, u32[]{:S(2)}, u32[]{:S(2)}) collective-permute-start(bf16[256,192]{1,0:T(8,128)(2,1)S(1)} %get-tuple-element.73), channel_id=1, source_target_pairs={{0,24},{8,0},{16,8},{24,16},{1,25},{9,1},{17,9},{25,17},{2,26},{10... | collective-permute-start | bytes 294920 | tf_op jit(solution)/shard_map/ppermute | solution.py:55
  110.5 2.4 collective-permute-done.6
  112.9 2.8 collective-permute-done.7
  118.7 3.1 %fusion.12 = f32[256,2304]{1,0:T(8,128)S(1)} fusion(bf16[256,768]{1,0:T(8,128)(2,1)S(1)} %get-tuple-element.147, bf16[768,5184]{1,0:T(8,128)(2,1)} %all-gather.7.cloned.1.call-done), kind=kOutput, calls=%fused_computation.19 | convolution fusion | flops 905969664 | bytes 6291456 | tf_op jit(solution)/shard_map/dot_general | solution.py:428
  123.9 3.1 %fusion.8 = f32[256,768]{1,0:T(8,128)S(1)} fusion(bf16[768,5184]{1,0:T(8,128)(2,1)} %all-gather.7.cloned.1.call-done, bf16[256,3072]{1,0:T(8,128)(2,1)S(1)} %multiply_convert_fusion), kind=kOutput, calls=%fused_computation.15 | convolution fusion | flops 905969664 | bytes 5505024 | tf_op jit(solution)/shard_map/dot_general | solution.py:46
  130.8 3.6 %convolution_convert_fusion.1 = bf16[768,3072]{1,0:T(8,128)(2,1)} fusion(bf16[256,768]{1,0:T(8,128)(2,1)S(1)} %get-tuple-element.77, bf16[256,3072]{1,0:T(8,128)(2,1)S(1)} %multiply_convert_fusion), kind=kOutput, calls=%fused_computation.1 | convolution fusion | flops 1210318848 | bytes 6684672 | tf_op jit(solution)/shard_map/dot_general | solution.py:465
  136.4 3.4 %fusion.6 = f32[256,2304]{1,0:T(8,128)S(1)} fusion(bf16[256,768]{1,0:T(8,128)(2,1)} %copy-done.44, bf16[768,5184]{1,0:T(8,128)(2,1)} %all-gather.7.cloned.1.call-done), kind=kOutput, calls=%fused_computation.13 | convolution fusion | flops 905969664 | bytes 6291456 | tf_op jit(solution)/shard_map/dot_general | solution.py:428
  160.5 5.1 %collective-permute-done.13.refs_2_ = bf16[256,192]{1,0:T(8,128)(2,1)S(1)} collective-permute-done((bf16[256,192]{1,0:T(8,128)(2,1)S(1)}, bf16[256,192]{1,0:T(8,128)(2,1)S(1)}, u32[]{:S(2)}, u32[]{:S(2)}) %collective-permute-start.13) | collective-permute-done | bytes 98336 | tf_op jit(solution)/shard_map/ppermute | solution.py:55
  165.7 12.4 %attend_back.1 = (bf16[1024,576]{1,0:T(8,128)(2,1)}, f32[16,576]{1,0:T(8,128)S(1)}, f32[256,768]{1,0:T(8,128)}, bf16[256,768]{1,0:T(8,128)(2,1)S(1)}, bf16[256,7...) custom-call(s32[1]{0:T(128)} %bitcast.1.place_ref, s32[1]{0:T(128)S(6)} %copy.119.length_ref, ...), custom_call_target="tpu_custom_call" | custom-call | flops 4026531840 | bytes 8388608 | tf_op jit(solution)/shard_map/attend_back/pallas_call | solution.py:271
  197.1 8.3 %reduce-scatter.2.cloned.1.call-done = bf16[96,3072]{1,0:T(8,128)(2,1)} async-done(((bf16[768,3072]{1,0:T(8,128)(2,1)}), bf16[96,3072]{1,0:T(8,128)(2,1)}) %reduce-scatter.2.cloned.1.call-update) | async-done | bytes 589840 | tf_op jit(solution)/shard_map/reduce_scatter | solution.py:481
  215.5 2.7 collective-permute-start.17
  218.2 2.7 collective-permute-start.18
  228.4 3.6 %collective-permute-start.34 = (bf16[96,768]{1,0:T(8,128)(2,1)}, bf16[96,768]{1,0:T(8,128)(2,1)S(1)}, u32[]{:S(2)}, u32[]{:S(2)}) collective-permute-start(bf16[96,768]{1,0:T(8,128)(2,1)} %get-tuple-element.160), channel_id=1, source_target_pairs={{0,16},{8,24},{16,0},{24,8},{1,17},{9,25},{17,1},{25,9},{2,18},{10... | collective-permute-start | bytes 442376 | tf_op jit(solution)/shard_map/ppermute | solution.py:55
  233.9 13.4 %collective-permute-done.18 = bf16[256,768]{1,0:T(8,128)(2,1)} collective-permute-done((bf16[256,768]{1,0:T(8,128)(2,1)S(1)}, bf16[256,768]{1,0:T(8,128)(2,1)}, u32[]{:S(2)}, u32[]{:S(2)}) %collective-permute-start.18) | collective-permute-done | bytes 393248 | tf_op jit(solution)/shard_map/ppermute | solution.py:55
  249.5 19.3 %collective-permute-start.30 = (bf16[96,960]{1,0:T(8,128)(2,1)}, bf16[96,960]{1,0:T(8,128)(2,1)S(1)}, u32[]{:S(2)}, u32[]{:S(2)}) collective-permute-start(bf16[96,960]{1,0:T(8,128)(2,1)} %pad_maximum_fusion.7), channel_id=1, source_target_pairs={{0,8},{8,16},{16,24},{24,0},{1,9},{9,17},{17,25},{25,1},{2,10},{10... | collective-permute-start | bytes 552968 | tf_op jit(solution)/shard_map/ppermute | solution.py:55
  268.7 2.5 add_add_fusion
  272.4 7.3 %collective-permute-done.31 = bf16[96,960]{1,0:T(8,128)(2,1)S(1)} collective-permute-done((bf16[96,960]{1,0:T(8,128)(2,1)}, bf16[96,960]{1,0:T(8,128)(2,1)S(1)}, u32[]{:S(2)}, u32[]{:S(2)}) %collective-permute-start.31) | collective-permute-done | bytes 184352 | tf_op jit(solution)/shard_map/ppermute | solution.py:55
  (326 shorter events, 99.3 us)
Async XLA Ops:
  7.2 102.0 %all-gather.5.cloned.1.call-start = ((), (), s32[]{:S(2)}) async-start(), calls=%async_computation.1 | async-start | bytes 3096576 | tf_op jit(solution)/shard_map/all_gather | solution.py:400
  10.2 105.5 %all-gather.7.cloned.1.call-start = ((), (), s32[]{:S(2)}) async-start(), calls=%async_computation.2 | async-start | bytes 9068544 | tf_op jit(solution)/shard_map/all_gather | solution.py:420
  10.2 22.7 %collective-permute-start.11 = (bf16[96,1728]{1,0:T(8,128)(2,1)}, bf16[96,1728]{1,0:T(8,128)(2,1)S(1)}, u32[]{:S(2)}, u32[]{:S(2)}) collective-permute-start(bf16[96,1728]{1,0:T(8,128)(2,1)} %pad_maximum_fusion.4), channel_id=1, source_target_pairs={{0,24},{8,0},{16,8},{24,16},{1,25},{9,1},{17,9},{25,17},{2,26},{10... | collective-permute-start | bytes 995336 | tf_op jit(solution)/shard_map/ppermute | solution.py:55
  15.4 29.6 %collective-permute-start.10 = (bf16[96,1728]{1,0:T(8,128)(2,1)}, bf16[96,1728]{1,0:T(8,128)(2,1)}, u32[]{:S(2)}, u32[]{:S(2)}) collective-permute-start(bf16[96,1728]{1,0:T(8,128)(2,1)} %pad_maximum_fusion.4), channel_id=1, source_target_pairs={{0,16},{8,24},{16,0},{24,8},{1,17},{9,25},{17,1},{25,9},{2,18},{10... | collective-permute-start | bytes 995336 | tf_op jit(solution)/shard_map/ppermute | solution.py:55
  15.4 29.6 %collective-permute-start.9 = (bf16[96,1728]{1,0:T(8,128)(2,1)}, bf16[96,1728]{1,0:T(8,128)(2,1)S(1)}, u32[]{:S(2)}, u32[]{:S(2)}) collective-permute-start(bf16[96,1728]{1,0:T(8,128)(2,1)} %pad_maximum_fusion.4), channel_id=1, source_target_pairs={{0,8},{8,16},{16,24},{24,0},{1,9},{9,17},{17,25},{25,1},{2,10},{10... | collective-permute-start | bytes 995336 | tf_op jit(solution)/shard_map/ppermute | solution.py:55
  48.0 157.4 %reduce-scatter.2.cloned.1.call-start = ((), (), s32[]{:S(2)}) async-start(), calls=%async_computation.3 | async-start | bytes 5308416 | tf_op jit(solution)/shard_map/reduce_scatter | solution.py:481
  48.1 33.3 %collective-permute-start.2 = (bf16[256,768]{1,0:T(8,128)(2,1)S(1)}, bf16[256,768]{1,0:T(8,128)(2,1)S(1)}, u32[]{:S(2)}, u32[]{:S(2)}) collective-permute-start(bf16[256,768]{1,0:T(8,128)(2,1)S(1)} %bitcast.124), channel_id=1, source_target_pairs={{0,24},{8,0},{16,8},{24,16},{1,25},{9,1},{17,9},{25,17},{2,26},{10... | collective-permute-start | bytes 1179656 | tf_op jit(solution)/shard_map/ppermute | solution.py:55
  48.2 33.3 %collective-permute-start.1 = (bf16[256,768]{1,0:T(8,128)(2,1)S(1)}, bf16[256,768]{1,0:T(8,128)(2,1)S(1)}, u32[]{:S(2)}, u32[]{:S(2)}) collective-permute-start(bf16[256,768]{1,0:T(8,128)(2,1)S(1)} %bitcast.125), channel_id=1, source_target_pairs={{0,16},{8,24},{16,0},{24,8},{1,17},{9,25},{17,1},{25,9},{2,18},{10... | collective-permute-start | bytes 1179656 | tf_op jit(solution)/shard_map/ppermute | solution.py:55
  50.9 29.1 %collective-permute-start.4 = (bf16[12,192]{0,1:T(8,128)(2,1)S(1)}, bf16[12,192]{0,1:T(8,128)(2,1)S(1)}, u32[]{:S(2)}, u32[]{:S(2)}) collective-permute-start(bf16[12,192]{0,1:T(8,128)(2,1)S(1)} %slice.394), channel_id=1, source_target_pairs={{0,16},{8,24},{16,0},{24,8},{1,17},{9,25},{17,1},{25,9},{2,18},{10... | collective-permute-start | bytes 13832 | tf_op jit(solution)/shard_map/ppermute | solution.py:55
  51.2 28.9 %collective-permute-start.3 = (bf16[12,192]{0,1:T(8,128)(2,1)S(1)}, bf16[12,192]{0,1:T(8,128)(2,1)S(1)}, u32[]{:S(2)}, u32[]{:S(2)}) collective-permute-start(bf16[12,192]{0,1:T(8,128)(2,1)S(1)} %slice.394), channel_id=1, source_target_pairs={{0,8},{8,16},{16,24},{24,0},{1,9},{9,17},{17,25},{25,1},{2,10},{10... | collective-permute-start | bytes 13832 | tf_op jit(solution)/shard_map/ppermute | solution.py:55
  53.1 27.0 %collective-permute-start.5 = (bf16[12,192]{0,1:T(8,128)(2,1)S(1)}, bf16[12,192]{0,1:T(8,128)(2,1)S(1)}, u32[]{:S(2)}, u32[]{:S(2)}) collective-permute-start(bf16[12,192]{0,1:T(8,128)(2,1)S(1)} %slice.394), channel_id=1, source_target_pairs={{0,24},{8,0},{16,8},{24,16},{1,25},{9,1},{17,9},{25,17},{2,26},{10... | collective-permute-start | bytes 13832 | tf_op jit(solution)/shard_map/ppermute | solution.py:55
  151.5 14.1 %collective-permute-start.13 = (bf16[256,192]{1,0:T(8,128)(2,1)S(1)}, bf16[256,192]{1,0:T(8,128)(2,1)S(1)}, u32[]{:S(2)}, u32[]{:S(2)}) collective-permute-start(bf16[256,192]{1,0:T(8,128)(2,1)S(1)} %get-tuple-element.174), channel_id=1, source_target_pairs={{0,16},{8,24},{16,0},{24,8},{1,17},{9,25},{17,1},{25,9},{2,18},{10... | collective-permute-start | bytes 294920 | tf_op jit(solution)/shard_map/ppermute | solution.py:55
  156.5 36.2 %collective-permute-start.26 = (bf16[2,96,1920]{2,1,0:T(8,128)(2,1)}, bf16[2,96,1920]{2,1,0:T(8,128)(2,1)}, u32[]{:S(2)}, u32[]{:S(2)}) collective-permute-start(bf16[2,96,1920]{2,1,0:T(8,128)(2,1)} %fusion.41), channel_id=1, source_target_pairs={{0,4},{1,5},{2,6},{3,7},{4,0},{5,1},{6,2},{7,3},{8,12},{9,13},{10,... | collective-permute-start | bytes 2211848 | tf_op jit(solution)/shard_map/ppermute | solution.py:102
  159.3 29.2 %collective-permute-start.24 = (bf16[2,96,1920]{2,1,0:T(8,128)(2,1)}, bf16[2,96,1920]{2,1,0:T(8,128)(2,1)}, u32[]{:S(2)}, u32[]{:S(2)}) collective-permute-start(bf16[2,96,1920]{2,1,0:T(8,128)(2,1)} %fusion.42), channel_id=1, source_target_pairs={{0,2},{1,3},{2,0},{3,1},{4,6},{5,7},{6,4},{7,5},{8,10},{9,11},{10,... | collective-permute-start | bytes 2211848 | tf_op jit(solution)/shard_map/ppermute | solution.py:102
  188.5 24.3 %collective-permute-start.23 = (bf16[4,112,576]{2,1,0:T(8,128)(2,1)}, bf16[4,112,576]{2,1,0:T(8,128)(2,1)}, u32[]{:S(2)}, u32[]{:S(2)}) collective-permute-start(bf16[4,112,576]{2,1,0:T(8,128)(2,1)} %fusion.45), channel_id=1, source_target_pairs={{0,1},{1,0},{2,3},{3,2},{4,5},{5,4},{6,7},{7,6},{8,9},{9,8},{10,11... | collective-permute-start | bytes 1548296 | tf_op jit(solution)/shard_map/ppermute | solution.py:102
  191.2 16.2 %collective-permute-start.25 = (bf16[1,96,1920]{2,1,0:T(8,128)(2,1)}, bf16[1,96,1920]{2,1,0:T(8,128)(2,1)}, u32[]{:S(2)}, u32[]{:S(2)}) collective-permute-start(bf16[1,96,1920]{2,1,0:T(8,128)(2,1)} %dynamic-slice_convert_fusion.2), channel_id=1, source_target_pairs={{0,4},{1,5},{2,6},{3,7},{4,0},{5,1},{6,2},{7,3},{8,12},{9,13},{10,... | collective-permute-start | bytes 1105928 | tf_op jit(solution)/shard_map/ppermute | solution.py:102
  215.5 17.5 %collective-permute-start.17 = (bf16[256,768]{1,0:T(8,128)(2,1)S(1)}, bf16[256,768]{1,0:T(8,128)(2,1)S(1)}, u32[]{:S(2)}, u32[]{:S(2)}) collective-permute-start(bf16[256,768]{1,0:T(8,128)(2,1)S(1)} %copy-done.22), channel_id=1, source_target_pairs={{0,8},{8,16},{16,24},{24,0},{1,9},{9,17},{17,25},{25,1},{2,10},{10... | collective-permute-start | bytes 1179656 | tf_op jit(solution)/shard_map/ppermute | solution.py:55
  218.2 29.2 %collective-permute-start.18 = (bf16[256,768]{1,0:T(8,128)(2,1)S(1)}, bf16[256,768]{1,0:T(8,128)(2,1)}, u32[]{:S(2)}, u32[]{:S(2)}) collective-permute-start(bf16[256,768]{1,0:T(8,128)(2,1)S(1)} %copy-done.20), channel_id=1, source_target_pairs={{0,16},{8,24},{16,0},{24,8},{1,17},{9,25},{17,1},{25,9},{2,18},{10... | collective-permute-start | bytes 1179656 | tf_op jit(solution)/shard_map/ppermute | solution.py:55
  220.9 28.6 %collective-permute-start.19 = (bf16[256,768]{1,0:T(8,128)(2,1)S(1)}, bf16[256,768]{1,0:T(8,128)(2,1)}, u32[]{:S(2)}, u32[]{:S(2)}) collective-permute-start(bf16[256,768]{1,0:T(8,128)(2,1)S(1)} %copy-done.18), channel_id=1, source_target_pairs={{0,24},{8,0},{16,8},{24,16},{1,25},{9,1},{17,9},{25,17},{2,26},{10... | collective-permute-start | bytes 1179656 | tf_op jit(solution)/shard_map/ppermute | solution.py:55
  224.9 46.3 %collective-permute-start.33 = (bf16[96,768]{1,0:T(8,128)(2,1)}, bf16[96,768]{1,0:T(8,128)(2,1)S(1)}, u32[]{:S(2)}, u32[]{:S(2)}) collective-permute-start(bf16[96,768]{1,0:T(8,128)(2,1)} %get-tuple-element.159), channel_id=1, source_target_pairs={{0,8},{8,16},{16,24},{24,0},{1,9},{9,17},{17,25},{25,1},{2,10},{10... | collective-permute-start | bytes 442376 | tf_op jit(solution)/shard_map/ppermute | solution.py:55
  228.4 42.9 %collective-permute-start.34 = (bf16[96,768]{1,0:T(8,128)(2,1)}, bf16[96,768]{1,0:T(8,128)(2,1)S(1)}, u32[]{:S(2)}, u32[]{:S(2)}) collective-permute-start(bf16[96,768]{1,0:T(8,128)(2,1)} %get-tuple-element.160), channel_id=1, source_target_pairs={{0,16},{8,24},{16,0},{24,8},{1,17},{9,25},{17,1},{25,9},{2,18},{10... | collective-permute-start | bytes 442376 | tf_op jit(solution)/shard_map/ppermute | solution.py:55
  233.0 38.3 %collective-permute-start.35 = (bf16[96,768]{1,0:T(8,128)(2,1)}, bf16[96,768]{1,0:T(8,128)(2,1)S(1)}, u32[]{:S(2)}, u32[]{:S(2)}) collective-permute-start(bf16[96,768]{1,0:T(8,128)(2,1)} %get-tuple-element.161), channel_id=1, source_target_pairs={{0,24},{8,0},{16,8},{24,16},{1,25},{9,1},{17,9},{25,17},{2,26},{10... | collective-permute-start | bytes 442376 | tf_op jit(solution)/shard_map/ppermute | solution.py:55
  247.4 32.3 %collective-permute-start.31 = (bf16[96,960]{1,0:T(8,128)(2,1)}, bf16[96,960]{1,0:T(8,128)(2,1)S(1)}, u32[]{:S(2)}, u32[]{:S(2)}) collective-permute-start(bf16[96,960]{1,0:T(8,128)(2,1)} %pad_maximum_fusion.6), channel_id=1, source_target_pairs={{0,16},{8,24},{16,0},{24,8},{1,17},{9,25},{17,1},{25,9},{2,18},{10... | collective-permute-start | bytes 552968 | tf_op jit(solution)/shard_map/ppermute | solution.py:55
  249.5 30.3 %collective-permute-start.30 = (bf16[96,960]{1,0:T(8,128)(2,1)}, bf16[96,960]{1,0:T(8,128)(2,1)S(1)}, u32[]{:S(2)}, u32[]{:S(2)}) collective-permute-start(bf16[96,960]{1,0:T(8,128)(2,1)} %pad_maximum_fusion.7), channel_id=1, source_target_pairs={{0,8},{8,16},{16,24},{24,0},{1,9},{9,17},{17,25},{25,1},{2,10},{10... | collective-permute-start | bytes 552968 | tf_op jit(solution)/shard_map/ppermute | solution.py:55
  (87 other events, 800.9 us)
Sparse Core Ops, SparseCore 0:
  10.5 36.0 all-gather.4
  48.4 52.9 all-gather.6
  134.6 70.7 reduce-scatter.1

commit v4 on v2

--- a/solution.py
+++ b/solution.py
@@ -48,26 +48,50 @@
     )
 
 
-def from_behind(piece, distance):
+def across(piece, bits):
     count = lax.axis_size("seq")
-    if distance % count == 0:
-        return piece
-    return lax.ppermute(piece, "seq", [(i, (i + distance) % count) for i in range(count)])
-
-
-def gather_behind(piece):
-    return [from_behind(piece, r) for r in range(lax.axis_size("seq"))]
-
-
-def swap_behind(pieces):
+    return lax.ppermute(piece, "seq", [(i, i ^ bits) for i in range(count)])
+
+
+def seq_bits():
+    return range(lax.axis_size("seq").bit_length() - 1)
+
+
+def gather_across(piece):
+    pieces = {0: piece}
+    for bit in reversed(seq_bits()):
+        for r in sorted(pieces, reverse=True):
+            pieces[r | 1 << bit] = across(pieces[r], 1 << bit)
+    return [pieces[r] for r in sorted(pieces)]
+
+
+def swap_across(pieces):
+    return pieces[:1] + [across(piece, r) for r, piece in enumerate(pieces) if r]
+
+
+def sum_across(pieces):
     count = len(pieces)
-    return [from_behind(pieces[(-r) % count], r) for r in range(count)]
+    totals = {r: [piece] for r, piece in enumerate(pieces)}
+    for bit in seq_bits():
+        step = 1 << bit
+        for r in reversed(range(step, count, 2 * step)):
+            terms = totals.pop(r)
+            sent = terms[0].astype(jnp.bfloat16) if len(terms) == 1 else total_of(terms)
+            totals[r - step].append(across(sent.astype(jnp.bfloat16), step))
+    return totals[0]
+
+
+def total_of(pieces):
+    total = pieces[0].astype(jnp.float32)
+    for piece in pieces[1:]:
+        total = total + piece.astype(jnp.float32)
+    return total
 
 
 def turn_blocks(blocks):
     count = blocks.shape[0]
     place = lax.axis_index("seq")
-    order = (place - jnp.arange(count, dtype=jnp.int32)) % count
+    order = place ^ jnp.arange(count, dtype=jnp.int32)
     mask = order[:, None] == jnp.arange(count, dtype=jnp.int32)[None, :]
     mask = mask.reshape((count, count) + (1,) * (blocks.ndim - 1))
     return jnp.sum(jnp.where(mask, blocks[None], jnp.zeros((), blocks.dtype)), axis=1)
@@ -159,7 +183,7 @@
     column = lax.broadcasted_iota(jnp.int32, (1, shard_len), 1)
     pieces = []
     for r in range(count):
-        start = lax.rem(place + count - r, count) * shard_len
+        start = (place ^ r) * shard_len
         pieces.append(jnp.where(column + start < length, 0.0, -jnp.inf))
     return jnp.concatenate(pieces, axis=1)
 
@@ -320,7 +344,7 @@
         for k in range(seq_count * per_place)
     ]
     for k in range(seq_count):
-        owner = (place_ref[0] + seq_count - k) % seq_count
+        owner = place_ref[0] ^ k
         for i in range(per_place):
             row = 8 + owner * per_place + i
             total = totals[k * per_place + i]
@@ -374,8 +398,8 @@
         [w_attn[:3].astype(bf16).reshape(3 * row_shard, head_width), vec_placed], axis=0
     )
     own_all = lax.all_gather(own_shard, "fsdp", axis=0, tiled=True)
-    weight_pieces = gather_behind(own_shard)[1:]
-    token_pieces = gather_behind(token_rows)
+    weight_pieces = gather_across(own_shard)[1:]
+    token_pieces = gather_across(token_rows)
     qkv_all = lax.all_gather(qkv_shard, "fsdp", axis=0, tiled=False)
     w_qkv = [
         qkv_all[:, i * row_shard : (i + 1) * row_shard].reshape(model_width, head_width)
@@ -383,7 +407,6 @@
     ]
     vec_own = jnp.sum(qkv_all[:, 3 * row_shard :].astype(f32), axis=0)[:vec_rows]
     vec_half = vec_own.astype(bf16)
-    weight_pieces = after(weight_pieces, w_qkv, vec_half)
     cuts = (0, hidden_shard, 2 * hidden_shard, 2 * hidden_shard + head_width)
     rest_cat = jnp.concatenate(
         [
@@ -408,13 +431,13 @@
         width = parts[0].shape[1]
         return dot_right_t(left[:, :width], parts[0]) + dot_right_t(left[:, width:], parts[1])
 
-    vec_near = [piece.astype(f32) for piece in gather_behind(vec_half)]
+    vec_near = [piece.astype(f32) for piece in gather_across(vec_half)]
 
     def near(order):
         return sum(jnp.where(order == r, piece, 0.0) for r, piece in enumerate(vec_near))
 
     vec_wide = jnp.concatenate(
-        [near((place - j) % seq_count) for j in range(seq_count)], axis=1
+        [near(place ^ j) for j in range(seq_count)], axis=1
     )
     up_bias = turn_blocks(vec_wide[8:12].reshape(seq_count, hidden_shard)).reshape(-1)
 
@@ -422,7 +445,7 @@
     queries, keys_all, values_all, lse, *mixed_pieces = attend(
         place, valid_len, vec_own[:2], after(token_pieces, vec_wide, up_bias), w_qkv
     )
-    mixed_rows = jnp.concatenate(swap_behind(mixed_pieces), axis=1)
+    mixed_rows = jnp.concatenate(swap_across(mixed_pieces), axis=1)
 
     hidden_one = token_rows.astype(f32) + times_t(mixed_rows, out_parts) + vec_wide[2]
     normed_one, inv_one = layer_norm(hidden_one)
@@ -442,15 +465,6 @@
             left, right, (((0,), (0,)), ((), ())), preferred_element_type=f32
         ).astype(bf16)
 
-    def total_of(pieces):
-        total = pieces[0].astype(f32)
-        for piece in pieces[1:]:
-            total = total + piece.astype(f32)
-        return total
-
-    def halves_of(pieces):
-        return [piece.astype(bf16) for piece in pieces]
-
     down_local, grad_two_half = lax.optimization_barrier(
         (outer(grad_two_half, act_half), grad_two_half)
     )
@@ -465,7 +479,7 @@
     grad_one = norm_back(grad_resid * vec_wide[4], normed_one, inv_one)
     grad_one_half = grad_one.astype(bf16)
     grad_mixed = times(grad_one_half, out_parts).astype(bf16)
-    grad_pieces = swap_behind(jnp.split(grad_mixed, seq_count, axis=1))
+    grad_pieces = swap_across(jnp.split(grad_mixed, seq_count, axis=1))
 
     out_kept, out_sent = halving(
         outer(after(grad_one_half, grad_mixed), mixed_rows).reshape(fsdp_count, row_shard, -1),
@@ -486,7 +500,7 @@
         grad_pre_half,
     )
     vec_order = turn_blocks(vec_blocks)
-    vec_moved = swap_behind([vec_order[r] for r in range(seq_count)])
+    vec_moved = swap_across([vec_order[r] for r in range(seq_count)])
     up_wide = joined(up_kept, up_received)
     out_wide = joined(out_kept, out_received)
     near_places = seq_count // 2
@@ -513,7 +527,7 @@
         grad_pieces,
         w_qkv,
     )
-    input_moved = swap_behind([input_own, *input_parts])
+    input_terms = sum_across([input_own, *input_parts])
     vec_part = sum(after(vec_moved, input_own))
     vec_lines = jnp.concatenate(
         [head_sums[:1, :head_width], head_sums[:1, 2 * head_width :], vec_part[2:]], axis=0
@@ -563,13 +577,13 @@
         wide_moving = moving
         if down_moved is None:
             down_pieces = jnp.split(after(down_part, step), seq_count, axis=1)
-            down_moved = swap_behind(down_pieces)
+            down_moved = sum_across(down_pieces)
             step = down_pieces
     wide_pieces = place_pieces(wide_moving[0], near_places) + place_pieces(
         wide_moving[1], seq_count - near_places
     )
-    wide_sent = halves_of(wide_pieces[1:])
-    wide_moved = swap_behind([wide_pieces[0]] + wide_sent)
+    wide_sent = [piece.astype(bf16) for piece in wide_pieces[1:]]
+    wide_moved = sum_across([wide_pieces[0]] + wide_sent)
     step = wide_sent
     for bit in bits[1:]:
         qkv_half = joined(qkv_kept, after(qkv_received, step))
@@ -577,9 +591,9 @@
         qkv_received = swapped(qkv_sent, bit)
         step = qkv_sent
     qkv_sum = joined(qkv_kept, qkv_received)[0]
-    input_grad = grad_one + total_of([input_moved[0]] + after(input_moved[1:], qkv_sum))
-    down_sum = total_of([down_moved[0]] + after(down_moved[1:], input_grad))
-    up_out_sum = total_of([wide_moved[0]] + after(wide_moved[1:], down_sum))
+    input_grad = grad_one + total_of(input_terms[:1] + after(input_terms[1:], qkv_sum))
+    down_sum = total_of(down_moved[:1] + after(down_moved[1:], input_grad))
+    up_out_sum = total_of(wide_moved[:1] + after(wide_moved[1:], down_sum))
 
     token_total = shard_len * seq_count * fsdp_count
     grad_scale = float(token_total) ** (-0.5)

time: 286 us -> 263 us (0.920)
  starting transfers between devices: 67.6 us -> 50.4 us
  local copies, waits for them, and re-layouts: 27.1 us -> 22.6 us
    ppermute x27, starting transfers between devices: 58.6 us -> 41.8 us  [across(): return lax.ppermute(piece, 'seq', [(i, i ^ bits) for i in range(count)])]
    ppermute x9, waiting for transfers between devices: 7.08 us -> 14.4 us  [swapped(): return lax.ppermute(sent, 'fsdp', pairs)]
    ppermute x27, waiting for transfers between devices: 74.6 us -> 68.3 us  [across(): return lax.ppermute(piece, 'seq', [(i, i ^ bits) for i in range(count)])]
    unnamed x138 -> x142, local copies, waits for them, and re-layouts: 10.5 us -> 10.6 us
  transfers between devices with their start and end apart: 39 -> 39, of which waited for: 13 -> 15; matrix products, arithmetic and copies ran while one was open for 17% -> 17% of each run, Pallas kernels for 8% -> 9%
where the time goes in v4:
time: 263 us; the launch traced here: 262 us
  waiting for transfers between devices  82.7 us (31%)
  starting transfers between devices  50.4 us (19%)
  matrix products  27.5 us (10%)
  other arithmetic  26.4 us (10%)
  Pallas kernels  23.2 us (9%)
  local copies, waits for them, and re-layouts  22.6 us (9%)
  between operations  15.8 us (6%)
  blocking collectives  13.3 us (5%)
    ppermute x27, waiting for transfers between devices, across(): return lax.ppermute(piece, 'seq', [(i, i ^ bits) for i in range(count)])  68.3 us
    ppermute x27, starting transfers between devices, across(): return lax.ppermute(piece, 'seq', [(i, i ^ bits) for i in range(count)])  41.8 us
    ppermute x9, waiting for transfers between devices, swapped(): return lax.ppermute(sent, 'fsdp', pairs)  14.4 us
    all_gather x1, blocking collectives, layer(): qkv_all = lax.all_gather(qkv_shard, 'fsdp', axis=0, tiled=False)  13.3 us
    pallas_call x1, Pallas kernels, attend_back(): pl.pallas_call(attend_back_kernel, out_shape=(jax.ShapeDtypeStruct((rows,...  12.2 us
    unnamed x142, local copies, waits for them, and re-layouts  10.6 us
    pallas_call x1, Pallas kernels, attend(): pl.pallas_call(attend_kernel, out_shape=(half, half, half, jax.ShapeDtype...  10.3 us
    dot_general x6, matrix products, times(): jnp.dot(left, part, preferred_element_type=f32)  9.55 us
  transfers between devices with their start and end apart: 39, of which 15 were waited for; matrix products, arithmetic and copies ran while one was open for 17% of the time, Pallas kernels for 9%

profile of v4, /device:TPU:0, one launch (start us, length us, event | category | flops | bytes accessed | tf_op | source)
XLA Modules:
  0.0 261.9 jit_solution(17728203137160636062)
XLA Ops:
  10.2 4.1 %collective-permute-start.10 = (bf16[96,1728]{1,0:T(8,128)(2,1)}, bf16[96,1728]{1,0:T(8,128)(2,1)S(1)}, u32[]{:S(2)}, u32[]{:S(2)}) collective-permute-start(bf16[96,1728]{1,0:T(8,128)(2,1)} %pad_maximum_fusion.4), channel_id=1, source_target_pairs={{0,16},{8,24},{16,0},{24,8},{1,17},{9,25},{17,1},{25,9},{2,18},{10... | collective-permute-start | bytes 995336 | tf_op jit(solution)/shard_map/ppermute | solution.py:53
  15.9 14.2 %collective-permute-done.10 = bf16[96,1728]{1,0:T(8,128)(2,1)S(1)} collective-permute-done((bf16[96,1728]{1,0:T(8,128)(2,1)}, bf16[96,1728]{1,0:T(8,128)(2,1)S(1)}, u32[]{:S(2)}, u32[]{:S(2)}) %collective-permute-start.10) | collective-permute-done | bytes 331808 | tf_op jit(solution)/shard_map/ppermute | solution.py:53
  30.9 8.4 %collective-permute-done.11 = bf16[96,1728]{1,0:T(8,128)(2,1)S(1)} collective-permute-done((bf16[96,1728]{1,0:T(8,128)(2,1)S(1)}, bf16[96,1728]{1,0:T(8,128)(2,1)S(1)}, u32[]{:S(2)}, u32[]{:S(2)}) %collective-permute-start.11) | collective-permute-done | bytes 331808 | tf_op jit(solution)/shard_map/ppermute | solution.py:53
  40.5 3.1 %collective-permute-start.1 = (bf16[256,768]{1,0:T(8,128)(2,1)S(1)}, bf16[256,768]{1,0:T(8,128)(2,1)S(1)}, u32[]{:S(2)}, u32[]{:S(2)}) collective-permute-start(bf16[256,768]{1,0:T(8,128)(2,1)S(1)} %bitcast.124), channel_id=1, source_target_pairs={{0,16},{8,24},{16,0},{24,8},{1,17},{9,25},{17,1},{25,9},{2,18},{10... | collective-permute-start | bytes 1179656 | tf_op jit(solution)/shard_map/ppermute | solution.py:53
  46.0 13.3 %all-gather.1 = bf16[8,304,192]{1,2,0:T(8,128)(2,1)S(1)} all-gather(bf16[1,304,192]{1,2,0:T(8,128)(2,1)S(1)} %copy.97), channel_id=2, replica_groups=mesh['seq'=4,'fsdp'=8] {'fsdp'}, dimensions={0}, use_global_device_ids=true | all-gather | bytes 1050624 | tf_op jit(solution)/shard_map/all_gather | solution.py:403
  61.1 5.0 %collective-permute-done.4 = bf16[12,192]{0,1:T(8,128)(2,1)} collective-permute-done((bf16[12,192]{0,1:T(8,128)(2,1)}, bf16[12,192]{0,1:T(8,128)(2,1)}, u32[]{:S(2)}, u32[]{:S(2)}) %collective-permute-start.4) | collective-permute-done | bytes 4640 | tf_op jit(solution)/shard_map/ppermute | solution.py:53
  75.9 5.6 %collective-permute-done.2.refs_3_ = bf16[256,768]{1,0:T(8,128)(2,1)S(1)} collective-permute-done((bf16[256,768]{1,0:T(8,128)(2,1)S(1)}, bf16[256,768]{1,0:T(8,128)(2,1)S(1)}, u32[]{:S(2)}, u32[]{:S(2)}) %collective-permute-start.2) | collective-permute-done | bytes 393248 | tf_op jit(solution)/shard_map/ppermute | solution.py:53
  81.5 10.3 %attend.1 = (bf16[1024,192]{1,0:T(8,128)(2,1)S(1)}, bf16[1024,192]{1,0:T(8,128)(2,1)S(1)}, bf16[1024,192]{1,0:T(8,128)(2,1)S(1)}, f32[1024,8]{1,0:T(8,128)S(1)},...) custom-call(s32[1]{0:T(128)} %bitcast.1.place_ref, ...), custom_call_target="tpu_custom_call" | custom-call | flops 4127195136 | bytes 8388608 | tf_op jit(solution)/shard_map/attend/pallas_call | solution.py:197
  102.1 4.4 %collective-permute-done.7 = bf16[256,192]{1,0:T(8,128)(2,1)S(1)} collective-permute-done((bf16[256,192]{1,0:T(8,128)(2,1)S(1)}, bf16[256,192]{1,0:T(8,128)(2,1)S(1)}, u32[]{:S(2)}, u32[]{:S(2)}) %collective-permute-start.7) | collective-permute-done | bytes 98336 | tf_op jit(solution)/shard_map/ppermute | solution.py:53
  109.6 3.1 %fusion.12 = f32[256,2304]{1,0:T(8,128)S(1)} fusion(bf16[256,768]{1,0:T(8,128)(2,1)S(1)} %get-tuple-element.139, bf16[768,5184]{1,0:T(8,128)(2,1)} %all-gather.7.cloned.1.call-done), kind=kOutput, calls=%fused_computation.19 | convolution fusion | flops 905969664 | bytes 6291456 | tf_op jit(solution)/shard_map/dot_general | solution.py:427
  114.2 3.3 %fusion.123 = (f32[256]{0:T(256)S(1)}, f32[256,768]{1,0:T(8,128)S(1)}) fusion(f32[768]{0:T(1024)S(1)} %get-tuple-element.116, f32[256,768]{1,0:T(8,128)S(1)} %fusion.46, bf16[768,5184]{1,0:T(8,128)(2,1)} %all-gather.7.cloned.1.call-done, bf16[256,3072]{1,0:T(8,128)(2,1)S(1)} %multiply_convert_fusion, f32[768]{0:T(1024)S(1)} %get-tuple-element.117, ...), kind=kOutput, calls=%fused_computation.232 | convolution fusion | flops 907149056 | bytes 7091200 | tf_op jit(solution)/shard_map/dot_general | solution.py:46
  120.6 3.6 %convolution_convert_fusion.1 = bf16[768,3072]{1,0:T(8,128)(2,1)} fusion(bf16[256,768]{1,0:T(8,128)(2,1)S(1)} %get-tuple-element.70, bf16[256,3072]{1,0:T(8,128)(2,1)S(1)} %multiply_convert_fusion), kind=kOutput, calls=%fused_computation.1 | convolution fusion | flops 1210318848 | bytes 6684672 | tf_op jit(solution)/shard_map/dot_general | solution.py:464
  126.1 3.4 %fusion.6 = f32[256,2304]{1,0:T(8,128)S(1)} fusion(bf16[256,768]{1,0:T(8,128)(2,1)} %copy-done.40, bf16[768,5184]{1,0:T(8,128)(2,1)} %all-gather.7.cloned.1.call-done), kind=kOutput, calls=%fused_computation.13 | convolution fusion | flops 905969664 | bytes 6291456 | tf_op jit(solution)/shard_map/dot_general | solution.py:427
  153.9 3.5 %collective-permute-start.20 = (f32[16,192]{1,0:T(8,128)S(1)}, f32[16,192]{1,0:T(8,128)S(1)}, u32[]{:S(2)}, u32[]{:S(2)}) collective-permute-start(f32[16,192]{1,0:T(8,128)S(1)} %get-tuple-element.178), channel_id=1, source_target_pairs={{0,8},{8,0},{16,24},{24,16},{1,9},{9,1},{17,25},{25,17},{2,10},{10... | collective-permute-start | bytes 36872 | tf_op jit(solution)/shard_map/ppermute | solution.py:53
  162.0 12.2 %attend_back.1 = (bf16[1024,576]{1,0:T(8,128)(2,1)}, f32[16,576]{1,0:T(8,128)S(1)}, f32[256,768]{1,0:T(8,128)}, bf16[256,768]{1,0:T(8,128)(2,1)S(1)}, bf16[256,7...) custom-call(s32[1]{0:T(128)} %bitcast.1.place_ref, s32[1]{0:T(128)S(6)} %copy.119.length_ref, ...), custom_call_target="tpu_custom_call" | custom-call | flops 4026531840 | bytes 8388608 | tf_op jit(solution)/shard_map/attend_back/pallas_call | solution.py:298
  174.2 3.4 %fusion.22 = bf16[768,576]{0,1:T(8,128)(2,1)} fusion(bf16[1024,576]{1,0:T(8,128)(2,1)} %get-tuple-element.90, bf16[256,768]{1,0:T(8,128)(2,1)S(1)} %copy-done.16, bf16[256,768]{1,0:T(8,128)(2,1)S(1)} %copy-done.12, bf16[256,768]{1,0:T(8,128)(2,1)S(1)} %copy-done.14, bf16[256,768]{1,0:T(8,128)(2,1)S(1)} %bitcast.127), kind=kOutput, calls=%fused_computation.40 | convolution fusion | flops 912703488 | bytes 3637248 | tf_op jit(solution)/shard_map/dot_general | solution.py:537
  180.2 5.3 %collective-permute-done.24 = bf16[2,96,1920]{2,1,0:T(8,128)(2,1)} collective-permute-done((bf16[2,96,1920]{2,1,0:T(8,128)(2,1)}, bf16[2,96,1920]{2,1,0:T(8,128)(2,1)}, u32[]{:S(2)}, u32[]{:S(2)}) %collective-permute-start.24) | collective-permute-done | bytes 737312 | tf_op jit(solution)/shard_map/ppermute | solution.py:126
  196.4 2.7 %collective-permute-done.27 = bf16[1,96,1920]{2,1,0:T(8,128)(2,1)} collective-permute-done((bf16[1,96,1920]{2,1,0:T(8,128)(2,1)}, bf16[1,96,1920]{2,1,0:T(8,128)(2,1)}, u32[]{:S(2)}, u32[]{:S(2)}) %collective-permute-start.27) | collective-permute-done | bytes 368672 | tf_op jit(solution)/shard_map/ppermute | solution.py:126
  201.3 3.2 %collective-permute-done.25 = bf16[1,96,1920]{2,1,0:T(8,128)(2,1)} collective-permute-done((bf16[1,96,1920]{2,1,0:T(8,128)(2,1)}, bf16[1,96,1920]{2,1,0:T(8,128)(2,1)}, u32[]{:S(2)}, u32[]{:S(2)}) %collective-permute-start.25) | collective-permute-done | bytes 368672 | tf_op jit(solution)/shard_map/ppermute | solution.py:126
  208.4 3.8 %collective-permute-done.18 = bf16[256,768]{1,0:T(8,128)(2,1)} collective-permute-done((bf16[256,768]{1,0:T(8,128)(2,1)S(1)}, bf16[256,768]{1,0:T(8,128)(2,1)}, u32[]{:S(2)}, u32[]{:S(2)}) %collective-permute-start.18) | collective-permute-done | bytes 393248 | tf_op jit(solution)/shard_map/ppermute | solution.py:53
  218.2 15.0 %collective-permute-done.31 = bf16[96,960]{1,0:T(8,128)(2,1)S(1)} collective-permute-done((bf16[96,960]{1,0:T(8,128)(2,1)S(1)}, bf16[96,960]{1,0:T(8,128)(2,1)S(1)}, u32[]{:S(2)}, u32[]{:S(2)}) %collective-permute-start.31) | collective-permute-done | bytes 184352 | tf_op jit(solution)/shard_map/ppermute | solution.py:53
  235.0 3.3 %collective-permute-done.29 = bf16[1,112,576]{2,1,0:T(8,128)(2,1)S(1)} collective-permute-done((bf16[1,112,576]{2,1,0:T(8,128)(2,1)S(1)}, bf16[1,112,576]{2,1,0:T(8,128)(2,1)S(1)}, u32[]{:S(2)}, u32[]{:S(2)}) %collective-permute-start.29) | collective-permute-done | bytes 129056 | tf_op jit(solution)/shard_map/ppermute | solution.py:126
  238.8 2.5 collective-permute-start.32
  242.4 6.6 %collective-permute-done.35 = bf16[96,768]{1,0:T(8,128)(2,1)S(1)} collective-permute-done((bf16[96,768]{1,0:T(8,128)(2,1)S(1)}, bf16[96,768]{1,0:T(8,128)(2,1)S(1)}, u32[]{:S(2)}, u32[]{:S(2)}) %collective-permute-start.35) | collective-permute-done | bytes 147488 | tf_op jit(solution)/shard_map/ppermute | solution.py:53
  (324 shorter events, 102.9 us)
Async XLA Ops:
  7.2 92.4 %all-gather.5.cloned.1.call-start = ((), (), s32[]{:S(2)}) async-start(), calls=%async_computation.1 | async-start | bytes 3096576 | tf_op jit(solution)/shard_map/all_gather | solution.py:400
  10.2 96.4 %all-gather.7.cloned.1.call-start = ((), (), s32[]{:S(2)}) async-start(), calls=%async_computation.2 | async-start | bytes 9068544 | tf_op jit(solution)/shard_map/all_gather | solution.py:419
  10.2 19.9 %collective-permute-start.10 = (bf16[96,1728]{1,0:T(8,128)(2,1)}, bf16[96,1728]{1,0:T(8,128)(2,1)S(1)}, u32[]{:S(2)}, u32[]{:S(2)}) collective-permute-start(bf16[96,1728]{1,0:T(8,128)(2,1)} %pad_maximum_fusion.4), channel_id=1, source_target_pairs={{0,16},{8,24},{16,0},{24,8},{1,17},{9,25},{17,1},{25,9},{2,18},{10... | collective-permute-start | bytes 995336 | tf_op jit(solution)/shard_map/ppermute | solution.py:53
  14.4 16.5 %collective-permute-start.9 = (bf16[96,1728]{1,0:T(8,128)(2,1)}, bf16[96,1728]{1,0:T(8,128)(2,1)S(1)}, u32[]{:S(2)}, u32[]{:S(2)}) collective-permute-start(bf16[96,1728]{1,0:T(8,128)(2,1)} %pad_maximum_fusion.4), channel_id=1, source_target_pairs={{0,8},{8,0},{16,24},{24,16},{1,9},{9,1},{17,25},{25,17},{2,10},{10... | collective-permute-start | bytes 995336 | tf_op jit(solution)/shard_map/ppermute | solution.py:53
  40.5 154.9 %reduce-scatter.2.cloned.1.call-start = ((), (), s32[]{:S(2)}) async-start(), calls=%async_computation.3 | async-start | bytes 5308416 | tf_op jit(solution)/shard_map/reduce_scatter | solution.py:471
  40.5 31.3 %collective-permute-start.1 = (bf16[256,768]{1,0:T(8,128)(2,1)S(1)}, bf16[256,768]{1,0:T(8,128)(2,1)S(1)}, u32[]{:S(2)}, u32[]{:S(2)}) collective-permute-start(bf16[256,768]{1,0:T(8,128)(2,1)S(1)} %bitcast.124), channel_id=1, source_target_pairs={{0,16},{8,24},{16,0},{24,8},{1,17},{9,25},{17,1},{25,9},{2,18},{10... | collective-permute-start | bytes 1179656 | tf_op jit(solution)/shard_map/ppermute | solution.py:53
  43.7 32.2 %collective-permute-start = (bf16[256,768]{1,0:T(8,128)(2,1)S(1)}, bf16[256,768]{1,0:T(8,128)(2,1)S(1)}, u32[]{:S(2)}, u32[]{:S(2)}) collective-permute-start(bf16[256,768]{1,0:T(8,128)(2,1)S(1)} %bitcast.125), channel_id=1, source_target_pairs={{0,8},{8,0},{16,24},{24,16},{1,9},{9,1},{17,25},{25,17},{2,10},{10... | collective-permute-start | bytes 1179656 | tf_op jit(solution)/shard_map/ppermute | solution.py:53
  139.5 38.2 %collective-permute-start.22 = (f32[16,192]{1,0:T(8,128)S(1)}, f32[16,192]{1,0:T(8,128)S(1)}, u32[]{:S(2)}, u32[]{:S(2)}) collective-permute-start(f32[16,192]{1,0:T(8,128)S(1)} %get-tuple-element.176), channel_id=1, source_target_pairs={{0,24},{8,16},{16,8},{24,0},{1,25},{9,17},{17,9},{25,1},{2,26},{10... | collective-permute-start | bytes 36872 | tf_op jit(solution)/shard_map/ppermute | solution.py:53
  141.1 36.6 %collective-permute-start.21 = (f32[16,192]{1,0:T(8,128)S(1)}, f32[16,192]{1,0:T(8,128)S(1)}, u32[]{:S(2)}, u32[]{:S(2)}) collective-permute-start(f32[16,192]{1,0:T(8,128)S(1)} %get-tuple-element.177), channel_id=1, source_target_pairs={{0,16},{8,24},{16,0},{24,8},{1,17},{9,25},{17,1},{25,9},{2,18},{10... | collective-permute-start | bytes 36872 | tf_op jit(solution)/shard_map/ppermute | solution.py:53
  146.5 12.7 %collective-permute-start.13 = (bf16[256,192]{1,0:T(8,128)(2,1)S(1)}, bf16[256,192]{1,0:T(8,128)(2,1)S(1)}, u32[]{:S(2)}, u32[]{:S(2)}) collective-permute-start(bf16[256,192]{1,0:T(8,128)(2,1)S(1)} %get-tuple-element.166), channel_id=1, source_target_pairs={{0,16},{8,24},{16,0},{24,8},{1,17},{9,25},{17,1},{25,9},{2,18},{10... | collective-permute-start | bytes 294920 | tf_op jit(solution)/shard_map/ppermute | solution.py:53
  147.4 13.7 %collective-permute-start.12 = (bf16[256,192]{1,0:T(8,128)(2,1)S(1)}, bf16[256,192]{1,0:T(8,128)(2,1)S(1)}, u32[]{:S(2)}, u32[]{:S(2)}) collective-permute-start(bf16[256,192]{1,0:T(8,128)(2,1)S(1)} %get-tuple-element.167), channel_id=1, source_target_pairs={{0,8},{8,0},{16,24},{24,16},{1,9},{9,1},{17,25},{25,17},{2,10},{10... | collective-permute-start | bytes 294920 | tf_op jit(solution)/shard_map/ppermute | solution.py:53
  153.9 23.8 %collective-permute-start.20 = (f32[16,192]{1,0:T(8,128)S(1)}, f32[16,192]{1,0:T(8,128)S(1)}, u32[]{:S(2)}, u32[]{:S(2)}) collective-permute-start(f32[16,192]{1,0:T(8,128)S(1)} %get-tuple-element.178), channel_id=1, source_target_pairs={{0,8},{8,0},{16,24},{24,16},{1,9},{9,1},{17,25},{25,17},{2,10},{10... | collective-permute-start | bytes 36872 | tf_op jit(solution)/shard_map/ppermute | solution.py:53
  159.2 28.8 %collective-permute-start.26 = (bf16[2,96,1920]{2,1,0:T(8,128)(2,1)}, bf16[2,96,1920]{2,1,0:T(8,128)(2,1)}, u32[]{:S(2)}, u32[]{:S(2)}) collective-permute-start(bf16[2,96,1920]{2,1,0:T(8,128)(2,1)} %fusion.55), channel_id=1, source_target_pairs={{0,4},{1,5},{2,6},{3,7},{4,0},{5,1},{6,2},{7,3},{8,12},{9,13},{10,... | collective-permute-start | bytes 2211848 | tf_op jit(solution)/shard_map/ppermute | solution.py:126
  161.2 24.3 %collective-permute-start.24 = (bf16[2,96,1920]{2,1,0:T(8,128)(2,1)}, bf16[2,96,1920]{2,1,0:T(8,128)(2,1)}, u32[]{:S(2)}, u32[]{:S(2)}) collective-permute-start(bf16[2,96,1920]{2,1,0:T(8,128)(2,1)} %fusion.56), channel_id=1, source_target_pairs={{0,2},{1,3},{2,0},{3,1},{4,6},{5,7},{6,4},{7,5},{8,10},{9,11},{10,... | collective-permute-start | bytes 2211848 | tf_op jit(solution)/shard_map/ppermute | solution.py:126
  191.6 14.4 %collective-permute-start.23 = (bf16[4,112,576]{2,1,0:T(8,128)(2,1)}, bf16[4,112,576]{2,1,0:T(8,128)(2,1)}, u32[]{:S(2)}, u32[]{:S(2)}) collective-permute-start(bf16[4,112,576]{2,1,0:T(8,128)(2,1)} %fusion.59), channel_id=1, source_target_pairs={{0,1},{1,0},{2,3},{3,2},{4,5},{5,4},{6,7},{7,6},{8,9},{9,8},{10,11... | collective-permute-start | bytes 1548296 | tf_op jit(solution)/shard_map/ppermute | solution.py:126
  191.6 47.1 %collective-permute-start.17 = (bf16[256,768]{1,0:T(8,128)(2,1)S(1)}, bf16[256,768]{1,0:T(8,128)(2,1)S(1)}, u32[]{:S(2)}, u32[]{:S(2)}) collective-permute-start(bf16[256,768]{1,0:T(8,128)(2,1)S(1)} %get-tuple-element.87), channel_id=1, source_target_pairs={{0,8},{8,0},{16,24},{24,16},{1,9},{9,1},{17,25},{25,17},{2,10},{10... | collective-permute-start | bytes 1179656 | tf_op jit(solution)/shard_map/ppermute | solution.py:53
  191.6 20.5 %collective-permute-start.18 = (bf16[256,768]{1,0:T(8,128)(2,1)S(1)}, bf16[256,768]{1,0:T(8,128)(2,1)}, u32[]{:S(2)}, u32[]{:S(2)}) collective-permute-start(bf16[256,768]{1,0:T(8,128)(2,1)S(1)} %get-tuple-element.89), channel_id=1, source_target_pairs={{0,8},{8,0},{16,24},{24,16},{1,9},{9,1},{17,25},{25,17},{2,10},{10... | collective-permute-start | bytes 1179656 | tf_op jit(solution)/shard_map/ppermute | solution.py:53
  199.1 16.9 %collective-permute-start.34 = (bf16[96,768]{1,0:T(8,128)(2,1)S(1)}, bf16[96,768]{1,0:T(8,128)(2,1)S(1)}, u32[]{:S(2)}, u32[]{:S(2)}) collective-permute-start(bf16[96,768]{1,0:T(8,128)(2,1)S(1)} %get-tuple-element.151), channel_id=1, source_target_pairs={{0,8},{8,0},{16,24},{24,16},{1,9},{9,1},{17,25},{25,17},{2,10},{10... | collective-permute-start | bytes 442376 | tf_op jit(solution)/shard_map/ppermute | solution.py:53
  213.3 28.1 %collective-permute-start.19 = (bf16[256,768]{1,0:T(8,128)(2,1)S(1)}, bf16[256,768]{1,0:T(8,128)(2,1)S(1)}, u32[]{:S(2)}, u32[]{:S(2)}) collective-permute-start(bf16[256,768]{1,0:T(8,128)(2,1)S(1)} %add_convert_fusion), channel_id=1, source_target_pairs={{0,16},{8,24},{16,0},{24,8},{1,17},{9,25},{17,1},{25,9},{2,18},{10... | collective-permute-start | bytes 1179656 | tf_op jit(solution)/shard_map/ppermute | solution.py:53
  213.9 28.6 %collective-permute-start.33 = (bf16[96,768]{1,0:T(8,128)(2,1)S(1)}, bf16[96,768]{1,0:T(8,128)(2,1)S(1)}, u32[]{:S(2)}, u32[]{:S(2)}) collective-permute-start(bf16[96,768]{1,0:T(8,128)(2,1)S(1)} %get-tuple-element.153), channel_id=1, source_target_pairs={{0,8},{8,0},{16,24},{24,16},{1,9},{9,1},{17,25},{25,17},{2,10},{10... | collective-permute-start | bytes 442376 | tf_op jit(solution)/shard_map/ppermute | solution.py:53
  215.9 17.2 %collective-permute-start.31 = (bf16[96,960]{1,0:T(8,128)(2,1)S(1)}, bf16[96,960]{1,0:T(8,128)(2,1)S(1)}, u32[]{:S(2)}, u32[]{:S(2)}) collective-permute-start(bf16[96,960]{1,0:T(8,128)(2,1)S(1)} %pad_maximum_fusion.7), channel_id=1, source_target_pairs={{0,8},{8,0},{16,24},{24,16},{1,9},{9,1},{17,25},{25,17},{2,10},{10... | collective-permute-start | bytes 552968 | tf_op jit(solution)/shard_map/ppermute | solution.py:53
  216.1 33.0 %collective-permute-start.30 = (bf16[96,960]{1,0:T(8,128)(2,1)S(1)}, bf16[96,960]{1,0:T(8,128)(2,1)S(1)}, u32[]{:S(2)}, u32[]{:S(2)}) collective-permute-start(bf16[96,960]{1,0:T(8,128)(2,1)S(1)} %pad_maximum_fusion.5), channel_id=1, source_target_pairs={{0,8},{8,0},{16,24},{24,16},{1,9},{9,1},{17,25},{25,17},{2,10},{10... | collective-permute-start | bytes 552968 | tf_op jit(solution)/shard_map/ppermute | solution.py:53
  238.3 10.8 %collective-permute-start.35 = (bf16[96,768]{1,0:T(8,128)(2,1)S(1)}, bf16[96,768]{1,0:T(8,128)(2,1)S(1)}, u32[]{:S(2)}, u32[]{:S(2)}) collective-permute-start(bf16[96,768]{1,0:T(8,128)(2,1)S(1)} %add_convert_fusion.4), channel_id=1, source_target_pairs={{0,16},{8,24},{16,0},{24,8},{1,17},{9,25},{17,1},{25,9},{2,18},{10... | collective-permute-start | bytes 442376 | tf_op jit(solution)/shard_map/ppermute | solution.py:53
  238.8 12.5 %collective-permute-start.32 = (bf16[96,960]{1,0:T(8,128)(2,1)S(1)}, bf16[96,960]{1,0:T(8,128)(2,1)S(1)}, u32[]{:S(2)}, u32[]{:S(2)}) collective-permute-start(bf16[96,960]{1,0:T(8,128)(2,1)S(1)} %add_convert_fusion.3), channel_id=1, source_target_pairs={{0,16},{8,24},{16,0},{24,8},{1,17},{9,25},{17,1},{25,9},{2,18},{10... | collective-permute-start | bytes 552968 | tf_op jit(solution)/shard_map/ppermute | solution.py:53
  (85 other events, 771.8 us)
Sparse Core Ops, SparseCore 0:
  10.4 33.2 all-gather.4
  45.6 52.8 all-gather.6
  124.4 61.1 reduce-scatter.1

commit v5 on v4

--- a/solution.py
+++ b/solution.py
@@ -69,16 +69,28 @@
     return pieces[:1] + [across(piece, r) for r, piece in enumerate(pieces) if r]
 
 
+def sum_first(pieces):
+    totals = {r: [piece] for r, piece in enumerate(pieces)}
+    return sum_bit(totals, 0, len(pieces)) if len(pieces) > 1 else totals
+
+
+def sum_rest(totals, count):
+    for bit in seq_bits()[1:]:
+        totals = sum_bit(totals, bit, count)
+    return totals[0]
+
+
+def sum_bit(totals, bit, count):
+    step = 1 << bit
+    for r in reversed(range(step, count, 2 * step)):
+        terms = totals.pop(r)
+        sent = terms[0] if len(terms) == 1 else total_of(terms)
+        totals[r - step].append(across(sent.astype(jnp.bfloat16), step))
+    return totals
+
+
 def sum_across(pieces):
-    count = len(pieces)
-    totals = {r: [piece] for r, piece in enumerate(pieces)}
-    for bit in seq_bits():
-        step = 1 << bit
-        for r in reversed(range(step, count, 2 * step)):
-            terms = totals.pop(r)
-            sent = terms[0].astype(jnp.bfloat16) if len(terms) == 1 else total_of(terms)
-            totals[r - step].append(across(sent.astype(jnp.bfloat16), step))
-    return totals[0]
+    return sum_rest(sum_first(pieces), len(pieces))
 
 
 def total_of(pieces):
@@ -407,6 +419,7 @@
     ]
     vec_own = jnp.sum(qkv_all[:, 3 * row_shard :].astype(f32), axis=0)[:vec_rows]
     vec_half = vec_own.astype(bf16)
+    weight_pieces[-1] = after(weight_pieces[-1], qkv_all)
     cuts = (0, hidden_shard, 2 * hidden_shard, 2 * hidden_shard + head_width)
     rest_cat = jnp.concatenate(
         [
@@ -431,7 +444,7 @@
         width = parts[0].shape[1]
         return dot_right_t(left[:, :width], parts[0]) + dot_right_t(left[:, width:], parts[1])
 
-    vec_near = [piece.astype(f32) for piece in gather_across(vec_half)]
+    vec_near = [piece.astype(f32) for piece in swap_across([vec_half] * seq_count)]
 
     def near(order):
         return sum(jnp.where(order == r, piece, 0.0) for r, piece in enumerate(vec_near))
@@ -443,7 +456,7 @@
 
     valid_len = lengths[0]
     queries, keys_all, values_all, lse, *mixed_pieces = attend(
-        place, valid_len, vec_own[:2], after(token_pieces, vec_wide, up_bias), w_qkv
+        place, valid_len, vec_own[:2], token_pieces, w_qkv
     )
     mixed_rows = jnp.concatenate(swap_across(mixed_pieces), axis=1)
 
@@ -527,7 +540,8 @@
         grad_pieces,
         w_qkv,
     )
-    input_terms = sum_across([input_own, *input_parts])
+    input_totals = sum_first([input_own, *input_parts])
+    input_terms = None
     vec_part = sum(after(vec_moved, input_own))
     vec_lines = jnp.concatenate(
         [head_sums[:1, :head_width], head_sums[:1, 2 * head_width :], vec_part[2:]], axis=0
@@ -575,6 +589,11 @@
             else:
                 moving.append(half[0])
         wide_moving = moving
+        if input_terms is None:
+            input_totals = {
+                r: terms[:1] + after(terms[1:], step) for r, terms in input_totals.items()
+            }
+            input_terms = sum_rest(input_totals, seq_count)
         if down_moved is None:
             down_pieces = jnp.split(after(down_part, step), seq_count, axis=1)
             down_moved = sum_across(down_pieces)

time: 263 us -> 279 us (1.061)
  waiting for transfers between devices: 82.7 us -> 102 us
    all_gather x1, waiting for transfers between devices: 0.01 us -> 25.6 us  [layer(): own_all = lax.all_gather(own_shard, 'fsdp', axis=0, tiled=True)]
    ppermute x27, waiting for transfers between devices: 68.3 us -> 60.5 us  [across(): return lax.ppermute(piece, 'seq', [(i, i ^ bits) for i in range(count)])]
    unnamed x142 -> x144, local copies, waits for them, and re-layouts: 10.6 us -> 9.91 us
  transfers between devices with their start and end apart: 39 -> 39, of which waited for: 15 -> 17; matrix products, arithmetic and copies ran while one was open for 17% -> 16% of each run, Pallas kernels for 9% -> 8%
where the time goes in v5:
time: 279 us; the launch traced here: 278 us
  waiting for transfers between devices  102 us (37%)
  starting transfers between devices  49.2 us (18%)
  matrix products  27.6 us (10%)
  other arithmetic  26.3 us (9%)
  Pallas kernels  23.2 us (8%)
  local copies, waits for them, and re-layouts  21.4 us (8%)
  between operations  15.9 us (6%)
  blocking collectives  11.8 us (4%)
    ppermute x27, waiting for transfers between devices, across(): return lax.ppermute(piece, 'seq', [(i, i ^ bits) for i in range(count)])  60.5 us
    ppermute x27, starting transfers between devices, across(): return lax.ppermute(piece, 'seq', [(i, i ^ bits) for i in range(count)])  42.4 us
    all_gather x1, waiting for transfers between devices, layer(): own_all = lax.all_gather(own_shard, 'fsdp', axis=0, tiled=True)  25.6 us
    ppermute x9, waiting for transfers between devices, swapped(): return lax.ppermute(sent, 'fsdp', pairs)  15.6 us
    pallas_call x1, Pallas kernels, attend_back(): pl.pallas_call(attend_back_kernel, out_shape=(jax.ShapeDtypeStruct((rows,...  12.2 us
    all_gather x1, blocking collectives, layer(): qkv_all = lax.all_gather(qkv_shard, 'fsdp', axis=0, tiled=False)  11.8 us
    pallas_call x1, Pallas kernels, attend(): pl.pallas_call(attend_kernel, out_shape=(half, half, half, jax.ShapeDtype...  10.3 us
    unnamed x144, local copies, waits for them, and re-layouts  9.91 us
  transfers between devices with their start and end apart: 39, of which 17 were waited for; matrix products, arithmetic and copies ran while one was open for 16% of the time, Pallas kernels for 8%

profile of v5, /device:TPU:0, one launch (start us, length us, event | category | flops | bytes accessed | tf_op | source)
XLA Modules:
  0.0 277.8 jit_solution(3398126124474245931)
XLA Ops:
  9.5 4.1 %collective-permute-start.7 = (bf16[96,1728]{1,0:T(8,128)(2,1)S(1)}, bf16[96,1728]{1,0:T(8,128)(2,1)S(1)}, u32[]{:S(2)}, u32[]{:S(2)}) collective-permute-start(bf16[96,1728]{1,0:T(8,128)(2,1)S(1)} %pad_maximum_fusion.4), channel_id=1, source_target_pairs={{0,16},{8,24},{16,0},{24,8},{1,17},{9,25},{17,1},{25,9},{2,18},{10... | collective-permute-start | bytes 995336 | tf_op jit(solution)/shard_map/ppermute | solution.py:53
  15.8 11.8 %all-gather.1 = bf16[8,304,192]{1,2,0:T(8,128)(2,1)S(1)} all-gather(bf16[1,304,192]{1,2,0:T(8,128)(2,1)S(1)} %copy.97), channel_id=2, replica_groups=mesh['seq'=4,'fsdp'=8] {'fsdp'}, dimensions={0}, use_global_device_ids=true | all-gather | bytes 1050624 | tf_op jit(solution)/shard_map/all_gather | solution.py:415
  29.8 8.5 %collective-permute-done.8 = bf16[96,1728]{1,0:T(8,128)(2,1)S(1)} collective-permute-done((bf16[96,1728]{1,0:T(8,128)(2,1)S(1)}, bf16[96,1728]{1,0:T(8,128)(2,1)S(1)}, u32[]{:S(2)}, u32[]{:S(2)}) %collective-permute-start.8) | collective-permute-done | bytes 331808 | tf_op jit(solution)/shard_map/ppermute | solution.py:53
  40.3 3.1 %collective-permute-start.1 = (bf16[256,768]{1,0:T(8,128)(2,1)S(1)}, bf16[256,768]{1,0:T(8,128)(2,1)S(1)}, u32[]{:S(2)}, u32[]{:S(2)}) collective-permute-start(bf16[256,768]{1,0:T(8,128)(2,1)S(1)} %bitcast.118), channel_id=1, source_target_pairs={{0,16},{8,24},{16,0},{24,8},{1,17},{9,25},{17,1},{25,9},{2,18},{10... | collective-permute-start | bytes 1179656 | tf_op jit(solution)/shard_map/ppermute | solution.py:53
  46.4 4.0 %collective-permute-start.11 = (bf16[12,192]{0,1:T(8,128)(2,1)}, bf16[12,192]{0,1:T(8,128)(2,1)}, u32[]{:S(2)}, u32[]{:S(2)}) collective-permute-start(bf16[12,192]{0,1:T(8,128)(2,1)} %slice.398), channel_id=1, source_target_pairs={{0,24},{8,16},{16,8},{24,0},{1,25},{9,17},{17,9},{25,1},{2,26},{10... | collective-permute-start | bytes 13832 | tf_op jit(solution)/shard_map/ppermute | solution.py:53
  53.2 8.9 %collective-permute-done.1.refs_2_ = bf16[256,768]{1,0:T(8,128)(2,1)S(1)} collective-permute-done((bf16[256,768]{1,0:T(8,128)(2,1)S(1)}, bf16[256,768]{1,0:T(8,128)(2,1)S(1)}, u32[]{:S(2)}, u32[]{:S(2)}) %collective-permute-start.1) | collective-permute-done | bytes 393248 | tf_op jit(solution)/shard_map/ppermute | solution.py:53
  67.5 5.1 %collective-permute-done.2.refs_3_ = bf16[256,768]{1,0:T(8,128)(2,1)S(1)} collective-permute-done((bf16[256,768]{1,0:T(8,128)(2,1)S(1)}, bf16[256,768]{1,0:T(8,128)(2,1)S(1)}, u32[]{:S(2)}, u32[]{:S(2)}) %collective-permute-start.2) | collective-permute-done | bytes 393248 | tf_op jit(solution)/shard_map/ppermute | solution.py:53
  72.6 10.3 %attend.1 = (bf16[1024,192]{1,0:T(8,128)(2,1)S(1)}, bf16[1024,192]{1,0:T(8,128)(2,1)S(1)}, bf16[1024,192]{1,0:T(8,128)(2,1)S(1)}, f32[1024,8]{1,0:T(8,128)S(1)},...) custom-call(s32[1]{0:T(128)} %bitcast.1.place_ref, ...), custom_call_target="tpu_custom_call" | custom-call | flops 4127195136 | bytes 8388608 | tf_op jit(solution)/shard_map/attend/pallas_call | solution.py:209
  92.9 7.2 %collective-permute-done.4 = bf16[256,192]{1,0:T(8,128)(2,1)S(1)} collective-permute-done((bf16[256,192]{1,0:T(8,128)(2,1)S(1)}, bf16[256,192]{1,0:T(8,128)(2,1)S(1)}, u32[]{:S(2)}, u32[]{:S(2)}) %collective-permute-start.4) | collective-permute-done | bytes 98336 | tf_op jit(solution)/shard_map/ppermute | solution.py:53
  101.8 25.6 %all-gather.5.cloned.1.call-done = bf16[768,1728]{1,0:T(8,128)(2,1)} async-done(((bf16[96,1728]{1,0:T(8,128)(2,1)}), bf16[768,1728]{1,0:T(8,128)(2,1)}) %all-gather.5.cloned.1.call-update) | async-done | bytes 2654224 | tf_op jit(solution)/shard_map/all_gather | solution.py:412
  130.0 3.1 %fusion.12 = f32[256,2304]{1,0:T(8,128)S(1)} fusion(bf16[256,768]{1,0:T(8,128)(2,1)S(1)} %get-tuple-element.137, bf16[768,5184]{1,0:T(8,128)(2,1)} %all-gather.7.cloned.1.call-done), kind=kOutput, calls=%fused_computation.19 | convolution fusion | flops 905969664 | bytes 6291456 | tf_op jit(solution)/shard_map/dot_general | solution.py:440
  134.6 3.3 %fusion.123 = (f32[256]{0:T(256)S(1)}, f32[256,768]{1,0:T(8,128)S(1)}) fusion(f32[768]{0:T(1024)S(1)} %get-tuple-element.114, f32[256,768]{1,0:T(8,128)S(1)} %fusion.46, bf16[768,5184]{1,0:T(8,128)(2,1)} %all-gather.7.cloned.1.call-done, bf16[256,3072]{1,0:T(8,128)(2,1)S(1)} %multiply_convert_fusion, f32[768]{0:T(1024)S(1)} %get-tuple-element.115, ...), kind=kOutput, calls=%fused_computation.232 | convolution fusion | flops 907149056 | bytes 7091200 | tf_op jit(solution)/shard_map/dot_general | solution.py:46
  141.0 3.6 %convolution_convert_fusion.1 = bf16[768,3072]{1,0:T(8,128)(2,1)} fusion(bf16[256,768]{1,0:T(8,128)(2,1)S(1)} %get-tuple-element.66, bf16[256,3072]{1,0:T(8,128)(2,1)S(1)} %multiply_convert_fusion), kind=kOutput, calls=%fused_computation.1 | convolution fusion | flops 1210318848 | bytes 6684672 | tf_op jit(solution)/shard_map/dot_general | solution.py:477
  146.5 3.4 %fusion.6 = f32[256,2304]{1,0:T(8,128)S(1)} fusion(bf16[256,768]{1,0:T(8,128)(2,1)} %copy-done.40, bf16[768,5184]{1,0:T(8,128)(2,1)} %all-gather.7.cloned.1.call-done), kind=kOutput, calls=%fused_computation.13 | convolution fusion | flops 905969664 | bytes 6291456 | tf_op jit(solution)/shard_map/dot_general | solution.py:440
  160.1 3.4 %collective-permute-start.22 = (f32[16,192]{1,0:T(8,128)S(1)}, f32[16,192]{1,0:T(8,128)S(1)}, u32[]{:S(2)}, u32[]{:S(2)}) collective-permute-start(f32[16,192]{1,0:T(8,128)S(1)} %get-tuple-element.174), channel_id=1, source_target_pairs={{0,24},{8,16},{16,8},{24,0},{1,25},{9,17},{17,9},{25,1},{2,26},{10... | collective-permute-start | bytes 36872 | tf_op jit(solution)/shard_map/ppermute | solution.py:53
  174.4 4.0 %collective-permute-start.20 = (f32[16,192]{1,0:T(8,128)S(1)}, f32[16,192]{1,0:T(8,128)S(1)}, u32[]{:S(2)}, u32[]{:S(2)}) collective-permute-start(f32[16,192]{1,0:T(8,128)S(1)} %get-tuple-element.176), channel_id=1, source_target_pairs={{0,8},{8,0},{16,24},{24,16},{1,9},{9,1},{17,25},{25,17},{2,10},{10... | collective-permute-start | bytes 36872 | tf_op jit(solution)/shard_map/ppermute | solution.py:53
  182.5 12.2 %attend_back.1 = (bf16[1024,576]{1,0:T(8,128)(2,1)}, f32[16,576]{1,0:T(8,128)S(1)}, f32[256,768]{1,0:T(8,128)}, bf16[256,768]{1,0:T(8,128)(2,1)S(1)}, bf16[256,7...) custom-call(s32[1]{0:T(128)} %bitcast.1.place_ref, s32[1]{0:T(128)S(6)} %copy.119.length_ref, ...), custom_call_target="tpu_custom_call" | custom-call | flops 4026531840 | bytes 8388608 | tf_op jit(solution)/shard_map/attend_back/pallas_call | solution.py:310
  194.7 3.4 %fusion.22 = bf16[768,576]{0,1:T(8,128)(2,1)} fusion(bf16[1024,576]{1,0:T(8,128)(2,1)} %get-tuple-element.84, bf16[256,768]{1,0:T(8,128)(2,1)S(1)} %copy-done.16, bf16[256,768]{1,0:T(8,128)(2,1)S(1)} %copy-done.12, bf16[256,768]{1,0:T(8,128)(2,1)S(1)} %copy-done.14, bf16[256,768]{1,0:T(8,128)(2,1)S(1)} %bitcast.121), kind=kOutput, calls=%fused_computation.40 | convolution fusion | flops 912703488 | bytes 3637248 | tf_op jit(solution)/shard_map/dot_general | solution.py:551
  200.7 5.8 %collective-permute-done.19 = bf16[2,96,1920]{2,1,0:T(8,128)(2,1)} collective-permute-done((bf16[2,96,1920]{2,1,0:T(8,128)(2,1)}, bf16[2,96,1920]{2,1,0:T(8,128)(2,1)}, u32[]{:S(2)}, u32[]{:S(2)}) %collective-permute-start.19) | collective-permute-done | bytes 737312 | tf_op jit(solution)/shard_map/ppermute | solution.py:138
  216.9 4.3 %collective-permute-done.27 = bf16[1,96,1920]{2,1,0:T(8,128)(2,1)} collective-permute-done((bf16[1,96,1920]{2,1,0:T(8,128)(2,1)}, bf16[1,96,1920]{2,1,0:T(8,128)(2,1)}, u32[]{:S(2)}, u32[]{:S(2)}) %collective-permute-start.27) | collective-permute-done | bytes 368672 | tf_op jit(solution)/shard_map/ppermute | solution.py:138
  229.1 3.1 %collective-permute-start.24 = (bf16[256,768]{1,0:T(8,128)(2,1)S(1)}, bf16[256,768]{1,0:T(8,128)(2,1)S(1)}, u32[]{:S(2)}, u32[]{:S(2)}) collective-permute-start(bf16[256,768]{1,0:T(8,128)(2,1)S(1)} %add_convert_fusion), channel_id=1, source_target_pairs={{0,16},{8,24},{16,0},{24,8},{1,17},{9,25},{17,1},{25,9},{2,18},{10... | collective-permute-start | bytes 1179656 | tf_op jit(solution)/shard_map/ppermute | solution.py:53
  237.7 17.0 %collective-permute-done.31 = bf16[96,960]{1,0:T(8,128)(2,1)S(1)} collective-permute-done((bf16[96,960]{1,0:T(8,128)(2,1)S(1)}, bf16[96,960]{1,0:T(8,128)(2,1)S(1)}, u32[]{:S(2)}, u32[]{:S(2)}) %collective-permute-start.31) | collective-permute-done | bytes 184352 | tf_op jit(solution)/shard_map/ppermute | solution.py:53
  255.5 4.4 %collective-permute-done.29 = bf16[1,112,576]{2,1,0:T(8,128)(2,1)S(1)} collective-permute-done((bf16[1,112,576]{2,1,0:T(8,128)(2,1)S(1)}, bf16[1,112,576]{2,1,0:T(8,128)(2,1)S(1)}, u32[]{:S(2)}, u32[]{:S(2)}) %collective-permute-start.29) | collective-permute-done | bytes 129056 | tf_op jit(solution)/shard_map/ppermute | solution.py:138
  261.1 6.1 %collective-permute-done.32 = bf16[96,960]{1,0:T(8,128)(2,1)S(1)} collective-permute-done((bf16[96,960]{1,0:T(8,128)(2,1)S(1)}, bf16[96,960]{1,0:T(8,128)(2,1)S(1)}, u32[]{:S(2)}, u32[]{:S(2)}) %collective-permute-start.32) | collective-permute-done | bytes 184352 | tf_op jit(solution)/shard_map/ppermute | solution.py:53
  (327 shorter events, 96.5 us)
Async XLA Ops:
  7.2 92.8 %all-gather.7.cloned.1.call-start = ((), (), s32[]{:S(2)}) async-start(), calls=%async_computation.2 | async-start | bytes 9068544 | tf_op jit(solution)/shard_map/all_gather | solution.py:432
  9.5 19.7 %collective-permute-start.7 = (bf16[96,1728]{1,0:T(8,128)(2,1)S(1)}, bf16[96,1728]{1,0:T(8,128)(2,1)S(1)}, u32[]{:S(2)}, u32[]{:S(2)}) collective-permute-start(bf16[96,1728]{1,0:T(8,128)(2,1)S(1)} %pad_maximum_fusion.4), channel_id=1, source_target_pairs={{0,16},{8,24},{16,0},{24,8},{1,17},{9,25},{17,1},{25,9},{2,18},{10... | collective-permute-start | bytes 995336 | tf_op jit(solution)/shard_map/ppermute | solution.py:53
  13.6 16.2 %collective-permute-start.6 = (bf16[96,1728]{1,0:T(8,128)(2,1)S(1)}, bf16[96,1728]{1,0:T(8,128)(2,1)S(1)}, u32[]{:S(2)}, u32[]{:S(2)}) collective-permute-start(bf16[96,1728]{1,0:T(8,128)(2,1)S(1)} %pad_maximum_fusion.4), channel_id=1, source_target_pairs={{0,8},{8,0},{16,24},{24,16},{1,9},{9,1},{17,25},{25,17},{2,10},{10... | collective-permute-start | bytes 995336 | tf_op jit(solution)/shard_map/ppermute | solution.py:53
  39.5 87.9 %all-gather.5.cloned.1.call-start = ((), (), s32[]{:S(2)}) async-start(), calls=%async_computation.1 | async-start | bytes 3096576 | tf_op jit(solution)/shard_map/all_gather | solution.py:412
  40.2 173.6 %reduce-scatter.2.cloned.1.call-start = ((), (), s32[]{:S(2)}) async-start(), calls=%async_computation.3 | async-start | bytes 5308416 | tf_op jit(solution)/shard_map/reduce_scatter | solution.py:484
  40.3 21.8 %collective-permute-start.1 = (bf16[256,768]{1,0:T(8,128)(2,1)S(1)}, bf16[256,768]{1,0:T(8,128)(2,1)S(1)}, u32[]{:S(2)}, u32[]{:S(2)}) collective-permute-start(bf16[256,768]{1,0:T(8,128)(2,1)S(1)} %bitcast.118), channel_id=1, source_target_pairs={{0,16},{8,24},{16,0},{24,8},{1,17},{9,25},{17,1},{25,9},{2,18},{10... | collective-permute-start | bytes 1179656 | tf_op jit(solution)/shard_map/ppermute | solution.py:53
  43.4 24.1 %collective-permute-start = (bf16[256,768]{1,0:T(8,128)(2,1)S(1)}, bf16[256,768]{1,0:T(8,128)(2,1)S(1)}, u32[]{:S(2)}, u32[]{:S(2)}) collective-permute-start(bf16[256,768]{1,0:T(8,128)(2,1)S(1)} %bitcast.119), channel_id=1, source_target_pairs={{0,8},{8,0},{16,24},{24,16},{1,9},{9,1},{17,25},{25,17},{2,10},{10... | collective-permute-start | bytes 1179656 | tf_op jit(solution)/shard_map/ppermute | solution.py:53
  46.0 18.2 %collective-permute-start.9 = (bf16[12,192]{0,1:T(8,128)(2,1)}, bf16[12,192]{0,1:T(8,128)(2,1)}, u32[]{:S(2)}, u32[]{:S(2)}) collective-permute-start(bf16[12,192]{0,1:T(8,128)(2,1)} %slice.398), channel_id=1, source_target_pairs={{0,8},{8,0},{16,24},{24,16},{1,9},{9,1},{17,25},{25,17},{2,10},{10... | collective-permute-start | bytes 13832 | tf_op jit(solution)/shard_map/ppermute | solution.py:53
  46.3 17.9 %collective-permute-start.10 = (bf16[12,192]{0,1:T(8,128)(2,1)}, bf16[12,192]{0,1:T(8,128)(2,1)}, u32[]{:S(2)}, u32[]{:S(2)}) collective-permute-start(bf16[12,192]{0,1:T(8,128)(2,1)} %slice.398), channel_id=1, source_target_pairs={{0,16},{8,24},{16,0},{24,8},{1,17},{9,25},{17,1},{25,9},{2,18},{10... | collective-permute-start | bytes 13832 | tf_op jit(solution)/shard_map/ppermute | solution.py:53
  46.4 18.6 %collective-permute-start.11 = (bf16[12,192]{0,1:T(8,128)(2,1)}, bf16[12,192]{0,1:T(8,128)(2,1)}, u32[]{:S(2)}, u32[]{:S(2)}) collective-permute-start(bf16[12,192]{0,1:T(8,128)(2,1)} %slice.398), channel_id=1, source_target_pairs={{0,24},{8,16},{16,8},{24,0},{1,25},{9,17},{17,9},{25,1},{2,26},{10... | collective-permute-start | bytes 13832 | tf_op jit(solution)/shard_map/ppermute | solution.py:53
  160.1 38.0 %collective-permute-start.22 = (f32[16,192]{1,0:T(8,128)S(1)}, f32[16,192]{1,0:T(8,128)S(1)}, u32[]{:S(2)}, u32[]{:S(2)}) collective-permute-start(f32[16,192]{1,0:T(8,128)S(1)} %get-tuple-element.174), channel_id=1, source_target_pairs={{0,24},{8,16},{16,8},{24,0},{1,25},{9,17},{17,9},{25,1},{2,26},{10... | collective-permute-start | bytes 36872 | tf_op jit(solution)/shard_map/ppermute | solution.py:53
  163.5 34.6 %collective-permute-start.21 = (f32[16,192]{1,0:T(8,128)S(1)}, f32[16,192]{1,0:T(8,128)S(1)}, u32[]{:S(2)}, u32[]{:S(2)}) collective-permute-start(f32[16,192]{1,0:T(8,128)S(1)} %get-tuple-element.175), channel_id=1, source_target_pairs={{0,16},{8,24},{16,0},{24,8},{1,17},{9,25},{17,1},{25,9},{2,18},{10... | collective-permute-start | bytes 36872 | tf_op jit(solution)/shard_map/ppermute | solution.py:53
  167.2 13.3 %collective-permute-start.13 = (bf16[256,192]{1,0:T(8,128)(2,1)S(1)}, bf16[256,192]{1,0:T(8,128)(2,1)S(1)}, u32[]{:S(2)}, u32[]{:S(2)}) collective-permute-start(bf16[256,192]{1,0:T(8,128)(2,1)S(1)} %get-tuple-element.164), channel_id=1, source_target_pairs={{0,16},{8,24},{16,0},{24,8},{1,17},{9,25},{17,1},{25,9},{2,18},{10... | collective-permute-start | bytes 294920 | tf_op jit(solution)/shard_map/ppermute | solution.py:53
  174.4 23.7 %collective-permute-start.20 = (f32[16,192]{1,0:T(8,128)S(1)}, f32[16,192]{1,0:T(8,128)S(1)}, u32[]{:S(2)}, u32[]{:S(2)}) collective-permute-start(f32[16,192]{1,0:T(8,128)S(1)} %get-tuple-element.176), channel_id=1, source_target_pairs={{0,8},{8,0},{16,24},{24,16},{1,9},{9,1},{17,25},{25,17},{2,10},{10... | collective-permute-start | bytes 36872 | tf_op jit(solution)/shard_map/ppermute | solution.py:53
  180.6 28.5 %collective-permute-start.18 = (bf16[2,96,1920]{2,1,0:T(8,128)(2,1)}, bf16[2,96,1920]{2,1,0:T(8,128)(2,1)}, u32[]{:S(2)}, u32[]{:S(2)}) collective-permute-start(bf16[2,96,1920]{2,1,0:T(8,128)(2,1)} %fusion.56), channel_id=1, source_target_pairs={{0,4},{1,5},{2,6},{3,7},{4,0},{5,1},{6,2},{7,3},{8,12},{9,13},{10,... | collective-permute-start | bytes 2211848 | tf_op jit(solution)/shard_map/ppermute | solution.py:138
  181.9 24.6 %collective-permute-start.19 = (bf16[2,96,1920]{2,1,0:T(8,128)(2,1)}, bf16[2,96,1920]{2,1,0:T(8,128)(2,1)}, u32[]{:S(2)}, u32[]{:S(2)}) collective-permute-start(bf16[2,96,1920]{2,1,0:T(8,128)(2,1)} %fusion.57), channel_id=1, source_target_pairs={{0,2},{1,3},{2,0},{3,1},{4,6},{5,7},{6,4},{7,5},{8,10},{9,11},{10,... | collective-permute-start | bytes 2211848 | tf_op jit(solution)/shard_map/ppermute | solution.py:138
  199.7 14.1 %collective-permute-start.23 = (bf16[256,768]{1,0:T(8,128)(2,1)S(1)}, bf16[256,768]{1,0:T(8,128)(2,1)}, u32[]{:S(2)}, u32[]{:S(2)}) collective-permute-start(bf16[256,768]{1,0:T(8,128)(2,1)S(1)} %get-tuple-element.94), channel_id=1, source_target_pairs={{0,8},{8,0},{16,24},{24,16},{1,9},{9,1},{17,25},{25,17},{2,10},{10... | collective-permute-start | bytes 1179656 | tf_op jit(solution)/shard_map/ppermute | solution.py:53
  212.1 16.9 %collective-permute-start.17 = (bf16[256,768]{1,0:T(8,128)(2,1)S(1)}, bf16[256,768]{1,0:T(8,128)(2,1)S(1)}, u32[]{:S(2)}, u32[]{:S(2)}) collective-permute-start(bf16[256,768]{1,0:T(8,128)(2,1)S(1)} %get-tuple-element.83), channel_id=1, source_target_pairs={{0,8},{8,0},{16,24},{24,16},{1,9},{9,1},{17,25},{25,17},{2,10},{10... | collective-permute-start | bytes 1179656 | tf_op jit(solution)/shard_map/ppermute | solution.py:53
  214.8 19.5 %collective-permute-start.34 = (bf16[96,768]{1,0:T(8,128)(2,1)S(1)}, bf16[96,768]{1,0:T(8,128)(2,1)S(1)}, u32[]{:S(2)}, u32[]{:S(2)}) collective-permute-start(bf16[96,768]{1,0:T(8,128)(2,1)S(1)} %get-tuple-element.149), channel_id=1, source_target_pairs={{0,8},{8,0},{16,24},{24,16},{1,9},{9,1},{17,25},{25,17},{2,10},{10... | collective-permute-start | bytes 442376 | tf_op jit(solution)/shard_map/ppermute | solution.py:53
  229.1 30.8 %collective-permute-start.24 = (bf16[256,768]{1,0:T(8,128)(2,1)S(1)}, bf16[256,768]{1,0:T(8,128)(2,1)S(1)}, u32[]{:S(2)}, u32[]{:S(2)}) collective-permute-start(bf16[256,768]{1,0:T(8,128)(2,1)S(1)} %add_convert_fusion), channel_id=1, source_target_pairs={{0,16},{8,24},{16,0},{24,8},{1,17},{9,25},{17,1},{25,9},{2,18},{10... | collective-permute-start | bytes 1179656 | tf_op jit(solution)/shard_map/ppermute | solution.py:53
  232.2 28.8 %collective-permute-start.33 = (bf16[96,768]{1,0:T(8,128)(2,1)S(1)}, bf16[96,768]{1,0:T(8,128)(2,1)S(1)}, u32[]{:S(2)}, u32[]{:S(2)}) collective-permute-start(bf16[96,768]{1,0:T(8,128)(2,1)S(1)} %get-tuple-element.151), channel_id=1, source_target_pairs={{0,8},{8,0},{16,24},{24,16},{1,9},{9,1},{17,25},{25,17},{2,10},{10... | collective-permute-start | bytes 442376 | tf_op jit(solution)/shard_map/ppermute | solution.py:53
  232.6 22.2 %collective-permute-start.31 = (bf16[96,960]{1,0:T(8,128)(2,1)S(1)}, bf16[96,960]{1,0:T(8,128)(2,1)S(1)}, u32[]{:S(2)}, u32[]{:S(2)}) collective-permute-start(bf16[96,960]{1,0:T(8,128)(2,1)S(1)} %pad_maximum_fusion.7), channel_id=1, source_target_pairs={{0,8},{8,0},{16,24},{24,16},{1,9},{9,1},{17,25},{25,17},{2,10},{10... | collective-permute-start | bytes 552968 | tf_op jit(solution)/shard_map/ppermute | solution.py:53
  234.3 26.8 %collective-permute-start.30 = (bf16[96,960]{1,0:T(8,128)(2,1)S(1)}, bf16[96,960]{1,0:T(8,128)(2,1)S(1)}, u32[]{:S(2)}, u32[]{:S(2)}) collective-permute-start(bf16[96,960]{1,0:T(8,128)(2,1)S(1)} %pad_maximum_fusion.5), channel_id=1, source_target_pairs={{0,8},{8,0},{16,24},{24,16},{1,9},{9,1},{17,25},{25,17},{2,10},{10... | collective-permute-start | bytes 552968 | tf_op jit(solution)/shard_map/ppermute | solution.py:53
  234.8 26.2 %collective-permute-start.35 = (bf16[96,768]{1,0:T(8,128)(2,1)S(1)}, bf16[96,768]{1,0:T(8,128)(2,1)S(1)}, u32[]{:S(2)}, u32[]{:S(2)}) collective-permute-start(bf16[96,768]{1,0:T(8,128)(2,1)S(1)} %add_convert_fusion.4), channel_id=1, source_target_pairs={{0,16},{8,24},{16,0},{24,8},{1,17},{9,25},{17,1},{25,9},{2,18},{10... | collective-permute-start | bytes 442376 | tf_op jit(solution)/shard_map/ppermute | solution.py:53
  (86 other events, 1020.0 us)
Sparse Core Ops, SparseCore 0:
  39.6 54.7 all-gather.6
  96.9 30.5 all-gather.4
  144.8 61.0 reduce-scatter.1
